TPU v7x, 256 devices: a whole 4x4x8 slice. The times are simulated.
256 devices in a mesh: tm: 16 (over z, y_lo), height: 16 (over x, y_hi, core).
Axes of the slice: x: 4, y: 4 (y_hi: 2, y_lo: 2; y = y_hi * 2 + y_lo), z: 8, core: 2. Of those that a mesh axis runs over, the one named last changes fastest.
Arguments:
- hidden: float32 [64, 64, 16, 1536], P('tm', 'height')
- projection: bfloat16 [1536, 4608], P('tm')
- adaptive_shift: float32 [1536], replicated, may hold values from -3 to 3
- adaptive_scale: float32 [1536], replicated, may hold values from -3 to 3
- query_gain: float32 [128], replicated, may hold values from 1 to 5.2
- key_gain: float32 [128], replicated, may hold values from 1 to 5.2
Outputs:
- attended: bfloat16 [64, 64, 16, 1536], P('tm', 'height')
All inputs are finite; a program needn't handle non-finite values.
Results may differ from a plain program's by a relative error of at most 0.0075.
The roundings to bfloat16 on the way count: a program that leaves them out, or rounds other values in their place, can miss the bound.
Values may be sent and summed in bfloat16 or wider, within the bound.
No kernel may reach another device: no remote copies, remote signals or barrier semaphores. Data moves between devices by JAX's collectives and lax.ppermute only.
A program may use at most 128 MiB of HBM per device.

v0:
```python
import jax
import jax.numpy as jnp
from jax import lax
from jax.sharding import PartitionSpec as P

TILE_W = 8


epsilon = 1e-06


def extended(block, sides, width):
    for axis, dim in sides:
        count = lax.axis_size(axis)
        forward = [(i, i + 1) for i in range(count - 1)]
        backward = [(target, source) for source, target in forward]
        low = lax.ppermute(
            lax.slice_in_dim(block, block.shape[dim] - width, None, axis=dim), axis, forward
        )
        high = lax.ppermute(lax.slice_in_dim(block, 0, width, axis=dim), axis, backward)
        block = jnp.concatenate([low, block, high], axis=dim)
    return block


def layer_norm(activations, adaptive_shift, adaptive_scale):
    flattened = activations.reshape(-1, activations.shape[-1])
    centre = jnp.mean(flattened, axis=1, keepdims=True)
    shifted = flattened - centre
    spread = jnp.mean(shifted * shifted, axis=1, keepdims=True)
    scaled = shifted * lax.rsqrt(spread + epsilon) * (1.0 + adaptive_scale) + adaptive_shift
    return scaled.astype(jnp.bfloat16)


def head_norm(activations, head_gain):
    by_head = activations.reshape(activations.shape[0], -1, head_gain.shape[0])
    mean_square = jnp.mean(by_head * by_head, axis=2, keepdims=True)
    return (
        (by_head * lax.rsqrt(mean_square + epsilon) * head_gain)
        .reshape(activations.shape)
        .astype(jnp.bfloat16)
    )


def neighbour_valid(position, count):
    offsets = jnp.arange(3, dtype=jnp.int32) + position - 1
    return (offsets >= 0) & (offsets < count)


def per_device(hidden, projection, adaptive_shift, adaptive_scale, query_gain, key_gain):
    frames, row_count, columns, features = hidden.shape
    head_dim = query_gain.shape[0]
    inner_width = projection.shape[1] // 3
    head_count = inner_width // head_dim
    normed = layer_norm(hidden, adaptive_shift, adaptive_scale)
    projected = jnp.dot(
        normed,
        lax.all_gather(projection, "tm", axis=0, tiled=True),
        preferred_element_type=jnp.float32,
    )
    queries = head_norm(projected[:, :inner_width], query_gain)
    keys_local = head_norm(projected[:, inner_width : 2 * inner_width], key_gain)
    values_local = projected[:, 2 * inner_width :].astype(jnp.bfloat16)
    grid_shape = (1, 1, frames, row_count, columns, inner_width)
    key_grid = keys_local.reshape(grid_shape)
    value_grid = values_local.reshape(grid_shape)
    key_window, value_window = (
        extended(key_grid, (("tm", 0), ("height", 1)), 1),
        extended(value_grid, (("tm", 0), ("height", 1)), 1),
    )
    width_tiles = columns // TILE_W
    window_tiles = min(3, width_tiles)
    window_cols = window_tiles * TILE_W
    time_valid = neighbour_valid(lax.axis_index("tm"), lax.axis_size("tm"))
    height_valid = neighbour_valid(lax.axis_index("height"), lax.axis_size("height"))
    query_grid = queries.reshape(frames, row_count, columns, inner_width)
    score_scale = head_dim ** (-0.5)
    slab_offsets = jnp.arange(window_cols, dtype=jnp.int32) // TILE_W

    def attend_tile(tile_index):
        first_tile = jnp.clip(tile_index - 1, 0, width_tiles - window_tiles)
        key_slab = key_window.reshape(-1, inner_width)
        value_slab = value_window.reshape(-1, inner_width)
        columns_here = jnp.abs(first_tile + slab_offsets - tile_index) <= 1
        tile_valid = (
            time_valid[:, None, None, None, None]
            & height_valid[None, :, None, None, None]
            & columns_here[None, None, None, None, :]
        )
        key_valid = jnp.broadcast_to(tile_valid, (3, 3, frames, row_count, window_cols)).reshape(-1)
        query_rows = lax.dynamic_slice_in_dim(query_grid, tile_index * TILE_W, TILE_W, 2).reshape(
            -1, inner_width
        )

        def attend_head(head_index):
            head_start = head_index * head_dim
            query_head = lax.dynamic_slice_in_dim(query_rows, head_start, head_dim, 1)
            key_head = lax.dynamic_slice_in_dim(key_slab, head_start, head_dim, 1)
            value_head = lax.dynamic_slice_in_dim(value_slab, head_start, head_dim, 1)
            scores = (
                lax.dot_general(
                    query_head,
                    key_head,
                    (((1,), (1,)), ((), ())),
                    preferred_element_type=jnp.float32,
                )
                * score_scale
            )
            scores = jnp.where(key_valid[None, :], scores, -jnp.inf)
            row_peak = jnp.max(scores, axis=1, keepdims=True)
            weights = jnp.exp(scores - row_peak)
            totals = jnp.sum(weights, axis=1, keepdims=True)
            mixture = (
                jnp.dot(
                    weights.astype(jnp.bfloat16), value_head, preferred_element_type=jnp.float32
                )
                / totals
            )
            return mixture.astype(jnp.bfloat16)

        per_head = lax.map(attend_head, jnp.arange(head_count, dtype=jnp.int32))
        return jnp.transpose(per_head, (1, 0, 2)).reshape(frames, row_count, TILE_W, inner_width)

    tiles_out = lax.map(attend_tile, jnp.arange(width_tiles, dtype=jnp.int32))
    return jnp.transpose(tiles_out, (1, 2, 0, 3, 4)).reshape(
        frames, row_count, columns, inner_width
    )


def solution(mesh):
    return jax.shard_map(
        per_device,
        mesh=mesh,
        in_specs=(P("tm", "height", None, None), P("tm", None), P(), P(), P(), P()),
        out_specs=P("tm", "height", None, None),
        check_vma=False,
    )
```

profile of v0, /device:TPU:7, one launch (start us, length us, event | category | flops | bytes accessed | tf_op | source)
XLA Modules:
  0.0 639.9 jit_solution(10956239748935922497)
XLA Ops:
  7.3 1.6 reduce_sum.45
  9.8 300.7 %all-gather.2.cloned.1.call-done = bf16[1536,4608]{1,0:T(8,128)(2,1)} async-done(((bf16[96,4608]{1,0:T(8,128)(2,1)}), bf16[1536,4608]{1,0:T(8,128)(2,1)}) %all-gather.2.cloned.1.call-update) | async-done | bytes 14155792 | tf_op jit(solution)/shard_map/all_gather | solution.py:57
  310.4 7.0 %fusion.30 = f32[256,4608]{1,0:T(8,128)S(1)} fusion(bf16[256,1536]{1,0:T(8,128)(2,1)S(1)} %fusion.28, bf16[1536,4608]{1,0:T(8,128)(2,1)} %all-gather.2.cloned.1.call-done), kind=kOutput, calls=%fused_computation.57 | convolution fusion | flops 3623878656 | bytes 19660800 | tf_op jit(solution)/shard_map/dot_general | solution.py:55
  317.5 1.6 slice_multiply_fusion
  320.1 1.9 copy.10
  322.2 1.6 copy.11
  324.6 1.6 copy.13
  326.2 3.1 multiply_convert_fusion
  329.3 2.3 collective-permute-start
  332.9 1.5 slice.21
  334.4 7.1 %collective-permute-start.4 = (bf16[1,1,4,4,16,1536]{5,4,3,2,1,0:T(8,128)(2,1)S(1)}, bf16[1,1,4,4,16,1536]{5,4,3,2,1,0:T(8,128)(2,1)S(1)}, u32[]{:S(2)}, u32[]{:S(2)}) collective-permute-start(bf16[1,1,4,4,16,1536]{5,4,3,2,1,0:T(8,128)(2,1)S(1)} %bitcast.59), channel_id=1, source_target_pairs={{0,16},{16,32},{32,48},{48,64},{64,80},{80,96},{96,112},{112,128},... | collective-permute-start | bytes 2359304 | tf_op jit(solution)/shard_map/ppermute | solution.py:17
  342.8 38.7 %collective-permute-done = bf16[1,1,4,4,16,1536]{5,4,3,2,1,0:T(8,128)(2,1)S(1)} collective-permute-done((bf16[1,1,4,4,16,1536]{5,4,3,2,1,0:T(8,128)(2,1)S(1)}, bf16[1,1,4,4,16,1536]{5,4,3,2,1,0:T(8,128)(2,1)S(1)}, u32[]{:S(2)}, u32[]{:S(2)}) %collective-permute-start) | collective-permute-done | bytes 786464 | tf_op jit(solution)/shard_map/ppermute | solution.py:17
  381.5 1.8 pad_maximum_fusion.2
  383.4 7.2 %collective-permute-start.2 = (bf16[3,1,4,4,16,1536]{5,4,3,2,1,0:T(8,128)(2,1)}, bf16[3,1,4,4,16,1536]{5,4,3,2,1,0:T(8,128)(2,1)}, u32[]{:S(2)}, u32[]{:S(2)}) collective-permute-start(bf16[3,1,4,4,16,1536]{5,4,3,2,1,0:T(8,128)(2,1)} %pad_maximum_fusion.2), channel_id=1, source_target_pairs={{0,1},{1,2},{2,3},{3,4},{4,5},{5,6},{6,7},{7,8},{8,9},{9,10},{10,1... | collective-permute-start | bytes 7077896 | tf_op jit(solution)/shard_map/ppermute | solution.py:17
  390.6 1.9 collective-permute-start.3
  392.5 5.8 collective-permute-done.4
  398.3 1.7 pad_maximum_fusion.3
  400.0 31.3 %collective-permute-start.6 = (bf16[3,1,4,4,16,1536]{5,4,3,2,1,0:T(8,128)(2,1)}, bf16[3,1,4,4,16,1536]{5,4,3,2,1,0:T(8,128)(2,1)}, u32[]{:S(2)}, u32[]{:S(2)}) collective-permute-start(bf16[3,1,4,4,16,1536]{5,4,3,2,1,0:T(8,128)(2,1)} %pad_maximum_fusion.3), channel_id=1, source_target_pairs={{0,1},{1,2},{2,3},{3,4},{4,5},{5,6},{6,7},{7,8},{8,9},{9,10},{10,1... | collective-permute-start | bytes 7077896 | tf_op jit(solution)/shard_map/ppermute | solution.py:17
  431.4 1.9 collective-permute-start.7
  433.4 45.2 %collective-permute-done.3 = bf16[3,1,4,4,16,1536]{5,4,3,2,1,0:T(8,128)(2,1)} collective-permute-done((bf16[3,1,4,4,16,1536]{5,4,3,2,1,0:T(8,128)(2,1)}, bf16[3,1,4,4,16,1536]{5,4,3,2,1,0:T(8,128)(2,1)}, u32[]{:S(2)}, u32[]{:S(2)}) %collective-permute-start.3) | collective-permute-done | bytes 2359328 | tf_op jit(solution)/shard_map/ppermute | solution.py:20
  478.6 6.2 pad_maximum_fusion
  484.8 19.1 %collective-permute-done.7 = bf16[3,1,4,4,16,1536]{5,4,3,2,1,0:T(8,128)(2,1)} collective-permute-done((bf16[3,1,4,4,16,1536]{5,4,3,2,1,0:T(8,128)(2,1)}, bf16[3,1,4,4,16,1536]{5,4,3,2,1,0:T(8,128)(2,1)}, u32[]{:S(2)}, u32[]{:S(2)}) %collective-permute-start.7) | collective-permute-done | bytes 2359328 | tf_op jit(solution)/shard_map/ppermute | solution.py:20
  503.9 5.9 pad_maximum_fusion.1
  509.7 121.2 %while.35 = (s32[]{:T(128)}, bf16[2,4,4,8,1536]{4,3,2,1,0:T(8,128)(2,1)}, s32[2]{0:T(128)S(1)}, bf16[4,4,16,1536]{3,2,1,0:T(8,128)(2,1)S(1)}, bf16[3,3,4,4,16,15...) while((s32[]{:T(128)}, ...), condition=%wide.region_9.10_spmd.clone, body=%wide.region_4.9_spmd.clone.sunk | while | flops 153092224 | bytes 14236388 | solution.py:123
  512.5 56.3 %while.36 = (s32[]{:T(128)}, bf16[12,128,128]{2,1,0:T(8,128)(2,1)S(1)}, s32[12]{0:T(128)S(1)}, bf16[128,1536]{1,0:T(8,128)(2,1)S(1)}, bf16[2304,1536]{1,0:T(8,12...) while((s32[]{:T(128)}, ...), condition=%wide.region_8.8_spmd.clone, body=%wide.region_5.7_spmd.clone.sunk | while | flops 153091840 | bytes 4798523 | solution.py:120
  523.3 1.5 fusion.43
  542.1 1.5 fusion.43
  560.9 1.5 fusion.43
  573.1 56.4 %while.36 = (s32[]{:T(128)}, bf16[12,128,128]{2,1,0:T(8,128)(2,1)S(1)}, s32[12]{0:T(128)S(1)}, bf16[128,1536]{1,0:T(8,128)(2,1)S(1)}, bf16[2304,1536]{1,0:T(8,12...) while((s32[]{:T(128)}, ...), condition=%wide.region_8.8_spmd.clone, body=%wide.region_5.7_spmd.clone.sunk | while | flops 153091840 | bytes 4798523 | solution.py:120
  588.6 1.5 fusion.43
  621.5 1.5 fusion.43
  631.0 2.1 copy_bitcast_fusion
  (216 shorter events, 101.4 us)
Async XLA Ops:
  6.5 2.4 copy-start
  6.5 2.8 copy-start.10
  6.5 2.8 copy-start.12
  6.5 2.8 copy-start.11
  6.5 2.9 copy-start.9
  6.5 303.9 %all-gather.2.cloned.1.call-start = ((), (), s32[]{:S(2)}) async-start(), calls=%async_computation | async-start | bytes 15040512 | tf_op jit(solution)/shard_map/all_gather | solution.py:57
  317.5 2.6 copy-start.1
  324.4 1.8 copy-start.2
  329.3 52.1 %collective-permute-start = (bf16[1,1,4,4,16,1536]{5,4,3,2,1,0:T(8,128)(2,1)S(1)}, bf16[1,1,4,4,16,1536]{5,4,3,2,1,0:T(8,128)(2,1)S(1)}, u32[]{:S(2)}, u32[]{:S(2)}) collective-permute-start(bf16[1,1,4,4,16,1536]{5,4,3,2,1,0:T(8,128)(2,1)S(1)} %bitcast.63), channel_id=1, source_target_pairs={{0,16},{16,32},{32,48},{48,64},{64,80},{80,96},{96,112},{112,128},... | collective-permute-start | bytes 2359304 | tf_op jit(solution)/shard_map/ppermute | solution.py:17
  331.6 49.8 %collective-permute-start.1 = (bf16[1,1,4,4,16,1536]{5,4,3,2,1,0:T(8,128)(2,1)S(1)}, bf16[1,1,4,4,16,1536]{5,4,3,2,1,0:T(8,128)(2,1)S(1)}, u32[]{:S(2)}, u32[]{:S(2)}) collective-permute-start(bf16[1,1,4,4,16,1536]{5,4,3,2,1,0:T(8,128)(2,1)S(1)} %bitcast.64), channel_id=1, source_target_pairs={{16,0},{32,16},{48,32},{64,48},{80,64},{96,80},{112,96},{128,112},... | collective-permute-start | bytes 2359304 | tf_op jit(solution)/shard_map/ppermute | solution.py:20
  334.4 63.9 %collective-permute-start.4 = (bf16[1,1,4,4,16,1536]{5,4,3,2,1,0:T(8,128)(2,1)S(1)}, bf16[1,1,4,4,16,1536]{5,4,3,2,1,0:T(8,128)(2,1)S(1)}, u32[]{:S(2)}, u32[]{:S(2)}) collective-permute-start(bf16[1,1,4,4,16,1536]{5,4,3,2,1,0:T(8,128)(2,1)S(1)} %bitcast.59), channel_id=1, source_target_pairs={{0,16},{16,32},{32,48},{48,64},{64,80},{80,96},{96,112},{112,128},... | collective-permute-start | bytes 2359304 | tf_op jit(solution)/shard_map/ppermute | solution.py:17
  341.5 56.8 %collective-permute-start.5 = (bf16[1,1,4,4,16,1536]{5,4,3,2,1,0:T(8,128)(2,1)S(1)}, bf16[1,1,4,4,16,1536]{5,4,3,2,1,0:T(8,128)(2,1)S(1)}, u32[]{:S(2)}, u32[]{:S(2)}) collective-permute-start(bf16[1,1,4,4,16,1536]{5,4,3,2,1,0:T(8,128)(2,1)S(1)} %bitcast.60), channel_id=1, source_target_pairs={{16,0},{32,16},{48,32},{64,48},{80,64},{96,80},{112,96},{128,112},... | collective-permute-start | bytes 2359304 | tf_op jit(solution)/shard_map/ppermute | solution.py:20
  381.5 1.8 copy-start.3
  381.5 1.9 copy-start.6
  383.4 50.0 %collective-permute-start.2 = (bf16[3,1,4,4,16,1536]{5,4,3,2,1,0:T(8,128)(2,1)}, bf16[3,1,4,4,16,1536]{5,4,3,2,1,0:T(8,128)(2,1)}, u32[]{:S(2)}, u32[]{:S(2)}) collective-permute-start(bf16[3,1,4,4,16,1536]{5,4,3,2,1,0:T(8,128)(2,1)} %pad_maximum_fusion.2), channel_id=1, source_target_pairs={{0,1},{1,2},{2,3},{3,4},{4,5},{5,6},{6,7},{7,8},{8,9},{9,10},{10,1... | collective-permute-start | bytes 7077896 | tf_op jit(solution)/shard_map/ppermute | solution.py:17
  390.6 88.0 %collective-permute-start.3 = (bf16[3,1,4,4,16,1536]{5,4,3,2,1,0:T(8,128)(2,1)}, bf16[3,1,4,4,16,1536]{5,4,3,2,1,0:T(8,128)(2,1)}, u32[]{:S(2)}, u32[]{:S(2)}) collective-permute-start(bf16[3,1,4,4,16,1536]{5,4,3,2,1,0:T(8,128)(2,1)} %pad_maximum_fusion.2), channel_id=1, source_target_pairs={{1,0},{2,1},{3,2},{4,3},{5,4},{6,5},{7,6},{8,7},{9,8},{10,9},{11,1... | collective-permute-start | bytes 7077896 | tf_op jit(solution)/shard_map/ppermute | solution.py:20
  398.3 1.7 copy-start.4
  400.0 84.7 %collective-permute-start.6 = (bf16[3,1,4,4,16,1536]{5,4,3,2,1,0:T(8,128)(2,1)}, bf16[3,1,4,4,16,1536]{5,4,3,2,1,0:T(8,128)(2,1)}, u32[]{:S(2)}, u32[]{:S(2)}) collective-permute-start(bf16[3,1,4,4,16,1536]{5,4,3,2,1,0:T(8,128)(2,1)} %pad_maximum_fusion.3), channel_id=1, source_target_pairs={{0,1},{1,2},{2,3},{3,4},{4,5},{5,6},{6,7},{7,8},{8,9},{9,10},{10,1... | collective-permute-start | bytes 7077896 | tf_op jit(solution)/shard_map/ppermute | solution.py:17
  431.4 72.5 %collective-permute-start.7 = (bf16[3,1,4,4,16,1536]{5,4,3,2,1,0:T(8,128)(2,1)}, bf16[3,1,4,4,16,1536]{5,4,3,2,1,0:T(8,128)(2,1)}, u32[]{:S(2)}, u32[]{:S(2)}) collective-permute-start(bf16[3,1,4,4,16,1536]{5,4,3,2,1,0:T(8,128)(2,1)} %pad_maximum_fusion.3), channel_id=1, source_target_pairs={{1,0},{2,1},{3,2},{4,3},{5,4},{6,5},{7,6},{8,7},{9,8},{10,9},{11,1... | collective-permute-start | bytes 7077896 | tf_op jit(solution)/shard_map/ppermute | solution.py:20
  433.4 70.5 %copy-start.5 = (bf16[1,1,4,4,16,1536]{5,4,3,2,1,0:T(8,128)(2,1)S(1)}, bf16[1,1,4,4,16,1536]{5,4,3,2,1,0:T(8,128)(2,1)}, u32[]{:S(2)}) copy-start(bf16[1,1,4,4,16,1536]{5,4,3,2,1,0:T(8,128)(2,1)} %copy-done.4) | copy-start | bytes 2359300
  512.5 56.9 %copy-start.7 = (bf16[2,4,4,8,1536]{4,3,2,1,0:T(8,128)(2,1)S(1)}, bf16[2,4,4,8,1536]{4,3,2,1,0:T(8,128)(2,1)}, u32[]{:S(2)}) copy-start(bf16[2,4,4,8,1536]{4,3,2,1,0:T(8,128)(2,1)} %get-tuple-element.412) | copy-start | bytes 2359300 | tf_op jit(solution)/shard_map/while
  569.5 0.9 copy-start.8
  573.1 56.9 %copy-start.7 = (bf16[2,4,4,8,1536]{4,3,2,1,0:T(8,128)(2,1)S(1)}, bf16[2,4,4,8,1536]{4,3,2,1,0:T(8,128)(2,1)}, u32[]{:S(2)}) copy-start(bf16[2,4,4,8,1536]{4,3,2,1,0:T(8,128)(2,1)} %get-tuple-element.412) | copy-start | bytes 2359300 | tf_op jit(solution)/shard_map/while
  630.1 0.9 copy-start.8
Sparse Core Ops, SparseCore 0:
  9.2 301.2 all-gather.1
where the time goes:
time: 647 us; the launch traced here: 640 us
  waiting for transfers between devices  410 us (63%)
  matrix products  77.8 us (12%)
  starting transfers between devices  54.4 us (8%)
  local copies, waits for them, and re-layouts  33.2 us (5%)
  other arithmetic  32.2 us (5%)
  loops' own time  18.6 us (3%)
  between operations  13.7 us (2%)
    all_gather x1, waiting for transfers between devices, per_device(): lax.all_gather(projection, 'tm', axis=0, tiled=True)  301 us
    ppermute x4, waiting for transfers between devices, extended(): lax.ppermute(lax.slice_in_dim(block, 0, width, axis=dim), axis, backward)  64.3 us
    ppermute x4, starting transfers between devices, extended(): lax.ppermute(lax.slice_in_dim(block, block.shape[dim] - width, None, axis...  47.9 us
    ppermute x4, waiting for transfers between devices, extended(): lax.ppermute(lax.slice_in_dim(block, block.shape[dim] - width, None, axis...  44.5 us
    dot_general x24, matrix products, attend_head(): lax.dot_general(query_head, key_head, (((1,), (1,)), ((), ())), preferred...  35.4 us
    dot_general x24, matrix products, attend_head(): jnp.dot(weights.astype(jnp.bfloat16), value_head, preferred_element_type=...  35.3 us
    another operation x2, loops' own time, attend_tile(): per_head = lax.map(attend_head, jnp.arange(head_count, dtype=jnp.int32))  16 us
    concatenate x4, other arithmetic, extended(): block = jnp.concatenate([low, block, high], axis=dim)  15.6 us
  transfers between devices with their start and end apart: 9, of which 5 were waited for; matrix products, arithmetic and copies ran while one was open for 2% of the time, Pallas kernels for 0%

commit v1 on v0

v1 whole, which is shorter than its diff:
```python
import math

import jax
import jax.numpy as jnp
import numpy as np
from jax import lax
from jax.experimental import pallas as pl
from jax.experimental.pallas import tpu as pltpu
from jax.sharding import Mesh, PartitionSpec as P

AXES = ("z", "yl", "x", "yh", "core")
SIZES = (8, 2, 4, 2, 2)
TOKENS = 256
D = 1536
HD = 128
GROUP_HEADS = 3
GROUP = GROUP_HEADS * HD
ROWS = 96
EPSILON = 1e-06
SCORE_SCALE = HD ** (-0.5) * math.log2(math.e)
F32 = jnp.float32
BF16 = jnp.bfloat16


def linear(z, y, x, core):
    return (((z % 8 * 2 + y % 2) * 4 + x % 4) * 2 + y % 4 // 2) * 2 + core


def pairs(move):
    return [
        (linear(z, y, x, core), linear(*move(z, y, x, core)))
        for z in range(8)
        for y in range(4)
        for x in range(4)
        for core in range(2)
    ]


def shift(array, dz=0, dy=0):
    return lax.ppermute(array, AXES, pairs(lambda z, y, x, core: (z + dz, y + dy, x, core)))


def swap_cores(array):
    return lax.ppermute(array, AXES, pairs(lambda z, y, x, core: (z, y, x, 1 - core)))


def outward(array, dz=0):
    return lax.ppermute(
        array, AXES, pairs(lambda z, y, x, core: (z + dz, y, x + (1 if core else -1), 1 - core))
    )


def swap_rows_owner(array):
    def move(z, y, x, core):
        yh, yl = y // 2, y % 2
        return (z, y, x, core) if core == yl else (z, yh * 2 + 1 - yl, x, 1 - core)

    return lax.ppermute(array, AXES, pairs(move))


def layer_norm(activations, adaptive_shift, adaptive_scale):
    centre = jnp.mean(activations, axis=1, keepdims=True)
    shifted = activations - centre
    spread = jnp.mean(shifted * shifted, axis=1, keepdims=True)
    scaled = shifted * lax.rsqrt(spread + EPSILON) * (1.0 + adaptive_scale) + adaptive_shift
    return scaled.astype(BF16)


STEPS = (0, 1, -1, 2)
HOPS = (0, 4, 3, -3, 2, -2, 1, -1)


def project_kernel(place, *refs):
    tokens = refs[:4]
    mine, other, query_gain, key_gain = refs[4:8]
    q_out, own, low, high, edge, edge_low, edge_high = refs[8:15]
    weights = refs[15]
    z, y, core = place[0], place[1], place[2]
    for index, hop in enumerate(HOPS):
        start = lax.rem(z - hop + 8, 8) * (2 * ROWS)
        weights[pl.ds(pl.multiple_of(start + core * ROWS, 32), ROWS), :] = mine[index]
        weights[pl.ds(pl.multiple_of(start + (1 - core) * ROWS, 32), ROWS), :] = other[index]

    def head_norm(block, gain):
        mean_square = jnp.mean(block * block, axis=1, keepdims=True)
        return (block * lax.rsqrt(mean_square + EPSILON) * gain[...]).astype(BF16)

    for index, step in enumerate(STEPS):
        source = lax.rem(y - step + 4, 4)
        yl = lax.rem(source, 2)
        role = jnp.where(source // 2 == core, 0, 1)
        rows = tokens[index][...]
        projected = jnp.dot(rows, weights[...], preferred_element_type=F32)
        for head in range(GROUP_HEADS):
            part = lambda kind: projected[:, kind * GROUP + head * HD : kind * GROUP + (head + 1) * HD]
            q = head_norm(part(0), query_gain)
            k = head_norm(part(1), key_gain)
            v = part(2).astype(BF16)
            q_out[yl * 2 + role, :, head * HD : (head + 1) * HD] = q
            ks = slice(head * 2 * HD, head * 2 * HD + HD)
            vs = slice(head * 2 * HD + HD, (head + 1) * 2 * HD)
            own[yl, role, :, ks] = k
            own[yl, role, :, vs] = v
    low[...] = own[0]
    high[...] = own[1]
    edge[...] = own[:, 0]
    edge_low[...] = own[0, 0]
    edge_high[...] = own[1, 0]


def project(place, tokens, mine, other, query_gain, key_gain):
    vmem = pl.BlockSpec(memory_space=pltpu.VMEM)
    kv = lambda *lead: jax.ShapeDtypeStruct(lead + (TOKENS, 2 * GROUP), BF16)
    return pl.pallas_call(
        project_kernel,
        name="project",
        out_shape=(
            jax.ShapeDtypeStruct((4, TOKENS, GROUP), BF16),
            kv(2, 2),
            kv(2),
            kv(2),
            kv(2),
            kv(),
            kv(),
        ),
        in_specs=[pl.BlockSpec(memory_space=pltpu.SMEM)] + [vmem] * 8,
        out_specs=[vmem] * 7,
        scratch_shapes=[pltpu.VMEM((D, 3 * GROUP), BF16)],
        compiler_params=pltpu.CompilerParams(vmem_limit_bytes=48 * 1024 * 1024),
        cost_estimate=pl.CostEstimate(
            flops=2 * 4 * TOKENS * D * 3 * GROUP, bytes_accessed=12_000_000, transcendentals=0
        ),
    )(place, *tokens, mine, other, query_gain.reshape(1, HD), key_gain.reshape(1, HD))


def attend_kernel(valid, q, own, mate, below, above, mate_below, mate_above, edge, edge_below, edge_above, out):
    penalty = lambda flag: jnp.where(flag > 0, 0.0, 1e30).astype(F32)
    no_below = penalty(valid[0])
    no_above = penalty(valid[1])
    no_edge = penalty(valid[2])
    core = valid[3]
    ones = jnp.ones((TOKENS, HD), BF16)
    for yl in range(2):
        row, mate_row, edge_row, no_row = (
            (below, mate_below, edge_below, no_below) if yl == 0 else (above, mate_above, edge_above, no_above)
        )
        for role in range(2):
            if role == 0:
                groups = [
                    (None, [own[0, 0], own[1, 0], mate[0, 1], mate[1, 1]]),
                    (no_row, [row[0], mate_row[1]]),
                    (no_edge, [edge[0], edge[1]]),
                    (jnp.maximum(no_row, no_edge), [edge_row[...]]),
                ]
            else:
                groups = [
                    (None, [own[0, 1], own[1, 1], mate[0, 0], mate[1, 0], mate[0, 1], mate[1, 1]]),
                    (no_row, [row[1], mate_row[0], mate_row[1]]),
                ]
            query = q[yl * 2 + role]
            scored = []
            peak = None
            for cost, tiles in groups:
                top = None
                for tile in tiles:
                    scores = lax.dot_general(
                        query, tile[:, :HD], (((1,), (1,)), ((), ())), preferred_element_type=F32
                    )
                    scored.append((cost, tile, scores))
                    top = scores if top is None else jnp.maximum(top, scores)
                top = jnp.max(top, axis=1, keepdims=True)
                if cost is not None:
                    top = top - cost
                peak = top if peak is None else jnp.maximum(peak, top)
            peak = peak * SCORE_SCALE
            total = None
            for cost, tile, scores in scored:
                base = peak if cost is None else peak + cost
                weights = jnp.exp2(scores * SCORE_SCALE - base).astype(BF16)
                wide = jnp.concatenate([tile[:, HD:], ones], axis=1)
                mixed = jnp.dot(weights, wide, preferred_element_type=F32)
                total = mixed if total is None else total + mixed
            yh = core if role == 0 else 1 - core
            out[yh * 2 + yl] = (total[:, :HD] / total[:, HD:]).astype(BF16)


def attend(valid, q, *kv):
    def spec(array, width):
        lead = array.ndim - 1
        return pl.BlockSpec(array.shape[:-1] + (width,), lambda h: (0,) * lead + (h,))

    return pl.pallas_call(
        attend_kernel,
        name="attend",
        grid=(GROUP_HEADS,),
        out_shape=jax.ShapeDtypeStruct((4, TOKENS, GROUP), BF16),
        in_specs=[pl.BlockSpec(memory_space=pltpu.SMEM), spec(q, HD)] + [spec(a, 2 * HD) for a in kv],
        out_specs=pl.BlockSpec((4, TOKENS, HD), lambda h: (0, 0, h)),
        compiler_params=pltpu.CompilerParams(
            dimension_semantics=("arbitrary",), vmem_limit_bytes=48 * 1024 * 1024
        ),
        cost_estimate=pl.CostEstimate(
            flops=4 * 12 * TOKENS * 9 * TOKENS * HD,
            bytes_accessed=10_000_000,
            transcendentals=12 * TOKENS * 9 * TOKENS,
        ),
    )(valid, q, *kv)


def per_device(hidden, projection, adaptive_shift, adaptive_scale, query_gain, key_gain):
    z, yl, x, yh, core = (lax.axis_index(a) for a in AXES)
    y = yh * 2 + yl

    inner = projection.shape[1] // 3
    start = (yh * 2 + core) * GROUP
    columns = jnp.concatenate(
        [lax.dynamic_slice_in_dim(projection, kind * inner + start, GROUP, 1) for kind in range(3)], axis=1
    )
    base = swap_rows_owner(columns)
    mine = jnp.stack([base] + [shift(base, dz=hop) for hop in HOPS[1:]])
    other = swap_cores(mine)

    normed = layer_norm(hidden.reshape(TOKENS, D), adaptive_shift, adaptive_scale)
    tokens = [normed] + [shift(normed, dy=step) for step in STEPS[1:]]

    place = jnp.stack([z, y, core]).astype(jnp.int32)
    q, own, low, high, edge, edge_low, edge_high = project(place, tokens, mine, other, query_gain, key_gain)
    mate = swap_cores(own)
    below = shift(high, dz=1)
    above = shift(low, dz=-1)
    edge_in = outward(edge)
    edge_below = outward(edge_high, dz=1)
    edge_above = outward(edge_low, dz=-1)
    mate_below = swap_cores(below)
    mate_above = swap_cores(above)
    last_x = jnp.where(core == 0, 0, 3)
    valid = jnp.stack([z > 0, z < 7, x != last_x, core]).astype(jnp.int32)
    attended = attend(
        valid, q, own, mate, below, above, mate_below, mate_above, edge_in, edge_below, edge_above
    )
    back = lax.all_to_all(attended, ("yh", "yl"), 0, 0)
    return jnp.transpose(back, (1, 0, 2)).reshape(hidden.shape)


def solution(mesh):
    split = Mesh(np.asarray(mesh.devices).reshape(SIZES), AXES)
    tm, height = ("z", "yl"), ("x", "yh", "core")
    return jax.shard_map(
        per_device,
        mesh=split,
        in_specs=(P(tm, height, None, None), P(tm, None), P(), P(), P(), P()),
        out_specs=P(tm, height, None, None),
        check_vma=False,
    )
```

time: 647 us -> 199 us (0.31)
  waiting for transfers between devices: 410 us -> 101 us
  matrix products: 77.8 us -> 0 us
  other arithmetic: 32.2 us -> 2.4 us
  Pallas kernels: 0 us -> 21.3 us
  local copies, waits for them, and re-layouts: 33.2 us -> 12.4 us
  loops' own time: 18.6 us -> 0 us
  blocking collectives: 0 us -> 16.2 us
  between operations: 13.7 us -> 0.15 us
  starting transfers between devices: 54.4 us -> 44.2 us
    all_gather x1 -> x0, waiting for transfers between devices: 301 us -> none  [per_device(): lax.all_gather(projection, 'tm', axis=0, tiled=True)]
    dot_general x49 -> x0, matrix products: 77.8 us -> none  [the longest x24 35.4 us: attend_head(): lax.dot_general(query_head, key_head, (((1,), (1,)), ((), ())), preferred...]
    pallas_call x0 -> x2, Pallas kernels: none -> 21.3 us  [the longest x1 12.8 us: attend(): pl.pallas_call(attend_kernel, name='attend', grid=(GROUP_HEADS,), out_sha...]
    another operation x3 -> x0, loops' own time: 18.6 us -> none  [the longest x2 16 us: attend_tile(): per_head = lax.map(attend_head, jnp.arange(head_count, dtype=jnp.int32))]
    all_to_all x0 -> x1, blocking collectives: none -> 16.2 us  [per_device(): back = lax.all_to_all(attended, ('yh', 'yl'), 0, 0)]
    dynamic_slice x28 -> x1, local copies, waits for them, and re-layouts: 16.7 us -> 0.98 us  [per_device(): lax.dynamic_slice_in_dim(projection, kind * inner + start, GROUP, 1)]
    concatenate x4 -> x1, other arithmetic: 15.6 us -> 0.02 us  [per_device(): jnp.concatenate([lax.dynamic_slice_in_dim(projection, kind * inner + star...]
    ppermute x8 -> x20, starting transfers between devices: 54.3 us -> 44.2 us  [the longest x12 29.2 us: shift(): lax.ppermute(array, AXES, pairs(lambda z, y, x, core: (z + dz, y + dy, x,...]
  transfers between devices with their start and end apart: 9 -> 20, of which waited for: 5 -> 10; matrix products, arithmetic and copies ran while one was open for 2% -> 4% of each run, Pallas kernels for 0% -> 0%
where the time goes in v1:
time: 199 us; the launch traced here: 197 us
  waiting for transfers between devices  101 us (51%)
  starting transfers between devices  44.2 us (22%)
  Pallas kernels  21.3 us (11%)
  blocking collectives  16.2 us (8%)
  local copies, waits for them, and re-layouts  12.4 us (6%)
  other arithmetic  2.4 us (1%)
    ppermute x12, waiting for transfers between devices, shift(): lax.ppermute(array, AXES, pairs(lambda z, y, x, core: (z + dz, y + dy, x,...  82.7 us
    ppermute x12, starting transfers between devices, shift(): lax.ppermute(array, AXES, pairs(lambda z, y, x, core: (z + dz, y + dy, x,...  29.2 us
    all_to_all x1, blocking collectives, per_device(): back = lax.all_to_all(attended, ('yh', 'yl'), 0, 0)  16.2 us
    ppermute x3, waiting for transfers between devices, outward(): lax.ppermute(array, AXES, pairs(lambda z, y, x, core: (z + dz, y, x + (1...  15.7 us
    pallas_call x1, Pallas kernels, attend(): pl.pallas_call(attend_kernel, name='attend', grid=(GROUP_HEADS,), out_sha...  12.8 us
    unnamed x29, local copies, waits for them, and re-layouts  8.74 us
    pallas_call x1, Pallas kernels, project(): pl.pallas_call(project_kernel, name='project', out_shape=(jax.ShapeDtypeS...  8.51 us
    ppermute x3, starting transfers between devices, outward(): lax.ppermute(array, AXES, pairs(lambda z, y, x, core: (z + dz, y, x + (1...  6.98 us
  transfers between devices with their start and end apart: 20, of which 10 were waited for; matrix products, arithmetic and copies ran while one was open for 4% of the time, Pallas kernels for 0%

profile of v1, /device:TPU:7, one launch (start us, length us, event | category | flops | bytes accessed | tf_op | source)
XLA Modules:
  0.0 197.4 jit_solution(17445468449278541139)
XLA Ops:
  0.0 1.0 constant_dynamic-slice_fusion.2
  1.0 3.8 %collective-permute-start.3 = (bf16[96,1152]{1,0:T(8,128)(2,1)S(1)}, bf16[96,1152]{1,0:T(8,128)(2,1)S(1)}, u32[]{:S(2)}, u32[]{:S(2)}) collective-permute-start(bf16[96,1152]{1,0:T(8,128)(2,1)S(1)} %pad_maximum_fusion), channel_id=1, source_target_pairs={{0,0},{1,16},{4,4},{5,20},{8,8},{9,24},{12,12},{13,28},{16,1},{17,... | collective-permute-start | bytes 663560 | tf_op jit(solution)/shard_map/ppermute | solution.py:58
  4.8 1.6 reduce_sum.18
  6.4 2.3 %collective-permute-done.3 = bf16[96,1152]{1,0:T(8,128)(2,1)S(1)} collective-permute-done((bf16[96,1152]{1,0:T(8,128)(2,1)S(1)}, bf16[96,1152]{1,0:T(8,128)(2,1)S(1)}, u32[]{:S(2)}, u32[]{:S(2)}) %collective-permute-start.3) | collective-permute-done | bytes 221216 | tf_op jit(solution)/shard_map/ppermute | solution.py:58
  8.7 5.6 %collective-permute-start.10 = (bf16[96,1152]{1,0:T(8,128)(2,1)S(1)}, bf16[96,1152]{1,0:T(8,128)(2,1)S(1)}, u32[]{:S(2)}, u32[]{:S(2)}) collective-permute-start(bf16[96,1152]{1,0:T(8,128)(2,1)S(1)} %collective-permute-done.3), channel_id=1, source_target_pairs={{0,224},{1,225},{4,228},{5,229},{8,232},{9,233},{12,236},{13,237},... | collective-permute-start | bytes 663560 | tf_op jit(solution)/shard_map/ppermute | solution.py:40
  14.3 1.9 collective-permute-start.8
  16.6 2.8 %collective-permute-start.4 = (bf16[96,1152]{1,0:T(8,128)(2,1)S(1)}, bf16[96,1152]{1,0:T(8,128)(2,1)S(1)}, u32[]{:S(2)}, u32[]{:S(2)}) collective-permute-start(bf16[96,1152]{1,0:T(8,128)(2,1)S(1)} %collective-permute-done.3), channel_id=1, source_target_pairs={{0,128},{1,129},{4,132},{5,133},{8,136},{9,137},{12,140},{13,141},... | collective-permute-start | bytes 663560 | tf_op jit(solution)/shard_map/ppermute | solution.py:40
  20.1 13.7 %collective-permute-done.4 = bf16[96,1152]{1,0:T(8,128)(2,1)S(1)} collective-permute-done((bf16[96,1152]{1,0:T(8,128)(2,1)S(1)}, bf16[96,1152]{1,0:T(8,128)(2,1)S(1)}, u32[]{:S(2)}, u32[]{:S(2)}) %collective-permute-start.4) | collective-permute-done | bytes 221216 | tf_op jit(solution)/shard_map/ppermute | solution.py:40
  33.9 1.0 collective-permute-start.5
  35.6 15.1 %collective-permute-done.5 = bf16[96,1152]{1,0:T(8,128)(2,1)S(1)} collective-permute-done((bf16[96,1152]{1,0:T(8,128)(2,1)S(1)}, bf16[96,1152]{1,0:T(8,128)(2,1)S(1)}, u32[]{:S(2)}, u32[]{:S(2)}) %collective-permute-start.5) | collective-permute-done | bytes 221216 | tf_op jit(solution)/shard_map/ppermute | solution.py:40
  50.7 3.9 %collective-permute-start.6 = (bf16[96,1152]{1,0:T(8,128)(2,1)S(1)}, bf16[96,1152]{1,0:T(8,128)(2,1)S(1)}, u32[]{:S(2)}, u32[]{:S(2)}) collective-permute-start(bf16[96,1152]{1,0:T(8,128)(2,1)S(1)} %collective-permute-done.3), channel_id=1, source_target_pairs={{0,160},{1,161},{4,164},{5,165},{8,168},{9,169},{12,172},{13,173},... | collective-permute-start | bytes 663560 | tf_op jit(solution)/shard_map/ppermute | solution.py:40
  55.3 9.2 %collective-permute-done.6 = bf16[96,1152]{1,0:T(8,128)(2,1)S(1)} collective-permute-done((bf16[96,1152]{1,0:T(8,128)(2,1)S(1)}, bf16[96,1152]{1,0:T(8,128)(2,1)S(1)}, u32[]{:S(2)}, u32[]{:S(2)}) %collective-permute-start.6) | collective-permute-done | bytes 221216 | tf_op jit(solution)/shard_map/ppermute | solution.py:40
  69.0 7.2 %collective-permute-start.2 = (bf16[256,1536]{1,0:T(8,128)(2,1)S(1)}, bf16[256,1536]{1,0:T(8,128)(2,1)S(1)}, u32[]{:S(2)}, u32[]{:S(2)}) collective-permute-start(bf16[256,1536]{1,0:T(8,128)(2,1)S(1)} %fusion.3.refs_0_), channel_id=1, source_target_pairs={{0,2},{1,3},{4,6},{5,7},{8,10},{9,11},{12,14},{13,15},{16,18},{17,... | collective-permute-start | bytes 2359304 | tf_op jit(solution)/shard_map/ppermute | solution.py:40
  76.1 1.5 collective-permute-start
  77.7 16.4 %collective-permute-done.2.refs_3_ = bf16[256,1536]{1,0:T(8,128)(2,1)S(1)} collective-permute-done((bf16[256,1536]{1,0:T(8,128)(2,1)S(1)}, bf16[256,1536]{1,0:T(8,128)(2,1)S(1)}, u32[]{:S(2)}, u32[]{:S(2)}) %collective-permute-start.2) | collective-permute-done | bytes 786464 | tf_op jit(solution)/shard_map/ppermute | solution.py:40
  94.1 9.6 %collective-permute-done.1.refs_2_ = bf16[256,1536]{1,0:T(8,128)(2,1)S(1)} collective-permute-done((bf16[256,1536]{1,0:T(8,128)(2,1)S(1)}, bf16[256,1536]{1,0:T(8,128)(2,1)S(1)}, u32[]{:S(2)}, u32[]{:S(2)}) %collective-permute-start.1) | collective-permute-done | bytes 786464 | tf_op jit(solution)/shard_map/ppermute | solution.py:40
  103.7 7.4 %collective-permute-done.refs_1_ = bf16[256,1536]{1,0:T(8,128)(2,1)S(1)} collective-permute-done((bf16[256,1536]{1,0:T(8,128)(2,1)S(1)}, bf16[256,1536]{1,0:T(8,128)(2,1)S(1)}, u32[]{:S(2)}, u32[]{:S(2)}) %collective-permute-start) | collective-permute-done | bytes 786464 | tf_op jit(solution)/shard_map/ppermute | solution.py:40
  111.1 8.5 %project.1 = (bf16[4,256,384]{2,1,0:T(8,128)(2,1)S(1)}, bf16[2,2,256,768]{3,2,1,0:T(8,128)(2,1)}, bf16[2,256,768]{2,1,0:T(8,128)(2,1)S(1)}, bf16[2,256,768]{2,1,...) custom-call(s32[3]{0:T(128)S(1)} %pad_add_fusion.1.place, ...), custom_call_target="tpu_custom_call" | custom-call | flops 3623878656 | bytes 12000000 | tf_op jit(solution)/shard_map/project/pallas_call | solution.py:114
  120.4 4.9 %collective-permute-start.13 = (bf16[2,256,768]{2,1,0:T(8,128)(2,1)S(1)}, bf16[2,256,768]{2,1,0:T(8,128)(2,1)S(1)}, u32[]{:S(2)}, u32[]{:S(2)}) collective-permute-start(bf16[2,256,768]{2,1,0:T(8,128)(2,1)S(1)} %get-tuple-element.14), channel_id=1, source_target_pairs={{0,32},{1,33},{4,36},{5,37},{8,40},{9,41},{12,44},{13,45},{16,48},... | collective-permute-start | bytes 2359304 | tf_op jit(solution)/shard_map/ppermute | solution.py:40
  126.1 1.5 collective-permute-start.18
  127.7 2.9 %collective-permute-start.17 = (bf16[2,256,768]{2,1,0:T(8,128)(2,1)S(1)}, bf16[2,256,768]{2,1,0:T(8,128)(2,1)}, u32[]{:S(2)}, u32[]{:S(2)}) collective-permute-start(bf16[2,256,768]{2,1,0:T(8,128)(2,1)S(1)} %get-tuple-element.16), channel_id=1, source_target_pairs={{0,13},{1,4},{4,1},{5,8},{8,5},{9,12},{12,9},{13,0},{16,29},{17,20... | collective-permute-start | bytes 2359304 | tf_op jit(solution)/shard_map/ppermute | solution.py:48
  130.5 11.3 %collective-permute-done.13.below = bf16[2,256,768]{2,1,0:T(8,128)(2,1)S(1)} collective-permute-done((bf16[2,256,768]{2,1,0:T(8,128)(2,1)S(1)}, bf16[2,256,768]{2,1,0:T(8,128)(2,1)S(1)}, u32[]{:S(2)}, u32[]{:S(2)}) %collective-permute-start.13) | collective-permute-done | bytes 786464 | tf_op jit(solution)/shard_map/ppermute | solution.py:40
  141.8 2.2 %collective-permute-start.15 = (bf16[2,256,768]{2,1,0:T(8,128)(2,1)S(1)}, bf16[2,256,768]{2,1,0:T(8,128)(2,1)S(1)}, u32[]{:S(2)}, u32[]{:S(2)}) collective-permute-start(bf16[2,256,768]{2,1,0:T(8,128)(2,1)S(1)} %collective-permute-done.13.below), channel_id=1, source_target_pairs={{0,1},{1,0},{4,5},{5,4},{8,9},{9,8},{12,13},{13,12},{16,17},{17,16... | collective-permute-start | bytes 2359304 | tf_op jit(solution)/shard_map/ppermute | solution.py:44
  144.1 1.3 collective-permute-start.16
  145.3 4.9 %collective-permute-done.18.edge_below = bf16[256,768]{1,0:T(8,128)(2,1)S(1)} collective-permute-done((bf16[256,768]{1,0:T(8,128)(2,1)S(1)}, bf16[256,768]{1,0:T(8,128)(2,1)S(1)}, u32[]{:S(2)}, u32[]{:S(2)}) %collective-permute-start.18) | collective-permute-done | bytes 393248 | tf_op jit(solution)/shard_map/ppermute | solution.py:48
  151.0 2.6 %collective-permute-start.19 = (bf16[256,768]{1,0:T(8,128)(2,1)S(1)}, bf16[256,768]{1,0:T(8,128)(2,1)}, u32[]{:S(2)}, u32[]{:S(2)}) collective-permute-start(bf16[256,768]{1,0:T(8,128)(2,1)S(1)} %get-tuple-element.18), channel_id=1, source_target_pairs={{0,237},{1,228},{4,225},{5,232},{8,229},{9,236},{12,233},{13,224},... | collective-permute-start | bytes 1179656 | tf_op jit(solution)/shard_map/ppermute | solution.py:48
  153.7 10.8 %collective-permute-done.19.edge_above = bf16[256,768]{1,0:T(8,128)(2,1)} collective-permute-done((bf16[256,768]{1,0:T(8,128)(2,1)S(1)}, bf16[256,768]{1,0:T(8,128)(2,1)}, u32[]{:S(2)}, u32[]{:S(2)}) %collective-permute-start.19) | collective-permute-done | bytes 393248 | tf_op jit(solution)/shard_map/ppermute | solution.py:48
  164.5 1.0 copy-done.1
  165.5 1.1 copy-done.5
  166.6 12.8 %attend.1 = bf16[4,256,384]{2,1,0:T(8,128)(2,1)S(1)} custom-call(s32[4]{0:T(128)S(1)} %pad_add_fusion.valid, bf16[4,256,384]{2,1,0:T(8,128)(2,1)S(1)} %copy-done.5, bf16[2,2,256,768]{3,2,1,0:T(8,128)(2,1)} %get-tuple-element.13.own, bf16[2,2,256,768]{3,2,1,0:T(8,128)(2,1)} %collective-permute-done.12.mate, ...), custom_call_target="tpu_custom_call" | custom-call | flops 3623878656 | bytes 10000000 | tf_op jit(solution)/shard_map/attend/pallas_call | solution.py:192
  179.4 16.2 %all_to_all.5 = bf16[4,256,384]{2,1,0:T(8,128)(2,1)S(1)} all-to-all(bf16[4,256,384]{2,1,0:T(8,128)(2,1)S(1)} %attend.1), channel_id=1, replica_groups=mesh['z'=8,'yl'=2,'x'=4,'yh'=2,'core'=2] {'yh','yl'}, dimensions={0} | all-to-all | bytes 1572864 | tf_op jit(solution)/shard_map/all_to_all | solution.py:241
  196.2 1.2 reshape.49
  (55 shorter events, 10.2 us)
Async XLA Ops:
  1.0 7.7 %collective-permute-start.3 = (bf16[96,1152]{1,0:T(8,128)(2,1)S(1)}, bf16[96,1152]{1,0:T(8,128)(2,1)S(1)}, u32[]{:S(2)}, u32[]{:S(2)}) collective-permute-start(bf16[96,1152]{1,0:T(8,128)(2,1)S(1)} %pad_maximum_fusion), channel_id=1, source_target_pairs={{0,0},{1,16},{4,4},{5,20},{8,8},{9,24},{12,12},{13,28},{16,1},{17,... | collective-permute-start | bytes 663560 | tf_op jit(solution)/shard_map/ppermute | solution.py:58
  6.4 61.7 %copy-start.6 = (f32[4,4,16,1536]{3,2,1,0:T(8,128)S(1)}, f32[4,4,16,1536]{3,2,1,0:T(8,128)}, u32[]{:S(2)}) copy-start(f32[4,4,16,1536]{3,2,1,0:T(8,128)} %param.6) | copy-start | bytes 4718596
  8.7 58.7 %collective-permute-start.10 = (bf16[96,1152]{1,0:T(8,128)(2,1)S(1)}, bf16[96,1152]{1,0:T(8,128)(2,1)S(1)}, u32[]{:S(2)}, u32[]{:S(2)}) collective-permute-start(bf16[96,1152]{1,0:T(8,128)(2,1)S(1)} %collective-permute-done.3), channel_id=1, source_target_pairs={{0,224},{1,225},{4,228},{5,229},{8,232},{9,233},{12,236},{13,237},... | collective-permute-start | bytes 663560 | tf_op jit(solution)/shard_map/ppermute | solution.py:40
  14.3 52.4 %collective-permute-start.9 = (bf16[96,1152]{1,0:T(8,128)(2,1)S(1)}, bf16[96,1152]{1,0:T(8,128)(2,1)S(1)}, u32[]{:S(2)}, u32[]{:S(2)}) collective-permute-start(bf16[96,1152]{1,0:T(8,128)(2,1)S(1)} %collective-permute-done.3), channel_id=1, source_target_pairs={{0,32},{1,33},{4,36},{5,37},{8,40},{9,41},{12,44},{13,45},{16,48},... | collective-permute-start | bytes 663560 | tf_op jit(solution)/shard_map/ppermute | solution.py:40
  14.3 51.7 %collective-permute-start.8 = (bf16[96,1152]{1,0:T(8,128)(2,1)S(1)}, bf16[96,1152]{1,0:T(8,128)(2,1)S(1)}, u32[]{:S(2)}, u32[]{:S(2)}) collective-permute-start(bf16[96,1152]{1,0:T(8,128)(2,1)S(1)} %collective-permute-done.3), channel_id=1, source_target_pairs={{0,192},{1,193},{4,196},{5,197},{8,200},{9,201},{12,204},{13,205},... | collective-permute-start | bytes 663560 | tf_op jit(solution)/shard_map/ppermute | solution.py:40
  16.2 49.1 %collective-permute-start.7 = (bf16[96,1152]{1,0:T(8,128)(2,1)S(1)}, bf16[96,1152]{1,0:T(8,128)(2,1)S(1)}, u32[]{:S(2)}, u32[]{:S(2)}) collective-permute-start(bf16[96,1152]{1,0:T(8,128)(2,1)S(1)} %collective-permute-done.3), channel_id=1, source_target_pairs={{0,64},{1,65},{4,68},{5,69},{8,72},{9,73},{12,76},{13,77},{16,80},... | collective-permute-start | bytes 663560 | tf_op jit(solution)/shard_map/ppermute | solution.py:40
  16.6 17.2 %collective-permute-start.4 = (bf16[96,1152]{1,0:T(8,128)(2,1)S(1)}, bf16[96,1152]{1,0:T(8,128)(2,1)S(1)}, u32[]{:S(2)}, u32[]{:S(2)}) collective-permute-start(bf16[96,1152]{1,0:T(8,128)(2,1)S(1)} %collective-permute-done.3), channel_id=1, source_target_pairs={{0,128},{1,129},{4,132},{5,133},{8,136},{9,137},{12,140},{13,141},... | collective-permute-start | bytes 663560 | tf_op jit(solution)/shard_map/ppermute | solution.py:40
  33.9 16.8 %collective-permute-start.5 = (bf16[96,1152]{1,0:T(8,128)(2,1)S(1)}, bf16[96,1152]{1,0:T(8,128)(2,1)S(1)}, u32[]{:S(2)}, u32[]{:S(2)}) collective-permute-start(bf16[96,1152]{1,0:T(8,128)(2,1)S(1)} %collective-permute-done.3), channel_id=1, source_target_pairs={{0,96},{1,97},{4,100},{5,101},{8,104},{9,105},{12,108},{13,109},{1... | collective-permute-start | bytes 663560 | tf_op jit(solution)/shard_map/ppermute | solution.py:40
  50.7 13.8 %collective-permute-start.6 = (bf16[96,1152]{1,0:T(8,128)(2,1)S(1)}, bf16[96,1152]{1,0:T(8,128)(2,1)S(1)}, u32[]{:S(2)}, u32[]{:S(2)}) collective-permute-start(bf16[96,1152]{1,0:T(8,128)(2,1)S(1)} %collective-permute-done.3), channel_id=1, source_target_pairs={{0,160},{1,161},{4,164},{5,165},{8,168},{9,169},{12,172},{13,173},... | collective-permute-start | bytes 663560 | tf_op jit(solution)/shard_map/ppermute | solution.py:40
  65.2 3.3 %copy-start.8 = (f32[1536]{0:T(1024)S(1)}, f32[1536]{0:T(1024)}, u32[]{:S(2)}) copy-start(f32[1536]{0:T(1024)} %param.9) | copy-start | bytes 18436
  65.2 3.3 %copy-start.7 = (f32[1536]{0:T(1024)S(1)}, f32[1536]{0:T(1024)}, u32[]{:S(2)}) copy-start(f32[1536]{0:T(1024)} %param.8) | copy-start | bytes 18436
  68.1 43.0 %copy-start.2 = (f32[128]{0:T(128)S(1)}, f32[128]{0:T(128)}, u32[]{:S(2)}) copy-start(f32[128]{0:T(128)} %param.10) | copy-start | bytes 1540
  68.1 43.0 %copy-start.3 = (f32[128]{0:T(128)S(1)}, f32[128]{0:T(128)}, u32[]{:S(2)}) copy-start(f32[128]{0:T(128)} %param.11) | copy-start | bytes 1540
  68.1 42.9 %collective-permute-start.11 = (bf16[8,96,1152]{2,1,0:T(8,128)(2,1)}, bf16[8,96,1152]{2,1,0:T(8,128)(2,1)}, u32[]{:S(2)}, u32[]{:S(2)}) collective-permute-start(bf16[8,96,1152]{2,1,0:T(8,128)(2,1)} %bitcast_dynamic-update-slice_fusion.refs_4_), channel_id=1, source_target_pairs={{0,1},{1,0},{4,5},{5,4},{8,9},{9,8},{12,13},{13,12},{16,17},{17,16... | collective-permute-start | bytes 5308424 | tf_op jit(solution)/shard_map/ppermute | solution.py:44
  69.0 25.1 %collective-permute-start.2 = (bf16[256,1536]{1,0:T(8,128)(2,1)S(1)}, bf16[256,1536]{1,0:T(8,128)(2,1)S(1)}, u32[]{:S(2)}, u32[]{:S(2)}) collective-permute-start(bf16[256,1536]{1,0:T(8,128)(2,1)S(1)} %fusion.3.refs_0_), channel_id=1, source_target_pairs={{0,2},{1,3},{4,6},{5,7},{8,10},{9,11},{12,14},{13,15},{16,18},{17,... | collective-permute-start | bytes 2359304 | tf_op jit(solution)/shard_map/ppermute | solution.py:40
  76.1 27.5 %collective-permute-start.1 = (bf16[256,1536]{1,0:T(8,128)(2,1)S(1)}, bf16[256,1536]{1,0:T(8,128)(2,1)S(1)}, u32[]{:S(2)}, u32[]{:S(2)}) collective-permute-start(bf16[256,1536]{1,0:T(8,128)(2,1)S(1)} %fusion.3.refs_0_), channel_id=1, source_target_pairs={{0,18},{1,19},{4,22},{5,23},{8,26},{9,27},{12,30},{13,31},{16,0},{... | collective-permute-start | bytes 2359304 | tf_op jit(solution)/shard_map/ppermute | solution.py:40
  76.1 34.9 %collective-permute-start = (bf16[256,1536]{1,0:T(8,128)(2,1)S(1)}, bf16[256,1536]{1,0:T(8,128)(2,1)S(1)}, u32[]{:S(2)}, u32[]{:S(2)}) collective-permute-start(bf16[256,1536]{1,0:T(8,128)(2,1)S(1)} %fusion.3.refs_0_), channel_id=1, source_target_pairs={{0,16},{1,17},{4,20},{5,21},{8,24},{9,25},{12,28},{13,29},{16,2},{... | collective-permute-start | bytes 2359304 | tf_op jit(solution)/shard_map/ppermute | solution.py:40
  94.1 16.9 %copy-start.9 = (bf16[256,1536]{1,0:T(8,128)(2,1)}, bf16[256,1536]{1,0:T(8,128)(2,1)S(1)}, u32[]{:S(2)}) copy-start(bf16[256,1536]{1,0:T(8,128)(2,1)S(1)} %collective-permute-done.2.refs_3_) | copy-start | bytes 2359300
  103.7 7.4 %copy-start.10 = (bf16[256,1536]{1,0:T(8,128)(2,1)}, bf16[256,1536]{1,0:T(8,128)(2,1)S(1)}, u32[]{:S(2)}) copy-start(bf16[256,1536]{1,0:T(8,128)(2,1)S(1)} %collective-permute-done.1.refs_2_) | copy-start | bytes 2359300
  119.6 0.9 copy-start.4
  120.4 21.4 %collective-permute-start.13 = (bf16[2,256,768]{2,1,0:T(8,128)(2,1)S(1)}, bf16[2,256,768]{2,1,0:T(8,128)(2,1)S(1)}, u32[]{:S(2)}, u32[]{:S(2)}) collective-permute-start(bf16[2,256,768]{2,1,0:T(8,128)(2,1)S(1)} %get-tuple-element.14), channel_id=1, source_target_pairs={{0,32},{1,33},{4,36},{5,37},{8,40},{9,41},{12,44},{13,45},{16,48},... | collective-permute-start | bytes 2359304 | tf_op jit(solution)/shard_map/ppermute | solution.py:40
  125.4 18.7 %collective-permute-start.14 = (bf16[2,256,768]{2,1,0:T(8,128)(2,1)S(1)}, bf16[2,256,768]{2,1,0:T(8,128)(2,1)S(1)}, u32[]{:S(2)}, u32[]{:S(2)}) collective-permute-start(bf16[2,256,768]{2,1,0:T(8,128)(2,1)S(1)} %get-tuple-element.15), channel_id=1, source_target_pairs={{0,224},{1,225},{4,228},{5,229},{8,232},{9,233},{12,236},{13,237},... | collective-permute-start | bytes 2359304 | tf_op jit(solution)/shard_map/ppermute | solution.py:40
  125.4 39.1 %collective-permute-start.12 = (bf16[2,2,256,768]{3,2,1,0:T(8,128)(2,1)}, bf16[2,2,256,768]{3,2,1,0:T(8,128)(2,1)}, u32[]{:S(2)}, u32[]{:S(2)}) collective-permute-start(bf16[2,2,256,768]{3,2,1,0:T(8,128)(2,1)} %get-tuple-element.13.own), channel_id=1, source_target_pairs={{0,1},{1,0},{4,5},{5,4},{8,9},{9,8},{12,13},{13,12},{16,17},{17,16... | collective-permute-start | bytes 4718600 | tf_op jit(solution)/shard_map/ppermute | solution.py:44
  126.1 24.1 %collective-permute-start.18 = (bf16[256,768]{1,0:T(8,128)(2,1)S(1)}, bf16[256,768]{1,0:T(8,128)(2,1)S(1)}, u32[]{:S(2)}, u32[]{:S(2)}) collective-permute-start(bf16[256,768]{1,0:T(8,128)(2,1)S(1)} %get-tuple-element.17), channel_id=1, source_target_pairs={{0,45},{1,36},{4,33},{5,40},{8,37},{9,44},{12,41},{13,32},{16,61},... | collective-permute-start | bytes 1179656 | tf_op jit(solution)/shard_map/ppermute | solution.py:48
  127.7 36.8 %collective-permute-start.17 = (bf16[2,256,768]{2,1,0:T(8,128)(2,1)S(1)}, bf16[2,256,768]{2,1,0:T(8,128)(2,1)}, u32[]{:S(2)}, u32[]{:S(2)}) collective-permute-start(bf16[2,256,768]{2,1,0:T(8,128)(2,1)S(1)} %get-tuple-element.16), channel_id=1, source_target_pairs={{0,13},{1,4},{4,1},{5,8},{8,5},{9,12},{12,9},{13,0},{16,29},{17,20... | collective-permute-start | bytes 2359304 | tf_op jit(solution)/shard_map/ppermute | solution.py:48
  141.8 22.6 %collective-permute-start.15 = (bf16[2,256,768]{2,1,0:T(8,128)(2,1)S(1)}, bf16[2,256,768]{2,1,0:T(8,128)(2,1)S(1)}, u32[]{:S(2)}, u32[]{:S(2)}) collective-permute-start(bf16[2,256,768]{2,1,0:T(8,128)(2,1)S(1)} %collective-permute-done.13.below), channel_id=1, source_target_pairs={{0,1},{1,0},{4,5},{5,4},{8,9},{9,8},{12,13},{13,12},{16,17},{17,16... | collective-permute-start | bytes 2359304 | tf_op jit(solution)/shard_map/ppermute | solution.py:44
  144.1 20.4 %collective-permute-start.16 = (bf16[2,256,768]{2,1,0:T(8,128)(2,1)S(1)}, bf16[2,256,768]{2,1,0:T(8,128)(2,1)}, u32[]{:S(2)}, u32[]{:S(2)}) collective-permute-start(bf16[2,256,768]{2,1,0:T(8,128)(2,1)S(1)} %collective-permute-done.14.above), channel_id=1, source_target_pairs={{0,1},{1,0},{4,5},{5,4},{8,9},{9,8},{12,13},{13,12},{16,17},{17,16... | collective-permute-start | bytes 2359304 | tf_op jit(solution)/shard_map/ppermute | solution.py:44
  150.3 0.8 copy-start
  151.0 13.4 %collective-permute-start.19 = (bf16[256,768]{1,0:T(8,128)(2,1)S(1)}, bf16[256,768]{1,0:T(8,128)(2,1)}, u32[]{:S(2)}, u32[]{:S(2)}) collective-permute-start(bf16[256,768]{1,0:T(8,128)(2,1)S(1)} %get-tuple-element.18), channel_id=1, source_target_pairs={{0,237},{1,228},{4,225},{5,232},{8,229},{9,236},{12,233},{13,224},... | collective-permute-start | bytes 1179656 | tf_op jit(solution)/shard_map/ppermute | solution.py:48
  164.5 1.0 copy-start.1
  165.5 1.1 copy-start.5

commit v2 on v1

v2 whole, which is shorter than its diff:
```python
import math

import jax
import jax.numpy as jnp
import numpy as np
from jax import lax
from jax.experimental import pallas as pl
from jax.experimental.pallas import tpu as pltpu
from jax.sharding import Mesh, PartitionSpec as P

AXES = ("z", "yl", "x", "yh", "core")
SIZES = (8, 2, 4, 2, 2)
TOKENS = 256
D = 1536
HD = 128
GROUP_HEADS = 3
GROUP = GROUP_HEADS * HD
ROWS = 96
EPSILON = 1e-06
SCORE_SCALE = HD ** (-0.5) * math.log2(math.e)
F32 = jnp.float32
BF16 = jnp.bfloat16


def linear(z, y, x, core):
    return (((z % 8 * 2 + y % 2) * 4 + x % 4) * 2 + y % 4 // 2) * 2 + core


def pairs(move):
    return [
        (linear(z, y, x, core), linear(*move(z, y, x, core)))
        for z in range(8)
        for y in range(4)
        for x in range(4)
        for core in range(2)
    ]


def shift(array, dz=0, dy=0):
    return lax.ppermute(array, AXES, pairs(lambda z, y, x, core: (z + dz, y + dy, x, core)))


def swap_cores(array):
    return lax.ppermute(array, AXES, pairs(lambda z, y, x, core: (z, y, x, 1 - core)))


def outward(array, dz=0):
    return lax.ppermute(
        array, AXES, pairs(lambda z, y, x, core: (z + dz, y, x + (1 if core else -1), 1 - core))
    )


def ring_step(array):
    return lax.ppermute(
        array, AXES, pairs(lambda z, y, x, core: (z + (-1 if core else 1), y, x, core))
    )


def swap_rows(array):
    return lax.ppermute(
        array, AXES, pairs(lambda z, y, x, core: (z, y // 2 * 2 + 1 - y % 2, x, core))
    )


def after(array, *others):
    return lax.optimization_barrier((array,) + others)[0]


def layer_norm(activations, adaptive_shift, adaptive_scale):
    centre = jnp.mean(activations, axis=1, keepdims=True)
    shifted = activations - centre
    spread = jnp.mean(shifted * shifted, axis=1, keepdims=True)
    scaled = shifted * lax.rsqrt(spread + EPSILON) * (1.0 + adaptive_scale) + adaptive_shift
    return scaled.astype(BF16)


STEPS = (0, 1, -1, 2)
HALF = TOKENS // 2
VMEM = pl.BlockSpec(memory_space=pltpu.VMEM)
SMEM = pl.BlockSpec(memory_space=pltpu.SMEM)
PARAMS = pltpu.CompilerParams(vmem_limit_bytes=60 * 1024 * 1024)
WIDE = pltpu.CompilerParams(vmem_limit_bytes=16 * 1024 * 1024)


def weight_copies(weights, pieces, sems, z, yl, core):
    sign = 2 * core - 1
    offsets = [0] + [sign * r for r in range(1, 5)] + [-sign * r for r in range(1, 4)]
    copies = []
    for index, (piece, offset) in enumerate(zip(pieces, offsets, strict=True)):
        start = lax.rem(z + offset + 8, 8) * (2 * ROWS)
        for half, lo in ((0, yl), (1, 1 - yl)):
            where = pl.ds(pl.multiple_of(start + lo * ROWS, 32), ROWS)
            copies.append(
                pltpu.make_async_copy(
                    piece.at[pl.ds(half * ROWS, ROWS)], weights.at[where], sems.at[2 * index + half]
                )
            )
    return copies


def head_norm(block, gain):
    mean_square = jnp.mean(block * block, axis=1, keepdims=True)
    return (block * lax.rsqrt(mean_square + EPSILON) * gain[...]).astype(BF16)


def sources(y, core):
    found = []
    for step in STEPS:
        source = lax.rem(y - step + 4, 4)
        found.append((lax.rem(source, 2), jnp.where(source // 2 == core, 0, 1)))
    return found


def token_copies(rows, tokens, slots, sems):
    copies = [pltpu.make_async_copy(tokens[n], rows.at[slots[n]], sems.at[n]) for n in range(3)]
    for half in range(2):
        where = rows.at[slots[3], pl.ds(half * HALF, HALF)]
        copies.append(pltpu.make_async_copy(tokens[3 + half], where, sems.at[3 + half]))
    return copies


def project_kernel(place, *refs):
    tokens, pieces = refs[:5], refs[5:13]
    query_gain, key_gain, q_out, own, edge = refs[13:18]
    alone = refs[18:22]
    weights, rows, sems, token_sems = refs[22:]
    y, core = place[0], place[1]
    slots = [role * 2 + yl for yl, role in sources(y, core)]
    copies = weight_copies(weights, pieces, sems, place[2], lax.rem(y, 2), core)
    copies += token_copies(rows, tokens, slots, token_sems)
    for copy in copies:
        copy.start()
    for copy in copies:
        copy.wait()
    for slot in range(4):
        role, yl = slot // 2, slot % 2
        projected = jnp.dot(rows[slot], weights[...], preferred_element_type=F32)
        for head in range(GROUP_HEADS):
            ks = slice(head * 2 * HD, head * 2 * HD + HD)
            vs = slice(head * 2 * HD + HD, (head + 1) * 2 * HD)
            span = slice(head * HD, (head + 1) * HD)
            part = lambda kind: projected[:, kind * GROUP + head * HD : kind * GROUP + (head + 1) * HD]
            k = head_norm(part(0), key_gain)
            v = part(1).astype(BF16)
            for out in [own.at[role, yl], alone[slot]] + ([edge.at[yl]] if role == 0 else []):
                out[:, ks] = k
                out[:, vs] = v
            q_out[slot, :, span] = head_norm(part(2), query_gain)


ANY = pl.BlockSpec(memory_space=pl.ANY)
LIGHT = pl.CostEstimate(flops=10_000_000, bytes_accessed=100_000, transcendentals=0)


def project(place, tokens, pieces, query_gain, key_gain):
    kv = lambda *lead: jax.ShapeDtypeStruct(lead + (TOKENS, 2 * GROUP), BF16)
    return pl.pallas_call(
        project_kernel,
        name="project",
        out_shape=(jax.ShapeDtypeStruct((4, TOKENS, GROUP), BF16), kv(2, 2), kv(2)) + (kv(),) * 4,
        in_specs=[SMEM] + [ANY] * 13 + [VMEM] * 2,
        out_specs=[VMEM] * 7,
        scratch_shapes=[
            pltpu.VMEM((D, 3 * GROUP), BF16),
            pltpu.VMEM((4, TOKENS, D), BF16),
            pltpu.SemaphoreType.DMA((16,)),
            pltpu.SemaphoreType.DMA((5,)),
        ],
        compiler_params=PARAMS,
        cost_estimate=LIGHT,
    )(place, *tokens, *pieces, query_gain.reshape(1, HD), key_gain.reshape(1, HD))


def fold(scores):
    return jnp.maximum(scores[:, :HD], scores[:, HD:])


def attend_tiles(query, groups, peak, total):
    ones = jnp.ones((TOKENS, HD), BF16)
    scored = []
    best = peak
    for cost, tiles in groups:
        top = None
        for tile in tiles:
            scores = lax.dot_general(
                query, tile[:, :HD], (((1,), (1,)), ((), ())), preferred_element_type=F32
            )
            scored.append((cost, scores))
            folded = fold(scores)
            top = folded if top is None else jnp.maximum(top, folded)
        top = top * SCORE_SCALE
        if cost is not None:
            top = top - cost
        best = top if best is None else jnp.maximum(best, top)
    high = jnp.max(best, axis=1, keepdims=True)
    weights = []
    for cost, scores in scored:
        base = high if cost is None else high + cost
        weights.append(jnp.exp2(scores * SCORE_SCALE - base).astype(BF16))
    wide = [jnp.concatenate([tile[:, HD:], ones], axis=1) for _, tiles in groups for tile in tiles]
    mixed = jnp.dot(
        jnp.concatenate(weights, axis=1), jnp.concatenate(wide, axis=0), preferred_element_type=F32
    )
    if total is not None:
        scale = jnp.exp2(peak - high)
        mixed = mixed + total * jnp.concatenate([scale, scale], axis=1)
    return high, mixed


def penalty(flag):
    return jnp.where(flag > 0, 0.0, 1e30).astype(F32)


def near_kernel(valid, q, own, mate, edge, below, above, peaks, totals):
    no_edge = penalty(valid[2])
    for yl in range(2):
        no_row, row = (penalty(valid[1]), above) if yl else (penalty(valid[0]), below)
        for role in range(2):
            slot = role * 2 + yl
            if role == 0:
                groups = [
                    (None, [own[0, 0], own[0, 1], mate[1, 0], mate[1, 1]]),
                    (no_edge, [edge[0], edge[1]]),
                    (no_row, [row[...]]),
                ]
            else:
                groups = [
                    (None, [own[1, 0], own[1, 1], mate[1, 0], mate[1, 1], mate[0, 0], mate[0, 1]])
                ]
            peak, total = attend_tiles(q[slot], groups, None, None)
            peaks[0, slot] = jnp.broadcast_to(peak, (TOKENS, HD))
            totals[0, slot] = total


def far_kernel(valid, q, peaks, totals, *refs):
    inner_rows, mate_outer_rows, mate_inner_rows, corners = refs[0:2], refs[2:4], refs[4:6], refs[6:8]
    outs, done = refs[8:12], refs[12]
    core = valid[3]
    for yl in range(2):
        no_row = penalty(valid[yl])
        for role in range(2):
            slot = role * 2 + yl
            if role == 0:
                groups = [
                    (no_row, [mate_inner_rows[yl][...]]),
                    (jnp.maximum(no_row, penalty(valid[2])), [corners[yl][...]]),
                ]
            else:
                groups = [(no_row, [rows[yl][...] for rows in (inner_rows, mate_inner_rows, mate_outer_rows)])]
            _, total = attend_tiles(q[slot], groups, peaks[0, slot], totals[0, slot])
            yh = 1 - core if role else core
            done[yh * 2 + yl] = (total[:, :HD] / total[:, HD:]).astype(BF16)
    for out, step in zip(outs, STEPS, strict=True):
        out[...] = done[lax.rem(valid[4] - step + 4, 4)]


def head_spec(array, width):
    lead = array.ndim - 1
    return pl.BlockSpec(array.shape[:-1] + (width,), lambda h: (0,) * lead + (h,))


STATE = lambda width: pl.BlockSpec((1, 4, TOKENS, width), lambda h: (h, 0, 0, 0))


def attend_near(valid, q, *kv):
    return pl.pallas_call(
        near_kernel,
        name="attend_near",
        grid=(GROUP_HEADS,),
        out_shape=(
            jax.ShapeDtypeStruct((GROUP_HEADS, 4, TOKENS, HD), F32),
            jax.ShapeDtypeStruct((GROUP_HEADS, 4, TOKENS, 2 * HD), F32),
        ),
        in_specs=[SMEM, head_spec(q, HD)] + [head_spec(a, 2 * HD) for a in kv],
        out_specs=[STATE(HD), STATE(2 * HD)],
        compiler_params=WIDE,
        cost_estimate=LIGHT,
    )(valid, q, *kv)


def attend_far(valid, q, peaks, totals, *kv):
    return pl.pallas_call(
        far_kernel,
        name="attend_far",
        grid=(GROUP_HEADS,),
        out_shape=(jax.ShapeDtypeStruct((TOKENS, GROUP), BF16),) * 4,
        in_specs=[SMEM, head_spec(q, HD), STATE(HD), STATE(2 * HD)] + [head_spec(a, 2 * HD) for a in kv],
        out_specs=[pl.BlockSpec((TOKENS, HD), lambda h: (0, h))] * 4,
        scratch_shapes=[pltpu.VMEM((4, TOKENS, HD), BF16)],
        compiler_params=WIDE,
        cost_estimate=LIGHT,
    )(valid, q, peaks, totals, *kv)


def side_kernel(place, *refs):
    for part, step in zip(refs[:4], STEPS, strict=True):
        start = lax.rem(place[0] + step + 4, 4) * GROUP
        refs[4][:, pl.ds(pl.multiple_of(start, HD), GROUP)] = part[...]


def side_by_side(place, parts, shape):
    return pl.pallas_call(
        side_kernel,
        name="side_by_side",
        out_shape=jax.ShapeDtypeStruct((TOKENS, D), BF16),
        in_specs=[SMEM] + [VMEM] * 4,
        out_specs=VMEM,
        compiler_params=WIDE,
    )(place, *parts).reshape(shape)


def per_device(hidden, projection, adaptive_shift, adaptive_scale, query_gain, key_gain):
    z, yl, x, yh, core = (lax.axis_index(a) for a in AXES)
    y = yh * 2 + yl
    inner = projection.shape[1] // 3

    def columns(chip, *kinds):
        parts = [lax.dynamic_slice_in_dim(projection, k * inner + chip * GROUP, GROUP, 1) for k in kinds]
        return parts[0] if len(parts) == 1 else jnp.concatenate(parts, axis=1)

    normed = layer_norm(hidden.reshape(TOKENS, D), adaptive_shift, adaptive_scale)
    theirs = swap_rows(columns(yh * 2 + 1 - yl, 1, 2, 0))
    normed = after(normed, theirs)
    behind, ahead = shift(normed, dy=1), shift(normed, dy=-1)
    base = jnp.concatenate([columns(y, 1, 2, 0), theirs], axis=0)
    base = after(base, normed)
    ring = [base, ring_step(base)]
    ring.append(ring_step(ring[1]))
    ring.append(ring_step(after(ring[2], behind, ahead)))
    ring.append(ring_step(ring[3]))
    pieces = ring + [swap_cores(piece) for piece in ring[1:4]]
    tokens = [normed, behind, ahead, shift(behind[:HALF], dy=1), shift(ahead[HALF:], dy=-1)]

    place = jnp.stack([y, core, z]).astype(jnp.int32)
    q, own, edge_out, outer_low, outer_high, inner_low, inner_high = project(
        place, tokens, pieces, query_gain, key_gain
    )
    outer_below = shift(outer_high, dz=1)
    outer_above = shift(outer_low, dz=-1)
    edge = outward(edge_out)
    mate = swap_cores(own)
    inner_below = shift(after(inner_high, mate), dz=1)
    inner_above = shift(after(inner_low, mate), dz=-1)
    corner_below = outward(outer_below)
    corner_above = outward(outer_above)
    last_x = jnp.where(core == 0, 0, 3)
    valid = jnp.stack([z > 0, z < 7, x != last_x, core, y]).astype(jnp.int32)
    peaks, totals = attend_near(valid, q, own, mate, edge, outer_below, outer_above)
    mate_outer_rows = [swap_cores(after(row, peaks)) for row in (outer_below, outer_above)]
    inner_rows = [inner_below, inner_above]
    mate_inner_rows = [swap_cores(after(row, peaks)) for row in inner_rows]
    attended = attend_far(
        valid, q, peaks, totals, *inner_rows, *mate_outer_rows, *mate_inner_rows, corner_below, corner_above
    )
    back = [attended[0]] + [shift(tile, dy=-step) for step, tile in zip(STEPS[1:], attended[1:], strict=True)]
    return side_by_side(place, back, hidden.shape)


def solution(mesh):
    split = Mesh(np.asarray(mesh.devices).reshape(SIZES), AXES)
    tm, height = ("z", "yl"), ("x", "yh", "core")
    return jax.shard_map(
        per_device,
        mesh=split,
        in_specs=(P(tm, height, None, None), P(tm, None), P(), P(), P(), P()),
        out_specs=P(tm, height, None, None),
        check_vma=False,
    )
```

time: 199 us -> 123 us (0.62)
  the two profiles are of different devices: /device:TPU:7 before, /device:TPU:1 now
where the time goes in v2:
time: 123 us
  waiting for transfers between devices  46.5 us (38%)
  starting transfers between devices  41.9 us (34%)
  Pallas kernels  25.2 us (20%)
  local copies, waits for them, and re-layouts  6.53 us (5%)
  other arithmetic  2.9 us (2%)
    ppermute x11, waiting for transfers between devices, shift(): lax.ppermute(array, AXES, pairs(lambda z, y, x, core: (z + dz, y + dy, x,...  34.2 us
    ppermute x11, starting transfers between devices, shift(): lax.ppermute(array, AXES, pairs(lambda z, y, x, core: (z + dz, y + dy, x,...  15.1 us
    ppermute x4, starting transfers between devices, ring_step(): lax.ppermute(array, AXES, pairs(lambda z, y, x, core: (z + (-1 if core el...  13.3 us
    pallas_call x1, Pallas kernels, project(): pl.pallas_call(project_kernel, name='project', out_shape=(jax.ShapeDtypeS...  9.89 us
    ppermute x4, waiting for transfers between devices, ring_step(): lax.ppermute(array, AXES, pairs(lambda z, y, x, core: (z + (-1 if core el...  8.66 us
    pallas_call x1, Pallas kernels, attend_near(): pl.pallas_call(near_kernel, name='attend_near', grid=(GROUP_HEADS,), out_...  8.13 us
    ppermute x8, starting transfers between devices, swap_cores(): lax.ppermute(array, AXES, pairs(lambda z, y, x, core: (z, y, x, 1 - core)))  7.26 us
    pallas_call x1, Pallas kernels, attend_far(): pl.pallas_call(far_kernel, name='attend_far', grid=(GROUP_HEADS,), out_sh...  5.69 us
  transfers between devices with their start and end apart: 27, of which 13 were waited for; matrix products, arithmetic and copies ran while one was open for 4% of the time, Pallas kernels for 7%

profile of v2, /device:TPU:1, one launch (start us, length us, event | category | flops | bytes accessed | tf_op | source)
XLA Modules:
  0.0 123.3 jit_solution(446861432246231813)
XLA Ops:
  0.0 1.2 constant_dynamic-slice_fusion.2
  1.3 2.2 %collective-permute-start = (bf16[96,1152]{1,0:T(8,128)(2,1)S(1)}, bf16[96,1152]{1,0:T(8,128)(2,1)S(1)}, u32[]{:S(2)}, u32[]{:S(2)}) collective-permute-start(bf16[96,1152]{1,0:T(8,128)(2,1)S(1)} %pad_maximum_fusion.1), channel_id=1, source_target_pairs={{0,16},{1,17},{4,20},{5,21},{8,24},{9,25},{12,28},{13,29},{16,0},{... | collective-permute-start | bytes 663560 | tf_op jit(solution)/shard_map/ppermute | solution.py:60
  3.5 1.6 %reduce_sum.18 = f32[4,4,16]{2,1,0:T(4,128)S(1)} reduce(f32[4,4,16,1536]{3,2,1,0:T(8,128)} %param.6, f32[]{:T(128)} %constant.44.clone.1), dimensions={3}, to_apply=%region_0.0 | reduce | flops 392960 | bytes 1573892 | tf_op jit(solution)/shard_map/reduce_sum | solution.py:70
  6.0 1.5 %collective-permute-done = bf16[96,1152]{1,0:T(8,128)(2,1)S(1)} collective-permute-done((bf16[96,1152]{1,0:T(8,128)(2,1)S(1)}, bf16[96,1152]{1,0:T(8,128)(2,1)S(1)}, u32[]{:S(2)}, u32[]{:S(2)}) %collective-permute-start) | collective-permute-done | bytes 221216 | tf_op jit(solution)/shard_map/ppermute | solution.py:60
  7.5 6.7 %collective-permute-start.5 = (bf16[192,1152]{1,0:T(8,128)(2,1)S(1)}, bf16[192,1152]{1,0:T(8,128)(2,1)S(1)}, u32[]{:S(2)}, u32[]{:S(2)}) collective-permute-start(bf16[192,1152]{1,0:T(8,128)(2,1)S(1)} %pad_maximum_fusion.refs_5_), channel_id=1, source_target_pairs={{0,32},{1,225},{4,36},{5,229},{8,40},{9,233},{12,44},{13,237},{16,... | collective-permute-start | bytes 1327112 | tf_op jit(solution)/shard_map/ppermute | solution.py:54
  14.2 1.3 %collective-permute-start.1 = (bf16[256,1536]{1,0:T(8,128)(2,1)S(1)}, bf16[256,1536]{1,0:T(8,128)(2,1)S(1)}, u32[]{:S(2)}, u32[]{:S(2)}) collective-permute-start(bf16[256,1536]{1,0:T(8,128)(2,1)S(1)} %fusion.3.refs_0_), channel_id=1, source_target_pairs={{0,16},{1,17},{4,20},{5,21},{8,24},{9,25},{12,28},{13,29},{16,2},{... | collective-permute-start | bytes 2359304 | tf_op jit(solution)/shard_map/ppermute | solution.py:40
  15.5 1.4 %collective-permute-start.2 = (bf16[256,1536]{1,0:T(8,128)(2,1)S(1)}, bf16[256,1536]{1,0:T(8,128)(2,1)S(1)}, u32[]{:S(2)}, u32[]{:S(2)}) collective-permute-start(bf16[256,1536]{1,0:T(8,128)(2,1)S(1)} %fusion.3.refs_0_), channel_id=1, source_target_pairs={{0,18},{1,19},{4,22},{5,23},{8,26},{9,27},{12,30},{13,31},{16,0},{... | collective-permute-start | bytes 2359304 | tf_op jit(solution)/shard_map/ppermute | solution.py:40
  16.9 2.5 %collective-permute-done.5.refs_6_ = bf16[192,1152]{1,0:T(8,128)(2,1)S(1)} collective-permute-done((bf16[192,1152]{1,0:T(8,128)(2,1)S(1)}, bf16[192,1152]{1,0:T(8,128)(2,1)S(1)}, u32[]{:S(2)}, u32[]{:S(2)}) %collective-permute-start.5) | collective-permute-done | bytes 442400 | tf_op jit(solution)/shard_map/ppermute | solution.py:54
  19.5 3.4 %collective-permute-start.6 = (bf16[192,1152]{1,0:T(8,128)(2,1)S(1)}, bf16[192,1152]{1,0:T(8,128)(2,1)}, u32[]{:S(2)}, u32[]{:S(2)}) collective-permute-start(bf16[192,1152]{1,0:T(8,128)(2,1)S(1)} %collective-permute-done.5.refs_6_), channel_id=1, source_target_pairs={{0,32},{1,225},{4,36},{5,229},{8,40},{9,233},{12,44},{13,237},{16,... | collective-permute-start | bytes 1327112 | tf_op jit(solution)/shard_map/ppermute | solution.py:54
  22.9 10.2 %collective-permute-done.1.refs_1_ = bf16[256,1536]{1,0:T(8,128)(2,1)S(1)} collective-permute-done((bf16[256,1536]{1,0:T(8,128)(2,1)S(1)}, bf16[256,1536]{1,0:T(8,128)(2,1)S(1)}, u32[]{:S(2)}, u32[]{:S(2)}) %collective-permute-start.1) | collective-permute-done | bytes 786464 | tf_op jit(solution)/shard_map/ppermute | solution.py:40
  35.0 6.1 %collective-permute-done.7.refs_8_ = bf16[192,1152]{1,0:T(8,128)(2,1)} collective-permute-done((bf16[192,1152]{1,0:T(8,128)(2,1)}, bf16[192,1152]{1,0:T(8,128)(2,1)}, u32[]{:S(2)}, u32[]{:S(2)}) %collective-permute-start.7) | collective-permute-done | bytes 442400 | tf_op jit(solution)/shard_map/ppermute | solution.py:54
  41.2 2.0 %collective-permute-start.8 = (bf16[192,1152]{1,0:T(8,128)(2,1)}, bf16[192,1152]{1,0:T(8,128)(2,1)}, u32[]{:S(2)}, u32[]{:S(2)}) collective-permute-start(bf16[192,1152]{1,0:T(8,128)(2,1)} %collective-permute-done.7.refs_8_), channel_id=1, source_target_pairs={{0,32},{1,225},{4,36},{5,229},{8,40},{9,233},{12,44},{13,237},{16,... | collective-permute-start | bytes 1327112 | tf_op jit(solution)/shard_map/ppermute | solution.py:54
  44.0 1.2 collective-permute-start.3
  46.8 1.5 %collective-permute-start.4 = (bf16[128,1536]{1,0:T(8,128)(2,1)}, bf16[128,1536]{1,0:T(8,128)(2,1)}, u32[]{:S(2)}, u32[]{:S(2)}) collective-permute-start(bf16[128,1536]{1,0:T(8,128)(2,1)} %slice.9), channel_id=1, source_target_pairs={{0,18},{1,19},{4,22},{5,23},{8,26},{9,27},{12,30},{13,31},{16,0},{... | collective-permute-start | bytes 1179656 | tf_op jit(solution)/shard_map/ppermute | solution.py:40
  49.0 6.7 %collective-permute-done.3.refs_3_ = bf16[128,1536]{1,0:T(8,128)(2,1)S(1)} collective-permute-done((bf16[128,1536]{1,0:T(8,128)(2,1)}, bf16[128,1536]{1,0:T(8,128)(2,1)S(1)}, u32[]{:S(2)}, u32[]{:S(2)}) %collective-permute-start.3) | collective-permute-done | bytes 393248 | tf_op jit(solution)/shard_map/ppermute | solution.py:40
  55.6 1.7 %collective-permute-done.4.refs_4_ = bf16[128,1536]{1,0:T(8,128)(2,1)} collective-permute-done((bf16[128,1536]{1,0:T(8,128)(2,1)}, bf16[128,1536]{1,0:T(8,128)(2,1)}, u32[]{:S(2)}, u32[]{:S(2)}) %collective-permute-start.4) | collective-permute-done | bytes 393248 | tf_op jit(solution)/shard_map/ppermute | solution.py:40
  57.4 9.9 %project.1 = (bf16[4,256,384]{2,1,0:T(8,128)(2,1)}, bf16[2,2,256,768]{3,2,1,0:T(8,128)(2,1)}, bf16[2,256,768]{2,1,0:T(8,128)(2,1)}, bf16[256,768]{1,0:T(8,128)(2...) custom-call(s32[3]{0:T(128)} %pad_add_fusion.place, ...), custom_call_target="tpu_custom_call" | custom-call | flops 10000000 | bytes 100000 | tf_op jit(solution)/shard_map/project/pallas_call | solution.py:157
  67.3 1.4 %collective-permute-start.12 = (bf16[2,2,256,768]{3,2,1,0:T(8,128)(2,1)}, bf16[2,2,256,768]{3,2,1,0:T(8,128)(2,1)S(1)}, u32[]{:S(2)}, u32[]{:S(2)}) collective-permute-start(bf16[2,2,256,768]{3,2,1,0:T(8,128)(2,1)} %get-tuple-element.31.own), channel_id=1, source_target_pairs={{0,1},{1,0},{4,5},{5,4},{8,9},{9,8},{12,13},{13,12},{16,17},{17,16... | collective-permute-start | bytes 4718600 | tf_op jit(solution)/shard_map/ppermute | solution.py:44
  68.7 1.2 collective-permute-start.13
  69.9 3.0 %collective-permute-start.15 = (bf16[256,768]{1,0:T(8,128)(2,1)}, bf16[256,768]{1,0:T(8,128)(2,1)}, u32[]{:S(2)}, u32[]{:S(2)}) collective-permute-start(bf16[256,768]{1,0:T(8,128)(2,1)} %get-tuple-element.34), channel_id=1, source_target_pairs={{0,224},{1,225},{4,228},{5,229},{8,232},{9,233},{12,236},{13,237},... | collective-permute-start | bytes 1179656 | tf_op jit(solution)/shard_map/ppermute | solution.py:40
  72.9 2.7 %collective-permute-start.17 = (bf16[256,768]{1,0:T(8,128)(2,1)}, bf16[256,768]{1,0:T(8,128)(2,1)S(1)}, u32[]{:S(2)}, u32[]{:S(2)}) collective-permute-start(bf16[256,768]{1,0:T(8,128)(2,1)} %get-tuple-element.40), channel_id=1, source_target_pairs={{0,224},{1,225},{4,228},{5,229},{8,232},{9,233},{12,236},{13,237},... | collective-permute-start | bytes 1179656 | tf_op jit(solution)/shard_map/ppermute | solution.py:40
  75.6 5.4 %collective-permute-done.14.below = bf16[256,768]{1,0:T(8,128)(2,1)} collective-permute-done((bf16[256,768]{1,0:T(8,128)(2,1)}, bf16[256,768]{1,0:T(8,128)(2,1)}, u32[]{:S(2)}, u32[]{:S(2)}) %collective-permute-start.14) | collective-permute-done | bytes 393248 | tf_op jit(solution)/shard_map/ppermute | solution.py:40
  81.0 2.8 %collective-permute-start.22 = (bf16[256,768]{1,0:T(8,128)(2,1)}, bf16[256,768]{1,0:T(8,128)(2,1)S(1)}, u32[]{:S(2)}, u32[]{:S(2)}) collective-permute-start(bf16[256,768]{1,0:T(8,128)(2,1)} %collective-permute-done.14.below), channel_id=1, source_target_pairs={{0,13},{1,4},{4,1},{5,8},{8,5},{9,12},{12,9},{13,0},{16,29},{17,20... | collective-permute-start | bytes 1179656 | tf_op jit(solution)/shard_map/ppermute | solution.py:48
  85.0 1.4 %copy-done.1 = bf16[2,2,256,768]{3,2,1,0:T(8,128)(2,1)S(1)} copy-done((bf16[2,2,256,768]{3,2,1,0:T(8,128)(2,1)S(1)}, bf16[2,2,256,768]{3,2,1,0:T(8,128)(2,1)}, u32[]{:S(2)}) %copy-start.1) | copy-done | bytes 1572888
  86.4 8.1 %attend_near.1 = (f32[3,4,256,128]{3,2,1,0:T(8,128)S(1)}, f32[3,4,256,256]{3,2,1,0:T(8,128)S(1)}) custom-call(s32[5]{0:T(128)S(1)} %stack.45.valid, bf16[4,256,384]{2,1,0:T(8,128)(2,1)S(1)} %copy-done, bf16[2,2,256,768]{3,2,1,0:T(8,128)(2,1)S(1)} %copy-done.1, bf16[2,2,256,768]{3,2,1,0:T(8,128)(2,1)S(1)} %collective-permute-done.12.mate, ...), custom_call_target="tpu_custom_call" | custom-call | flops 10000000 | bytes 100000 | tf_op jit(solution)/shard_map/attend_near/pallas_call | solution.py:266
  94.5 4.5 %collective-permute-start.18 = (bf16[256,768]{1,0:T(8,128)(2,1)}, bf16[256,768]{1,0:T(8,128)(2,1)S(1)}, u32[]{:S(2)}, u32[]{:S(2)}) collective-permute-start(bf16[256,768]{1,0:T(8,128)(2,1)} %collective-permute-done.14.below), channel_id=1, source_target_pairs={{0,1},{1,0},{4,5},{5,4},{8,9},{9,8},{12,13},{13,12},{16,17},{17,16... | collective-permute-start | bytes 1179656 | tf_op jit(solution)/shard_map/ppermute | solution.py:44
  102.1 5.7 %attend_far.1 = (bf16[256,384]{1,0:T(8,128)(2,1)S(1)}, bf16[256,384]{1,0:T(8,128)(2,1)S(1)}, bf16[256,384]{1,0:T(8,128)(2,1)S(1)}, bf16[256,384]{1,0:T(8,128)(2,1)S(1)}) custom-call(s32[5]{0:T(128)S(1)} %stack.45.valid, bf16[4,256,384]{2,1,0:T(8,128)(2,1)S(1)} %copy-done, f32[3,4,256,128]{3,2,1,0:T(8,128)S(1)} %get-tuple-element.35.peaks, ...), custom_call_target="tpu_custom_call" | custom-call | flops 10000000 | bytes 100000 | tf_op jit(solution)/shard_map/attend_far/pallas_call | solution.py:282
  107.8 2.8 %collective-permute-start.24 = (bf16[256,384]{1,0:T(8,128)(2,1)S(1)}, bf16[256,384]{1,0:T(8,128)(2,1)S(1)}, u32[]{:S(2)}, u32[]{:S(2)}) collective-permute-start(bf16[256,384]{1,0:T(8,128)(2,1)S(1)} %get-tuple-element.46), channel_id=1, source_target_pairs={{0,18},{1,19},{4,22},{5,23},{8,26},{9,27},{12,30},{13,31},{16,0},{... | collective-permute-start | bytes 589832 | tf_op jit(solution)/shard_map/ppermute | solution.py:40
  110.6 1.3 %collective-permute-start.26 = (bf16[256,384]{1,0:T(8,128)(2,1)S(1)}, bf16[256,384]{1,0:T(8,128)(2,1)S(1)}, u32[]{:S(2)}, u32[]{:S(2)}) collective-permute-start(bf16[256,384]{1,0:T(8,128)(2,1)S(1)} %get-tuple-element.48), channel_id=1, source_target_pairs={{0,2},{1,3},{4,6},{5,7},{8,10},{9,11},{12,14},{13,15},{16,18},{17,... | collective-permute-start | bytes 589832 | tf_op jit(solution)/shard_map/ppermute | solution.py:40
  111.9 2.5 %collective-permute-done.24.refs_1_ = bf16[256,384]{1,0:T(8,128)(2,1)S(1)} collective-permute-done((bf16[256,384]{1,0:T(8,128)(2,1)S(1)}, bf16[256,384]{1,0:T(8,128)(2,1)S(1)}, u32[]{:S(2)}, u32[]{:S(2)}) %collective-permute-start.24) | collective-permute-done | bytes 196640 | tf_op jit(solution)/shard_map/ppermute | solution.py:40
  114.3 7.4 %collective-permute-done.25.refs_2_ = bf16[256,384]{1,0:T(8,128)(2,1)S(1)} collective-permute-done((bf16[256,384]{1,0:T(8,128)(2,1)S(1)}, bf16[256,384]{1,0:T(8,128)(2,1)S(1)}, u32[]{:S(2)}, u32[]{:S(2)}) %collective-permute-start.25) | collective-permute-done | bytes 196640 | tf_op jit(solution)/shard_map/ppermute | solution.py:40
  121.8 1.5 %side_by_side.1 = bf16[256,1536]{1,0:T(8,128)(2,1)} custom-call(s32[3]{0:T(128)S(1)} %copy-done.2, bf16[256,384]{1,0:T(8,128)(2,1)S(1)} %get-tuple-element.45.refs_0_, bf16[256,384]{1,0:T(8,128)(2,1)S(1)} %collective-permute-done.24.refs_1_, bf16[256,384]{1,0:T(8,128)(2,1)S(1)} %collective-permute-done.25.refs_2_, ...), custom_call_target="tpu_custom_call" | custom-call | tf_op jit(solution)/shard_map/side_by_side/pallas_call | solution.py:302
  (67 shorter events, 10.3 us)
Async XLA Ops:
  1.3 6.1 %collective-permute-start = (bf16[96,1152]{1,0:T(8,128)(2,1)S(1)}, bf16[96,1152]{1,0:T(8,128)(2,1)S(1)}, u32[]{:S(2)}, u32[]{:S(2)}) collective-permute-start(bf16[96,1152]{1,0:T(8,128)(2,1)S(1)} %pad_maximum_fusion.1), channel_id=1, source_target_pairs={{0,16},{1,17},{4,20},{5,21},{8,24},{9,25},{12,28},{13,29},{16,0},{... | collective-permute-start | bytes 663560 | tf_op jit(solution)/shard_map/ppermute | solution.py:60
  5.9 51.4 %copy-start.4 = (bf16[256,1536]{1,0:T(8,128)(2,1)}, bf16[256,1536]{1,0:T(8,128)(2,1)S(1)}, u32[]{:S(2)}) copy-start(bf16[256,1536]{1,0:T(8,128)(2,1)S(1)} %fusion.3.refs_0_) | copy-start | bytes 2359300
  7.5 49.9 %copy-start.5 = (bf16[192,1152]{1,0:T(8,128)(2,1)}, bf16[192,1152]{1,0:T(8,128)(2,1)S(1)}, u32[]{:S(2)}) copy-start(bf16[192,1152]{1,0:T(8,128)(2,1)S(1)} %pad_maximum_fusion.refs_5_) | copy-start | bytes 1327108
  7.5 12.0 %collective-permute-start.5 = (bf16[192,1152]{1,0:T(8,128)(2,1)S(1)}, bf16[192,1152]{1,0:T(8,128)(2,1)S(1)}, u32[]{:S(2)}, u32[]{:S(2)}) collective-permute-start(bf16[192,1152]{1,0:T(8,128)(2,1)S(1)} %pad_maximum_fusion.refs_5_), channel_id=1, source_target_pairs={{0,32},{1,225},{4,36},{5,229},{8,40},{9,233},{12,44},{13,237},{16,... | collective-permute-start | bytes 1327112 | tf_op jit(solution)/shard_map/ppermute | solution.py:54
  14.2 18.8 %collective-permute-start.1 = (bf16[256,1536]{1,0:T(8,128)(2,1)S(1)}, bf16[256,1536]{1,0:T(8,128)(2,1)S(1)}, u32[]{:S(2)}, u32[]{:S(2)}) collective-permute-start(bf16[256,1536]{1,0:T(8,128)(2,1)S(1)} %fusion.3.refs_0_), channel_id=1, source_target_pairs={{0,16},{1,17},{4,20},{5,21},{8,24},{9,25},{12,28},{13,29},{16,2},{... | collective-permute-start | bytes 2359304 | tf_op jit(solution)/shard_map/ppermute | solution.py:40
  15.5 17.9 %collective-permute-start.2 = (bf16[256,1536]{1,0:T(8,128)(2,1)S(1)}, bf16[256,1536]{1,0:T(8,128)(2,1)S(1)}, u32[]{:S(2)}, u32[]{:S(2)}) collective-permute-start(bf16[256,1536]{1,0:T(8,128)(2,1)S(1)} %fusion.3.refs_0_), channel_id=1, source_target_pairs={{0,18},{1,19},{4,22},{5,23},{8,26},{9,27},{12,30},{13,31},{16,0},{... | collective-permute-start | bytes 2359304 | tf_op jit(solution)/shard_map/ppermute | solution.py:40
  19.5 13.9 %collective-permute-start.6 = (bf16[192,1152]{1,0:T(8,128)(2,1)S(1)}, bf16[192,1152]{1,0:T(8,128)(2,1)}, u32[]{:S(2)}, u32[]{:S(2)}) collective-permute-start(bf16[192,1152]{1,0:T(8,128)(2,1)S(1)} %collective-permute-done.5.refs_6_), channel_id=1, source_target_pairs={{0,32},{1,225},{4,36},{5,229},{8,40},{9,233},{12,44},{13,237},{16,... | collective-permute-start | bytes 1327112 | tf_op jit(solution)/shard_map/ppermute | solution.py:54
  33.0 24.4 %copy-start.6 = (bf16[256,1536]{1,0:T(8,128)(2,1)}, bf16[256,1536]{1,0:T(8,128)(2,1)S(1)}, u32[]{:S(2)}) copy-start(bf16[256,1536]{1,0:T(8,128)(2,1)S(1)} %collective-permute-done.1.refs_1_) | copy-start | bytes 2359300
  33.4 24.0 %copy-start.7 = (bf16[256,1536]{1,0:T(8,128)(2,1)}, bf16[256,1536]{1,0:T(8,128)(2,1)S(1)}, u32[]{:S(2)}) copy-start(bf16[256,1536]{1,0:T(8,128)(2,1)S(1)} %collective-permute-done.2.refs_2_) | copy-start | bytes 2359300
  33.4 7.8 %collective-permute-start.7 = (bf16[192,1152]{1,0:T(8,128)(2,1)}, bf16[192,1152]{1,0:T(8,128)(2,1)}, u32[]{:S(2)}, u32[]{:S(2)}) collective-permute-start(bf16[192,1152]{1,0:T(8,128)(2,1)} %collective-permute-done.6.refs_7_), channel_id=1, source_target_pairs={{0,32},{1,225},{4,36},{5,229},{8,40},{9,233},{12,44},{13,237},{16,... | collective-permute-start | bytes 1327112 | tf_op jit(solution)/shard_map/ppermute | solution.py:54
  34.5 11.5 %collective-permute-start.9 = (bf16[192,1152]{1,0:T(8,128)(2,1)S(1)}, bf16[192,1152]{1,0:T(8,128)(2,1)S(1)}, u32[]{:S(2)}, u32[]{:S(2)}) collective-permute-start(bf16[192,1152]{1,0:T(8,128)(2,1)S(1)} %collective-permute-done.5.refs_6_), channel_id=1, source_target_pairs={{0,1},{1,0},{4,5},{5,4},{8,9},{9,8},{12,13},{13,12},{16,17},{17,16... | collective-permute-start | bytes 1327112 | tf_op jit(solution)/shard_map/ppermute | solution.py:44
  34.5 22.8 %collective-permute-start.10 = (bf16[192,1152]{1,0:T(8,128)(2,1)}, bf16[192,1152]{1,0:T(8,128)(2,1)}, u32[]{:S(2)}, u32[]{:S(2)}) collective-permute-start(bf16[192,1152]{1,0:T(8,128)(2,1)} %collective-permute-done.6.refs_7_), channel_id=1, source_target_pairs={{0,1},{1,0},{4,5},{5,4},{8,9},{9,8},{12,13},{13,12},{16,17},{17,16... | collective-permute-start | bytes 1327112 | tf_op jit(solution)/shard_map/ppermute | solution.py:44
  41.2 16.2 %collective-permute-start.8 = (bf16[192,1152]{1,0:T(8,128)(2,1)}, bf16[192,1152]{1,0:T(8,128)(2,1)}, u32[]{:S(2)}, u32[]{:S(2)}) collective-permute-start(bf16[192,1152]{1,0:T(8,128)(2,1)} %collective-permute-done.7.refs_8_), channel_id=1, source_target_pairs={{0,32},{1,225},{4,36},{5,229},{8,40},{9,233},{12,44},{13,237},{16,... | collective-permute-start | bytes 1327112 | tf_op jit(solution)/shard_map/ppermute | solution.py:54
  43.2 14.2 %collective-permute-start.11 = (bf16[192,1152]{1,0:T(8,128)(2,1)}, bf16[192,1152]{1,0:T(8,128)(2,1)}, u32[]{:S(2)}, u32[]{:S(2)}) collective-permute-start(bf16[192,1152]{1,0:T(8,128)(2,1)} %collective-permute-done.7.refs_8_), channel_id=1, source_target_pairs={{0,1},{1,0},{4,5},{5,4},{8,9},{9,8},{12,13},{13,12},{16,17},{17,16... | collective-permute-start | bytes 1327112 | tf_op jit(solution)/shard_map/ppermute | solution.py:44
  44.0 11.6 %collective-permute-start.3 = (bf16[128,1536]{1,0:T(8,128)(2,1)}, bf16[128,1536]{1,0:T(8,128)(2,1)S(1)}, u32[]{:S(2)}, u32[]{:S(2)}) collective-permute-start(bf16[128,1536]{1,0:T(8,128)(2,1)} %slice.8), channel_id=1, source_target_pairs={{0,16},{1,17},{4,20},{5,21},{8,24},{9,25},{12,28},{13,29},{16,2},{... | collective-permute-start | bytes 1179656 | tf_op jit(solution)/shard_map/ppermute | solution.py:40
  46.8 10.5 %collective-permute-start.4 = (bf16[128,1536]{1,0:T(8,128)(2,1)}, bf16[128,1536]{1,0:T(8,128)(2,1)}, u32[]{:S(2)}, u32[]{:S(2)}) collective-permute-start(bf16[128,1536]{1,0:T(8,128)(2,1)} %slice.9), channel_id=1, source_target_pairs={{0,18},{1,19},{4,22},{5,23},{8,26},{9,27},{12,30},{13,31},{16,0},{... | collective-permute-start | bytes 1179656 | tf_op jit(solution)/shard_map/ppermute | solution.py:40
  67.3 5.6 %collective-permute-start.12 = (bf16[2,2,256,768]{3,2,1,0:T(8,128)(2,1)}, bf16[2,2,256,768]{3,2,1,0:T(8,128)(2,1)S(1)}, u32[]{:S(2)}, u32[]{:S(2)}) collective-permute-start(bf16[2,2,256,768]{3,2,1,0:T(8,128)(2,1)} %get-tuple-element.31.own), channel_id=1, source_target_pairs={{0,1},{1,0},{4,5},{5,4},{8,9},{9,8},{12,13},{13,12},{16,17},{17,16... | collective-permute-start | bytes 4718600 | tf_op jit(solution)/shard_map/ppermute | solution.py:44
  68.7 15.1 %collective-permute-start.13 = (bf16[2,256,768]{2,1,0:T(8,128)(2,1)}, bf16[2,256,768]{2,1,0:T(8,128)(2,1)S(1)}, u32[]{:S(2)}, u32[]{:S(2)}) collective-permute-start(bf16[2,256,768]{2,1,0:T(8,128)(2,1)} %get-tuple-element.32), channel_id=1, source_target_pairs={{0,13},{1,4},{4,1},{5,8},{8,5},{9,12},{12,9},{13,0},{16,29},{17,20... | collective-permute-start | bytes 2359304 | tf_op jit(solution)/shard_map/ppermute | solution.py:48
  69.9 11.0 %collective-permute-start.14 = (bf16[256,768]{1,0:T(8,128)(2,1)}, bf16[256,768]{1,0:T(8,128)(2,1)}, u32[]{:S(2)}, u32[]{:S(2)}) collective-permute-start(bf16[256,768]{1,0:T(8,128)(2,1)} %get-tuple-element.33), channel_id=1, source_target_pairs={{0,32},{1,33},{4,36},{5,37},{8,40},{9,41},{12,44},{13,45},{16,48},... | collective-permute-start | bytes 1179656 | tf_op jit(solution)/shard_map/ppermute | solution.py:40
  69.9 13.9 %collective-permute-start.15 = (bf16[256,768]{1,0:T(8,128)(2,1)}, bf16[256,768]{1,0:T(8,128)(2,1)}, u32[]{:S(2)}, u32[]{:S(2)}) collective-permute-start(bf16[256,768]{1,0:T(8,128)(2,1)} %get-tuple-element.34), channel_id=1, source_target_pairs={{0,224},{1,225},{4,228},{5,229},{8,232},{9,233},{12,236},{13,237},... | collective-permute-start | bytes 1179656 | tf_op jit(solution)/shard_map/ppermute | solution.py:40
  72.9 26.1 %collective-permute-start.16 = (bf16[256,768]{1,0:T(8,128)(2,1)}, bf16[256,768]{1,0:T(8,128)(2,1)S(1)}, u32[]{:S(2)}, u32[]{:S(2)}) collective-permute-start(bf16[256,768]{1,0:T(8,128)(2,1)} %get-tuple-element.38), channel_id=1, source_target_pairs={{0,32},{1,33},{4,36},{5,37},{8,40},{9,41},{12,44},{13,45},{16,48},... | collective-permute-start | bytes 1179656 | tf_op jit(solution)/shard_map/ppermute | solution.py:40
  72.9 26.5 %collective-permute-start.17 = (bf16[256,768]{1,0:T(8,128)(2,1)}, bf16[256,768]{1,0:T(8,128)(2,1)S(1)}, u32[]{:S(2)}, u32[]{:S(2)}) collective-permute-start(bf16[256,768]{1,0:T(8,128)(2,1)} %get-tuple-element.40), channel_id=1, source_target_pairs={{0,224},{1,225},{4,228},{5,229},{8,232},{9,233},{12,236},{13,237},... | collective-permute-start | bytes 1179656 | tf_op jit(solution)/shard_map/ppermute | solution.py:40
  81.0 18.6 %collective-permute-start.22 = (bf16[256,768]{1,0:T(8,128)(2,1)}, bf16[256,768]{1,0:T(8,128)(2,1)S(1)}, u32[]{:S(2)}, u32[]{:S(2)}) collective-permute-start(bf16[256,768]{1,0:T(8,128)(2,1)} %collective-permute-done.14.below), channel_id=1, source_target_pairs={{0,13},{1,4},{4,1},{5,8},{8,5},{9,12},{12,9},{13,0},{16,29},{17,20... | collective-permute-start | bytes 1179656 | tf_op jit(solution)/shard_map/ppermute | solution.py:48
  83.8 16.1 %collective-permute-start.23 = (bf16[256,768]{1,0:T(8,128)(2,1)}, bf16[256,768]{1,0:T(8,128)(2,1)S(1)}, u32[]{:S(2)}, u32[]{:S(2)}) collective-permute-start(bf16[256,768]{1,0:T(8,128)(2,1)} %collective-permute-done.15.above), channel_id=1, source_target_pairs={{0,13},{1,4},{4,1},{5,8},{8,5},{9,12},{12,9},{13,0},{16,29},{17,20... | collective-permute-start | bytes 1179656 | tf_op jit(solution)/shard_map/ppermute | solution.py:48
  94.5 6.1 %collective-permute-start.18 = (bf16[256,768]{1,0:T(8,128)(2,1)}, bf16[256,768]{1,0:T(8,128)(2,1)S(1)}, u32[]{:S(2)}, u32[]{:S(2)}) collective-permute-start(bf16[256,768]{1,0:T(8,128)(2,1)} %collective-permute-done.14.below), channel_id=1, source_target_pairs={{0,1},{1,0},{4,5},{5,4},{8,9},{9,8},{12,13},{13,12},{16,17},{17,16... | collective-permute-start | bytes 1179656 | tf_op jit(solution)/shard_map/ppermute | solution.py:44
  99.0 2.7 %collective-permute-start.19 = (bf16[256,768]{1,0:T(8,128)(2,1)}, bf16[256,768]{1,0:T(8,128)(2,1)S(1)}, u32[]{:S(2)}, u32[]{:S(2)}) collective-permute-start(bf16[256,768]{1,0:T(8,128)(2,1)} %collective-permute-done.15.above), channel_id=1, source_target_pairs={{0,1},{1,0},{4,5},{5,4},{8,9},{9,8},{12,13},{13,12},{16,17},{17,16... | collective-permute-start | bytes 1179656 | tf_op jit(solution)/shard_map/ppermute | solution.py:44
  99.4 2.4 %collective-permute-start.20 = (bf16[256,768]{1,0:T(8,128)(2,1)S(1)}, bf16[256,768]{1,0:T(8,128)(2,1)S(1)}, u32[]{:S(2)}, u32[]{:S(2)}) collective-permute-start(bf16[256,768]{1,0:T(8,128)(2,1)S(1)} %collective-permute-done.16.refs_0_), channel_id=1, source_target_pairs={{0,1},{1,0},{4,5},{5,4},{8,9},{9,8},{12,13},{13,12},{16,17},{17,16... | collective-permute-start | bytes 1179656 | tf_op jit(solution)/shard_map/ppermute | solution.py:44
  99.6 2.5 %collective-permute-start.21 = (bf16[256,768]{1,0:T(8,128)(2,1)S(1)}, bf16[256,768]{1,0:T(8,128)(2,1)S(1)}, u32[]{:S(2)}, u32[]{:S(2)}) collective-permute-start(bf16[256,768]{1,0:T(8,128)(2,1)S(1)} %collective-permute-done.17.refs_1_), channel_id=1, source_target_pairs={{0,1},{1,0},{4,5},{5,4},{8,9},{9,8},{12,13},{13,12},{16,17},{17,16... | collective-permute-start | bytes 1179656 | tf_op jit(solution)/shard_map/ppermute | solution.py:44
  102.1 19.7 %copy-start.2 = (s32[3]{0:T(128)S(1)}, s32[3]{0:T(128)}, u32[]{:S(2)}) copy-start(s32[3]{0:T(128)} %pad_add_fusion.place) | copy-start | bytes 40
  107.8 6.6 %collective-permute-start.24 = (bf16[256,384]{1,0:T(8,128)(2,1)S(1)}, bf16[256,384]{1,0:T(8,128)(2,1)S(1)}, u32[]{:S(2)}, u32[]{:S(2)}) collective-permute-start(bf16[256,384]{1,0:T(8,128)(2,1)S(1)} %get-tuple-element.46), channel_id=1, source_target_pairs={{0,18},{1,19},{4,22},{5,23},{8,26},{9,27},{12,30},{13,31},{16,0},{... | collective-permute-start | bytes 589832 | tf_op jit(solution)/shard_map/ppermute | solution.py:40
  110.6 11.2 %collective-permute-start.25 = (bf16[256,384]{1,0:T(8,128)(2,1)S(1)}, bf16[256,384]{1,0:T(8,128)(2,1)S(1)}, u32[]{:S(2)}, u32[]{:S(2)}) collective-permute-start(bf16[256,384]{1,0:T(8,128)(2,1)S(1)} %get-tuple-element.47), channel_id=1, source_target_pairs={{0,16},{1,17},{4,20},{5,21},{8,24},{9,25},{12,28},{13,29},{16,2},{... | collective-permute-start | bytes 589832 | tf_op jit(solution)/shard_map/ppermute | solution.py:40
  110.6 11.2 %collective-permute-start.26 = (bf16[256,384]{1,0:T(8,128)(2,1)S(1)}, bf16[256,384]{1,0:T(8,128)(2,1)S(1)}, u32[]{:S(2)}, u32[]{:S(2)}) collective-permute-start(bf16[256,384]{1,0:T(8,128)(2,1)S(1)} %get-tuple-element.48), channel_id=1, source_target_pairs={{0,2},{1,3},{4,6},{5,7},{8,10},{9,11},{12,14},{13,15},{16,18},{17,... | collective-permute-start | bytes 589832 | tf_op jit(solution)/shard_map/ppermute | solution.py:40
  (8 other events, 33.8 us)

commit v3 on v2

--- a/solution.py
+++ b/solution.py
@@ -79,7 +79,9 @@
 VMEM = pl.BlockSpec(memory_space=pltpu.VMEM)
 SMEM = pl.BlockSpec(memory_space=pltpu.SMEM)
 PARAMS = pltpu.CompilerParams(vmem_limit_bytes=60 * 1024 * 1024)
-WIDE = pltpu.CompilerParams(vmem_limit_bytes=16 * 1024 * 1024)
+NEAR = pltpu.CompilerParams(vmem_limit_bytes=60 * 1024 * 1024)
+FAR = pltpu.CompilerParams(vmem_limit_bytes=60 * 1024 * 1024)
+SIDE = pltpu.CompilerParams(vmem_limit_bytes=8 * 1024 * 1024)
 
 
 def weight_copies(weights, pieces, sems, z, yl, core):
@@ -123,7 +125,7 @@
     tokens, pieces = refs[:5], refs[5:13]
     query_gain, key_gain, q_out, own, edge = refs[13:18]
     alone = refs[18:22]
-    weights, rows, sems, token_sems = refs[22:]
+    weights, rows, q_done, kv_done, sems, token_sems, out_sems = refs[22:]
     y, core = place[0], place[1]
     slots = [role * 2 + yl for yl, role in sources(y, core)]
     copies = weight_copies(weights, pieces, sems, place[2], lax.rem(y, 2), core)
@@ -132,6 +134,7 @@
         copy.start()
     for copy in copies:
         copy.wait()
+    leaving = []
     for slot in range(4):
         role, yl = slot // 2, slot % 2
         projected = jnp.dot(rows[slot], weights[...], preferred_element_type=F32)
@@ -140,12 +143,16 @@
             vs = slice(head * 2 * HD + HD, (head + 1) * 2 * HD)
             span = slice(head * HD, (head + 1) * HD)
             part = lambda kind: projected[:, kind * GROUP + head * HD : kind * GROUP + (head + 1) * HD]
-            k = head_norm(part(0), key_gain)
-            v = part(1).astype(BF16)
-            for out in [own.at[role, yl], alone[slot]] + ([edge.at[yl]] if role == 0 else []):
-                out[:, ks] = k
-                out[:, vs] = v
-            q_out[slot, :, span] = head_norm(part(2), query_gain)
+            kv_done[slot, :, ks] = head_norm(part(0), key_gain)
+            kv_done[slot, :, vs] = part(1).astype(BF16)
+            q_done[slot, :, span] = head_norm(part(2), query_gain)
+        targets = [own.at[role, yl], alone[slot]] + ([edge.at[yl]] if role == 0 else [])
+        moves = [(kv_done.at[slot], target) for target in targets] + [(q_done.at[slot], q_out.at[slot])]
+        for index, (source, target) in enumerate(moves):
+            leaving.append(pltpu.make_async_copy(source, target, out_sems.at[slot, index]))
+            leaving[-1].start()
+    for copy in leaving:
+        copy.wait()
 
 
 ANY = pl.BlockSpec(memory_space=pl.ANY)
@@ -159,12 +166,15 @@
         name="project",
         out_shape=(jax.ShapeDtypeStruct((4, TOKENS, GROUP), BF16), kv(2, 2), kv(2)) + (kv(),) * 4,
         in_specs=[SMEM] + [ANY] * 13 + [VMEM] * 2,
-        out_specs=[VMEM] * 7,
+        out_specs=[ANY] * 7,
         scratch_shapes=[
             pltpu.VMEM((D, 3 * GROUP), BF16),
             pltpu.VMEM((4, TOKENS, D), BF16),
+            pltpu.VMEM((4, TOKENS, GROUP), BF16),
+            pltpu.VMEM((4, TOKENS, 2 * GROUP), BF16),
             pltpu.SemaphoreType.DMA((16,)),
             pltpu.SemaphoreType.DMA((5,)),
+            pltpu.SemaphoreType.DMA((4, 4)),
         ],
         compiler_params=PARAMS,
         cost_estimate=LIGHT,
@@ -211,71 +221,70 @@
     return jnp.where(flag > 0, 0.0, 1e30).astype(F32)
 
 
-def near_kernel(valid, q, own, mate, edge, below, above, peaks, totals):
-    no_edge = penalty(valid[2])
+def near_kernel(q, own, mate, *states):
+    peaks, totals = states[:2], states[2:]
     for yl in range(2):
-        no_row, row = (penalty(valid[1]), above) if yl else (penalty(valid[0]), below)
         for role in range(2):
-            slot = role * 2 + yl
-            if role == 0:
-                groups = [
-                    (None, [own[0, 0], own[0, 1], mate[1, 0], mate[1, 1]]),
-                    (no_edge, [edge[0], edge[1]]),
-                    (no_row, [row[...]]),
-                ]
-            else:
-                groups = [
-                    (None, [own[1, 0], own[1, 1], mate[1, 0], mate[1, 1], mate[0, 0], mate[0, 1]])
-                ]
-            peak, total = attend_tiles(q[slot], groups, None, None)
-            peaks[0, slot] = jnp.broadcast_to(peak, (TOKENS, HD))
-            totals[0, slot] = total
-
-
-def far_kernel(valid, q, peaks, totals, *refs):
-    inner_rows, mate_outer_rows, mate_inner_rows, corners = refs[0:2], refs[2:4], refs[4:6], refs[6:8]
-    outs, done = refs[8:12], refs[12]
+            tiles = [own[role, 0], own[role, 1], mate[1, 0], mate[1, 1]]
+            if role:
+                tiles += [mate[0, 0], mate[0, 1]]
+            peak, total = attend_tiles(q[role * 2 + yl], [(None, tiles)], None, None)
+            peaks[role][0, yl] = jnp.broadcast_to(peak, (TOKENS, HD))
+            totals[role][0, yl] = total
+
+
+def far_kernel(valid, q, *refs):
+    peaks, totals = refs[:2], refs[2:4]
+    outer_rows, inner_rows, mate_outer_rows, mate_inner_rows, corners = (refs[n : n + 2] for n in range(4, 14, 2))
+    edge, outs, done = refs[14], refs[15:19], refs[19]
     core = valid[3]
     for yl in range(2):
         no_row = penalty(valid[yl])
         for role in range(2):
-            slot = role * 2 + yl
             if role == 0:
                 groups = [
-                    (no_row, [mate_inner_rows[yl][...]]),
+                    (no_row, [outer_rows[yl][...], mate_inner_rows[yl][...]]),
+                    (penalty(valid[2]), [edge[0], edge[1]]),
                     (jnp.maximum(no_row, penalty(valid[2])), [corners[yl][...]]),
                 ]
             else:
                 groups = [(no_row, [rows[yl][...] for rows in (inner_rows, mate_inner_rows, mate_outer_rows)])]
-            _, total = attend_tiles(q[slot], groups, peaks[0, slot], totals[0, slot])
+            _, total = attend_tiles(q[role * 2 + yl], groups, peaks[role][0, yl], totals[role][0, yl])
             yh = 1 - core if role else core
             done[yh * 2 + yl] = (total[:, :HD] / total[:, HD:]).astype(BF16)
     for out, step in zip(outs, STEPS, strict=True):
         out[...] = done[lax.rem(valid[4] - step + 4, 4)]
 
 
+def penalty(flag):
+    return jnp.where(flag > 0, 0.0, 1e30).astype(F32)
+
+
 def head_spec(array, width):
     lead = array.ndim - 1
     return pl.BlockSpec(array.shape[:-1] + (width,), lambda h: (0,) * lead + (h,))
 
 
-STATE = lambda width: pl.BlockSpec((1, 4, TOKENS, width), lambda h: (h, 0, 0, 0))
-
-
-def attend_near(valid, q, *kv):
+PEAK, TOTAL = (
+    (
+        jax.ShapeDtypeStruct((GROUP_HEADS, 2, TOKENS, width), F32),
+        pl.BlockSpec((1, 2, TOKENS, width), lambda h: (h, 0, 0, 0)),
+    )
+    for width in (HD, 2 * HD)
+)
+
+
+def attend_near(q, own, mate):
     return pl.pallas_call(
         near_kernel,
         name="attend_near",
         grid=(GROUP_HEADS,),
-        out_shape=(
-            jax.ShapeDtypeStruct((GROUP_HEADS, 4, TOKENS, HD), F32),
-            jax.ShapeDtypeStruct((GROUP_HEADS, 4, TOKENS, 2 * HD), F32),
-        ),
-        in_specs=[SMEM, head_spec(q, HD)] + [head_spec(a, 2 * HD) for a in kv],
-        out_specs=[STATE(HD), STATE(2 * HD)],
-        compiler_params=WIDE,
+        out_shape=(PEAK[0], PEAK[0], TOTAL[0], TOTAL[0]),
+        in_specs=[head_spec(q, HD), head_spec(own, 2 * HD), head_spec(mate, 2 * HD)],
+        out_specs=[PEAK[1], PEAK[1], TOTAL[1], TOTAL[1]],
+        compiler_params=NEAR,
         cost_estimate=LIGHT,
-    )(valid, q, *kv)
+    )(q, own, mate)
 
 
 def attend_far(valid, q, peaks, totals, *kv):
@@ -284,12 +293,13 @@
         name="attend_far",
         grid=(GROUP_HEADS,),
         out_shape=(jax.ShapeDtypeStruct((TOKENS, GROUP), BF16),) * 4,
-        in_specs=[SMEM, head_spec(q, HD), STATE(HD), STATE(2 * HD)] + [head_spec(a, 2 * HD) for a in kv],
+        in_specs=[SMEM, head_spec(q, HD), PEAK[1], PEAK[1], TOTAL[1], TOTAL[1]]
+        + [head_spec(a, 2 * HD) for a in kv],
         out_specs=[pl.BlockSpec((TOKENS, HD), lambda h: (0, h))] * 4,
         scratch_shapes=[pltpu.VMEM((4, TOKENS, HD), BF16)],
-        compiler_params=WIDE,
+        compiler_params=FAR,
         cost_estimate=LIGHT,
-    )(valid, q, peaks, totals, *kv)
+    )(valid, q, *peaks, *totals, *kv)
 
 
 def side_kernel(place, *refs):
@@ -305,7 +315,7 @@
         out_shape=jax.ShapeDtypeStruct((TOKENS, D), BF16),
         in_specs=[SMEM] + [VMEM] * 4,
         out_specs=VMEM,
-        compiler_params=WIDE,
+        compiler_params=SIDE,
     )(place, *parts).reshape(shape)
 
 
@@ -328,8 +338,9 @@
     ring.append(ring_step(ring[1]))
     ring.append(ring_step(after(ring[2], behind, ahead)))
     ring.append(ring_step(ring[3]))
-    pieces = ring + [swap_cores(piece) for piece in ring[1:4]]
-    tokens = [normed, behind, ahead, shift(behind[:HALF], dy=1), shift(ahead[HALF:], dy=-1)]
+    opposite = [shift(behind[:HALF], dy=1), shift(ahead[HALF:], dy=-1)]
+    pieces = ring + [swap_cores(ring[1]), swap_cores(ring[2]), swap_cores(after(ring[3], *opposite))]
+    tokens = [normed, behind, ahead] + opposite
 
     place = jnp.stack([y, core, z]).astype(jnp.int32)
     q, own, edge_out, outer_low, outer_high, inner_low, inner_high = project(
@@ -341,16 +352,26 @@
     mate = swap_cores(own)
     inner_below = shift(after(inner_high, mate), dz=1)
     inner_above = shift(after(inner_low, mate), dz=-1)
-    corner_below = outward(outer_below)
-    corner_above = outward(outer_above)
+    outer_peak, inner_peak, outer_total, inner_total = attend_near(q, own, mate)
+    corner_below = outward(after(outer_below, inner_peak))
+    corner_above = outward(after(outer_above, inner_peak))
     last_x = jnp.where(core == 0, 0, 3)
     valid = jnp.stack([z > 0, z < 7, x != last_x, core, y]).astype(jnp.int32)
-    peaks, totals = attend_near(valid, q, own, mate, edge, outer_below, outer_above)
-    mate_outer_rows = [swap_cores(after(row, peaks)) for row in (outer_below, outer_above)]
-    inner_rows = [inner_below, inner_above]
-    mate_inner_rows = [swap_cores(after(row, peaks)) for row in inner_rows]
+    outer_rows, inner_rows = (outer_below, outer_above), (inner_below, inner_above)
+    mate_outer_rows = [swap_cores(after(row, *inner_rows)) for row in outer_rows]
+    mate_inner_rows = [swap_cores(after(row, inner_peak)) for row in inner_rows]
     attended = attend_far(
-        valid, q, peaks, totals, *inner_rows, *mate_outer_rows, *mate_inner_rows, corner_below, corner_above
+        valid,
+        q,
+        (outer_peak, inner_peak),
+        (outer_total, inner_total),
+        *outer_rows,
+        *inner_rows,
+        *mate_outer_rows,
+        *mate_inner_rows,
+        corner_below,
+        corner_above,
+        edge,
     )
     back = [attended[0]] + [shift(tile, dy=-step) for step, tile in zip(STEPS[1:], attended[1:], strict=True)]
     return side_by_side(place, back, hidden.shape)

time: 123 us -> 119 us (0.967)
  the two profiles are of different devices: /device:TPU:1 before, /device:TPU:7 now
where the time goes in v3:
time: 119 us; the launch traced here: 118 us
  waiting for transfers between devices  47.4 us (40%)
  starting transfers between devices  35.7 us (30%)
  Pallas kernels  28.4 us (24%)
  local copies, waits for them, and re-layouts  3.76 us (3%)
  other arithmetic  2.9 us (2%)
    ppermute x11, waiting for transfers between devices, shift(): lax.ppermute(array, AXES, pairs(lambda z, y, x, core: (z + dz, y + dy, x,...  30.9 us
    ppermute x11, starting transfers between devices, shift(): lax.ppermute(array, AXES, pairs(lambda z, y, x, core: (z + dz, y + dy, x,...  14.8 us
    ppermute x4, starting transfers between devices, ring_step(): lax.ppermute(array, AXES, pairs(lambda z, y, x, core: (z + (-1 if core el...  10.2 us
    pallas_call x1, Pallas kernels, attend_near(): pl.pallas_call(near_kernel, name='attend_near', grid=(GROUP_HEADS,), out_...  9.36 us
    pallas_call x1, Pallas kernels, project(): pl.pallas_call(project_kernel, name='project', out_shape=(jax.ShapeDtypeS...  9.21 us
    pallas_call x1, Pallas kernels, attend_far(): pl.pallas_call(far_kernel, name='attend_far', grid=(GROUP_HEADS,), out_sh...  8.28 us
    ppermute x4, waiting for transfers between devices, ring_step(): lax.ppermute(array, AXES, pairs(lambda z, y, x, core: (z + (-1 if core el...  8.23 us
    ppermute x3, waiting for transfers between devices, outward(): lax.ppermute(array, AXES, pairs(lambda z, y, x, core: (z + dz, y, x + (1...  5.65 us
  transfers between devices with their start and end apart: 27, of which 13 were waited for; matrix products, arithmetic and copies ran while one was open for 3% of the time, Pallas kernels for 8%

profile of v3, /device:TPU:7, one launch (start us, length us, event | category | flops | bytes accessed | tf_op | source)
XLA Modules:
  0.0 118.4 jit_solution(7771420222806472811)
XLA Ops:
  0.0 1.2 %constant_dynamic-slice_fusion.2 = (bf16[96,384]{1,0:T(8,128)(2,1)S(1)}, bf16[96,384]{1,0:T(8,128)(2,1)S(1)}, bf16[96,384]{1,0:T(8,128)(2,1)S(1)}, bf16[96,384]{...) fusion(bf16[96,4608]{1,0:T(8,128)(2,1)} %param.7, s32[]{:T(128)S(6)} %select_n.26, ...), kind=kLoop, calls=%fused_computation.13 | loop fusion | bytes 884760 | tf_op jit(solution)/shard_map/dynamic_slice | solution.py:328
  1.3 1.4 %collective-permute-start = (bf16[96,1152]{1,0:T(8,128)(2,1)S(1)}, bf16[96,1152]{1,0:T(8,128)(2,1)S(1)}, u32[]{:S(2)}, u32[]{:S(2)}) collective-permute-start(bf16[96,1152]{1,0:T(8,128)(2,1)S(1)} %pad_maximum_fusion.1), channel_id=1, source_target_pairs={{0,16},{1,17},{4,20},{5,21},{8,24},{9,25},{12,28},{13,29},{16,0},{... | collective-permute-start | bytes 663560 | tf_op jit(solution)/shard_map/ppermute | solution.py:60
  2.7 1.6 %reduce_sum.18 = f32[4,4,16]{2,1,0:T(4,128)S(1)} reduce(f32[4,4,16,1536]{3,2,1,0:T(8,128)} %param.6, f32[]{:T(128)} %constant.44.clone.1), dimensions={3}, to_apply=%region_0.0 | reduce | flops 392960 | bytes 1573892 | tf_op jit(solution)/shard_map/reduce_sum | solution.py:70
  5.1 2.5 %collective-permute-done = bf16[96,1152]{1,0:T(8,128)(2,1)S(1)} collective-permute-done((bf16[96,1152]{1,0:T(8,128)(2,1)S(1)}, bf16[96,1152]{1,0:T(8,128)(2,1)S(1)}, u32[]{:S(2)}, u32[]{:S(2)}) %collective-permute-start) | collective-permute-done | bytes 221216 | tf_op jit(solution)/shard_map/ppermute | solution.py:60
  7.7 5.7 %collective-permute-start.5 = (bf16[192,1152]{1,0:T(8,128)(2,1)S(1)}, bf16[192,1152]{1,0:T(8,128)(2,1)}, u32[]{:S(2)}, u32[]{:S(2)}) collective-permute-start(bf16[192,1152]{1,0:T(8,128)(2,1)S(1)} %pad_maximum_fusion.refs_5_), channel_id=1, source_target_pairs={{0,32},{1,225},{4,36},{5,229},{8,40},{9,233},{12,44},{13,237},{16,... | collective-permute-start | bytes 1327112 | tf_op jit(solution)/shard_map/ppermute | solution.py:54
  13.4 1.3 %collective-permute-start.1 = (bf16[256,1536]{1,0:T(8,128)(2,1)S(1)}, bf16[256,1536]{1,0:T(8,128)(2,1)S(1)}, u32[]{:S(2)}, u32[]{:S(2)}) collective-permute-start(bf16[256,1536]{1,0:T(8,128)(2,1)S(1)} %fusion.3.refs_0_), channel_id=1, source_target_pairs={{0,16},{1,17},{4,20},{5,21},{8,24},{9,25},{12,28},{13,29},{16,2},{... | collective-permute-start | bytes 2359304 | tf_op jit(solution)/shard_map/ppermute | solution.py:40
  14.7 1.4 %collective-permute-start.2 = (bf16[256,1536]{1,0:T(8,128)(2,1)S(1)}, bf16[256,1536]{1,0:T(8,128)(2,1)S(1)}, u32[]{:S(2)}, u32[]{:S(2)}) collective-permute-start(bf16[256,1536]{1,0:T(8,128)(2,1)S(1)} %fusion.3.refs_0_), channel_id=1, source_target_pairs={{0,18},{1,19},{4,22},{5,23},{8,26},{9,27},{12,30},{13,31},{16,0},{... | collective-permute-start | bytes 2359304 | tf_op jit(solution)/shard_map/ppermute | solution.py:40
  16.1 2.5 %collective-permute-done.5.refs_6_ = bf16[192,1152]{1,0:T(8,128)(2,1)} collective-permute-done((bf16[192,1152]{1,0:T(8,128)(2,1)S(1)}, bf16[192,1152]{1,0:T(8,128)(2,1)}, u32[]{:S(2)}, u32[]{:S(2)}) %collective-permute-start.5) | collective-permute-done | bytes 442400 | tf_op jit(solution)/shard_map/ppermute | solution.py:54
  18.6 3.4 %collective-permute-start.6 = (bf16[192,1152]{1,0:T(8,128)(2,1)}, bf16[192,1152]{1,0:T(8,128)(2,1)}, u32[]{:S(2)}, u32[]{:S(2)}) collective-permute-start(bf16[192,1152]{1,0:T(8,128)(2,1)} %collective-permute-done.5.refs_6_), channel_id=1, source_target_pairs={{0,32},{1,225},{4,36},{5,229},{8,40},{9,233},{12,44},{13,237},{16,... | collective-permute-start | bytes 1327112 | tf_op jit(solution)/shard_map/ppermute | solution.py:54
  22.0 10.2 %collective-permute-done.1.refs_1_ = bf16[256,1536]{1,0:T(8,128)(2,1)S(1)} collective-permute-done((bf16[256,1536]{1,0:T(8,128)(2,1)S(1)}, bf16[256,1536]{1,0:T(8,128)(2,1)S(1)}, u32[]{:S(2)}, u32[]{:S(2)}) %collective-permute-start.1) | collective-permute-done | bytes 786464 | tf_op jit(solution)/shard_map/ppermute | solution.py:40
  32.6 1.1 collective-permute-start.7
  33.7 0.9 collective-permute-start.3
  34.7 1.9 %collective-permute-start.4 = (bf16[128,1536]{1,0:T(8,128)(2,1)S(1)}, bf16[128,1536]{1,0:T(8,128)(2,1)}, u32[]{:S(2)}, u32[]{:S(2)}) collective-permute-start(bf16[128,1536]{1,0:T(8,128)(2,1)S(1)} %slice.9), channel_id=1, source_target_pairs={{0,18},{1,19},{4,22},{5,23},{8,26},{9,27},{12,30},{13,31},{16,0},{... | collective-permute-start | bytes 1179656 | tf_op jit(solution)/shard_map/ppermute | solution.py:40
  37.1 7.4 %collective-permute-done.3.refs_3_ = bf16[128,1536]{1,0:T(8,128)(2,1)S(1)} collective-permute-done((bf16[128,1536]{1,0:T(8,128)(2,1)S(1)}, bf16[128,1536]{1,0:T(8,128)(2,1)S(1)}, u32[]{:S(2)}, u32[]{:S(2)}) %collective-permute-start.3) | collective-permute-done | bytes 393248 | tf_op jit(solution)/shard_map/ppermute | solution.py:40
  45.1 1.4 %collective-permute-start.11 = (bf16[192,1152]{1,0:T(8,128)(2,1)}, bf16[192,1152]{1,0:T(8,128)(2,1)}, u32[]{:S(2)}, u32[]{:S(2)}) collective-permute-start(bf16[192,1152]{1,0:T(8,128)(2,1)} %collective-permute-done.7.refs_8_), channel_id=1, source_target_pairs={{0,1},{1,0},{4,5},{5,4},{8,9},{9,8},{12,13},{13,12},{16,17},{17,16... | collective-permute-start | bytes 1327112 | tf_op jit(solution)/shard_map/ppermute | solution.py:44
  47.1 5.7 %collective-permute-done.8.refs_9_ = bf16[192,1152]{1,0:T(8,128)(2,1)} collective-permute-done((bf16[192,1152]{1,0:T(8,128)(2,1)}, bf16[192,1152]{1,0:T(8,128)(2,1)}, u32[]{:S(2)}, u32[]{:S(2)}) %collective-permute-start.8) | collective-permute-done | bytes 442400 | tf_op jit(solution)/shard_map/ppermute | solution.py:54
  52.9 9.2 %project.1 = (bf16[4,256,384]{2,1,0:T(8,128)(2,1)}, bf16[2,2,256,768]{3,2,1,0:T(8,128)(2,1)}, bf16[2,256,768]{2,1,0:T(8,128)(2,1)}, bf16[256,768]{1,0:T(8,128)(2...) custom-call(s32[3]{0:T(128)} %pad_add_fusion.place, ...), custom_call_target="tpu_custom_call" | custom-call | flops 10000000 | bytes 100000 | tf_op jit(solution)/shard_map/project/pallas_call | solution.py:164
  62.1 2.2 %collective-permute-start.12 = (bf16[2,2,256,768]{3,2,1,0:T(8,128)(2,1)}, bf16[2,2,256,768]{3,2,1,0:T(8,128)(2,1)S(1)}, u32[]{:S(2)}, u32[]{:S(2)}) collective-permute-start(bf16[2,2,256,768]{3,2,1,0:T(8,128)(2,1)} %get-tuple-element.37.own), channel_id=1, source_target_pairs={{0,1},{1,0},{4,5},{5,4},{8,9},{9,8},{12,13},{13,12},{16,17},{17,16... | collective-permute-start | bytes 4718600 | tf_op jit(solution)/shard_map/ppermute | solution.py:44
  64.6 2.8 %collective-permute-start.14 = (bf16[256,768]{1,0:T(8,128)(2,1)}, bf16[256,768]{1,0:T(8,128)(2,1)S(1)}, u32[]{:S(2)}, u32[]{:S(2)}) collective-permute-start(bf16[256,768]{1,0:T(8,128)(2,1)} %get-tuple-element.43), channel_id=1, source_target_pairs={{0,224},{1,225},{4,228},{5,229},{8,232},{9,233},{12,236},{13,237},... | collective-permute-start | bytes 1179656 | tf_op jit(solution)/shard_map/ppermute | solution.py:40
  67.6 2.7 %collective-permute-start.16 = (bf16[256,768]{1,0:T(8,128)(2,1)}, bf16[256,768]{1,0:T(8,128)(2,1)S(1)}, u32[]{:S(2)}, u32[]{:S(2)}) collective-permute-start(bf16[256,768]{1,0:T(8,128)(2,1)} %get-tuple-element.47), channel_id=1, source_target_pairs={{0,224},{1,225},{4,228},{5,229},{8,232},{9,233},{12,236},{13,237},... | collective-permute-start | bytes 1179656 | tf_op jit(solution)/shard_map/ppermute | solution.py:40
  70.2 9.4 %attend_near.1 = (f32[3,2,256,128]{3,2,1,0:T(8,128)}, f32[3,2,256,128]{3,2,1,0:T(8,128)}, f32[3,2,256,256]{3,2,1,0:T(8,128)}, f32[3,2,256,256]{3,2,1,0:T(8,128)}) custom-call(bf16[4,256,384]{2,1,0:T(8,128)(2,1)} %get-tuple-element.36.q, bf16[2,2,256,768]{3,2,1,0:T(8,128)(2,1)} %get-tuple-element.37.own, bf16[2,2,256,768]{3,2,1,0:T(8,128)(2,1)} %copy-done.7), custom_call_target="tpu_custom_call" | custom-call | flops 10000000 | bytes 100000 | tf_op jit(solution)/shard_map/attend_near/pallas_call | solution.py:278
  79.6 3.3 %collective-permute-start.21 = (bf16[256,768]{1,0:T(8,128)(2,1)S(1)}, bf16[256,768]{1,0:T(8,128)(2,1)S(1)}, u32[]{:S(2)}, u32[]{:S(2)}) collective-permute-start(bf16[256,768]{1,0:T(8,128)(2,1)S(1)} %collective-permute-done.13.refs_4_), channel_id=1, source_target_pairs={{0,13},{1,4},{4,1},{5,8},{8,5},{9,12},{12,9},{13,0},{16,29},{17,20... | collective-permute-start | bytes 1179656 | tf_op jit(solution)/shard_map/ppermute | solution.py:48
  83.1 1.8 %collective-permute-done.15.refs_6_ = bf16[256,768]{1,0:T(8,128)(2,1)S(1)} collective-permute-done((bf16[256,768]{1,0:T(8,128)(2,1)}, bf16[256,768]{1,0:T(8,128)(2,1)S(1)}, u32[]{:S(2)}, u32[]{:S(2)}) %collective-permute-start.15) | collective-permute-done | bytes 393248 | tf_op jit(solution)/shard_map/ppermute | solution.py:40
  84.8 0.9 collective-permute-start.17
  86.3 2.1 %collective-permute-done.21.refs_12_ = bf16[256,768]{1,0:T(8,128)(2,1)S(1)} collective-permute-done((bf16[256,768]{1,0:T(8,128)(2,1)S(1)}, bf16[256,768]{1,0:T(8,128)(2,1)S(1)}, u32[]{:S(2)}, u32[]{:S(2)}) %collective-permute-start.21) | collective-permute-done | bytes 393248 | tf_op jit(solution)/shard_map/ppermute | solution.py:48
  89.1 3.5 %collective-permute-done.22.refs_13_ = bf16[256,768]{1,0:T(8,128)(2,1)S(1)} collective-permute-done((bf16[256,768]{1,0:T(8,128)(2,1)S(1)}, bf16[256,768]{1,0:T(8,128)(2,1)S(1)}, u32[]{:S(2)}, u32[]{:S(2)}) %collective-permute-start.22) | collective-permute-done | bytes 393248 | tf_op jit(solution)/shard_map/ppermute | solution.py:48
  93.4 8.3 %attend_far.1 = (bf16[256,384]{1,0:T(8,128)(2,1)}, bf16[256,384]{1,0:T(8,128)(2,1)}, bf16[256,384]{1,0:T(8,128)(2,1)}, bf16[256,384]{1,0:T(8,128)(2,1)}) custom-call(s32[5]{0:T(128)} %stack.45.valid, bf16[4,256,384]{2,1,0:T(8,128)(2,1)} %get-tuple-element.36.q, f32[3,2,256,128]{3,2,1,0:T(8,128)} %get-tuple-element.38.refs_0_, ...), custom_call_target="tpu_custom_call" | custom-call | flops 10000000 | bytes 100000 | tf_op jit(solution)/shard_map/attend_far/pallas_call | solution.py:291
  101.7 2.2 %collective-permute-start.24 = (bf16[256,384]{1,0:T(8,128)(2,1)}, bf16[256,384]{1,0:T(8,128)(2,1)S(1)}, u32[]{:S(2)}, u32[]{:S(2)}) collective-permute-start(bf16[256,384]{1,0:T(8,128)(2,1)} %get-tuple-element.56), channel_id=1, source_target_pairs={{0,18},{1,19},{4,22},{5,23},{8,26},{9,27},{12,30},{13,31},{16,0},{... | collective-permute-start | bytes 589832 | tf_op jit(solution)/shard_map/ppermute | solution.py:40
  103.8 1.6 %collective-permute-start.26 = (bf16[256,384]{1,0:T(8,128)(2,1)}, bf16[256,384]{1,0:T(8,128)(2,1)S(1)}, u32[]{:S(2)}, u32[]{:S(2)}) collective-permute-start(bf16[256,384]{1,0:T(8,128)(2,1)} %get-tuple-element.58), channel_id=1, source_target_pairs={{0,2},{1,3},{4,6},{5,7},{8,10},{9,11},{12,14},{13,15},{16,18},{17,... | collective-permute-start | bytes 589832 | tf_op jit(solution)/shard_map/ppermute | solution.py:40
  105.4 7.4 %collective-permute-done.24.refs_1_ = bf16[256,384]{1,0:T(8,128)(2,1)S(1)} collective-permute-done((bf16[256,384]{1,0:T(8,128)(2,1)}, bf16[256,384]{1,0:T(8,128)(2,1)S(1)}, u32[]{:S(2)}, u32[]{:S(2)}) %collective-permute-start.24) | collective-permute-done | bytes 196640 | tf_op jit(solution)/shard_map/ppermute | solution.py:40
  112.8 3.2 %collective-permute-done.25.refs_2_ = bf16[256,384]{1,0:T(8,128)(2,1)S(1)} collective-permute-done((bf16[256,384]{1,0:T(8,128)(2,1)}, bf16[256,384]{1,0:T(8,128)(2,1)S(1)}, u32[]{:S(2)}, u32[]{:S(2)}) %collective-permute-start.25) | collective-permute-done | bytes 196640 | tf_op jit(solution)/shard_map/ppermute | solution.py:40
  116.9 1.5 %side_by_side.1 = bf16[256,1536]{1,0:T(8,128)(2,1)} custom-call(s32[3]{0:T(128)S(1)} %copy-done.1, bf16[256,384]{1,0:T(8,128)(2,1)S(1)} %copy-done, bf16[256,384]{1,0:T(8,128)(2,1)S(1)} %collective-permute-done.24.refs_1_, bf16[256,384]{1,0:T(8,128)(2,1)S(1)} %collective-permute-done.25.refs_2_, bf16[256,384]{1,0:T(8,128)(2,1)S(1)} %collective-permute-done.26.refs_3_), custom_call_target="tpu_custom_call" | custom-call | tf_op jit(solution)/shard_map/side_by_side/pallas_call | solution.py:312
  (77 shorter events, 6.4 us)
Async XLA Ops:
  1.3 6.4 %collective-permute-start = (bf16[96,1152]{1,0:T(8,128)(2,1)S(1)}, bf16[96,1152]{1,0:T(8,128)(2,1)S(1)}, u32[]{:S(2)}, u32[]{:S(2)}) collective-permute-start(bf16[96,1152]{1,0:T(8,128)(2,1)S(1)} %pad_maximum_fusion.1), channel_id=1, source_target_pairs={{0,16},{1,17},{4,20},{5,21},{8,24},{9,25},{12,28},{13,29},{16,0},{... | collective-permute-start | bytes 663560 | tf_op jit(solution)/shard_map/ppermute | solution.py:60
  5.1 47.7 %copy-start.3 = (bf16[256,1536]{1,0:T(8,128)(2,1)}, bf16[256,1536]{1,0:T(8,128)(2,1)S(1)}, u32[]{:S(2)}) copy-start(bf16[256,1536]{1,0:T(8,128)(2,1)S(1)} %fusion.3.refs_0_) | copy-start | bytes 2359300
  7.7 45.1 %copy-start.4 = (bf16[192,1152]{1,0:T(8,128)(2,1)}, bf16[192,1152]{1,0:T(8,128)(2,1)S(1)}, u32[]{:S(2)}) copy-start(bf16[192,1152]{1,0:T(8,128)(2,1)S(1)} %pad_maximum_fusion.refs_5_) | copy-start | bytes 1327108
  7.7 10.9 %collective-permute-start.5 = (bf16[192,1152]{1,0:T(8,128)(2,1)S(1)}, bf16[192,1152]{1,0:T(8,128)(2,1)}, u32[]{:S(2)}, u32[]{:S(2)}) collective-permute-start(bf16[192,1152]{1,0:T(8,128)(2,1)S(1)} %pad_maximum_fusion.refs_5_), channel_id=1, source_target_pairs={{0,32},{1,225},{4,36},{5,229},{8,40},{9,233},{12,44},{13,237},{16,... | collective-permute-start | bytes 1327112 | tf_op jit(solution)/shard_map/ppermute | solution.py:54
  13.4 18.8 %collective-permute-start.1 = (bf16[256,1536]{1,0:T(8,128)(2,1)S(1)}, bf16[256,1536]{1,0:T(8,128)(2,1)S(1)}, u32[]{:S(2)}, u32[]{:S(2)}) collective-permute-start(bf16[256,1536]{1,0:T(8,128)(2,1)S(1)} %fusion.3.refs_0_), channel_id=1, source_target_pairs={{0,16},{1,17},{4,20},{5,21},{8,24},{9,25},{12,28},{13,29},{16,2},{... | collective-permute-start | bytes 2359304 | tf_op jit(solution)/shard_map/ppermute | solution.py:40
  14.7 17.9 %collective-permute-start.2 = (bf16[256,1536]{1,0:T(8,128)(2,1)S(1)}, bf16[256,1536]{1,0:T(8,128)(2,1)S(1)}, u32[]{:S(2)}, u32[]{:S(2)}) collective-permute-start(bf16[256,1536]{1,0:T(8,128)(2,1)S(1)} %fusion.3.refs_0_), channel_id=1, source_target_pairs={{0,18},{1,19},{4,22},{5,23},{8,26},{9,27},{12,30},{13,31},{16,0},{... | collective-permute-start | bytes 2359304 | tf_op jit(solution)/shard_map/ppermute | solution.py:40
  18.6 13.9 %collective-permute-start.6 = (bf16[192,1152]{1,0:T(8,128)(2,1)}, bf16[192,1152]{1,0:T(8,128)(2,1)}, u32[]{:S(2)}, u32[]{:S(2)}) collective-permute-start(bf16[192,1152]{1,0:T(8,128)(2,1)} %collective-permute-done.5.refs_6_), channel_id=1, source_target_pairs={{0,32},{1,225},{4,36},{5,229},{8,40},{9,233},{12,44},{13,237},{16,... | collective-permute-start | bytes 1327112 | tf_op jit(solution)/shard_map/ppermute | solution.py:54
  32.2 20.6 %copy-start.5 = (bf16[256,1536]{1,0:T(8,128)(2,1)}, bf16[256,1536]{1,0:T(8,128)(2,1)S(1)}, u32[]{:S(2)}) copy-start(bf16[256,1536]{1,0:T(8,128)(2,1)S(1)} %collective-permute-done.1.refs_1_) | copy-start | bytes 2359300
  32.6 20.3 %copy-start.6 = (bf16[256,1536]{1,0:T(8,128)(2,1)}, bf16[256,1536]{1,0:T(8,128)(2,1)S(1)}, u32[]{:S(2)}) copy-start(bf16[256,1536]{1,0:T(8,128)(2,1)S(1)} %collective-permute-done.2.refs_2_) | copy-start | bytes 2359300
  32.6 12.5 %collective-permute-start.7 = (bf16[192,1152]{1,0:T(8,128)(2,1)}, bf16[192,1152]{1,0:T(8,128)(2,1)}, u32[]{:S(2)}, u32[]{:S(2)}) collective-permute-start(bf16[192,1152]{1,0:T(8,128)(2,1)} %collective-permute-done.6.refs_7_), channel_id=1, source_target_pairs={{0,32},{1,225},{4,36},{5,229},{8,40},{9,233},{12,44},{13,237},{16,... | collective-permute-start | bytes 1327112 | tf_op jit(solution)/shard_map/ppermute | solution.py:54
  33.7 10.8 %collective-permute-start.3 = (bf16[128,1536]{1,0:T(8,128)(2,1)S(1)}, bf16[128,1536]{1,0:T(8,128)(2,1)S(1)}, u32[]{:S(2)}, u32[]{:S(2)}) collective-permute-start(bf16[128,1536]{1,0:T(8,128)(2,1)S(1)} %slice.8), channel_id=1, source_target_pairs={{0,16},{1,17},{4,20},{5,21},{8,24},{9,25},{12,28},{13,29},{16,2},{... | collective-permute-start | bytes 1179656 | tf_op jit(solution)/shard_map/ppermute | solution.py:40
  34.7 10.4 %collective-permute-start.4 = (bf16[128,1536]{1,0:T(8,128)(2,1)S(1)}, bf16[128,1536]{1,0:T(8,128)(2,1)}, u32[]{:S(2)}, u32[]{:S(2)}) collective-permute-start(bf16[128,1536]{1,0:T(8,128)(2,1)S(1)} %slice.9), channel_id=1, source_target_pairs={{0,18},{1,19},{4,22},{5,23},{8,26},{9,27},{12,30},{13,31},{16,0},{... | collective-permute-start | bytes 1179656 | tf_op jit(solution)/shard_map/ppermute | solution.py:40
  36.6 10.5 %collective-permute-start.9 = (bf16[192,1152]{1,0:T(8,128)(2,1)}, bf16[192,1152]{1,0:T(8,128)(2,1)}, u32[]{:S(2)}, u32[]{:S(2)}) collective-permute-start(bf16[192,1152]{1,0:T(8,128)(2,1)} %collective-permute-done.5.refs_6_), channel_id=1, source_target_pairs={{0,1},{1,0},{4,5},{5,4},{8,9},{9,8},{12,13},{13,12},{16,17},{17,16... | collective-permute-start | bytes 1327112 | tf_op jit(solution)/shard_map/ppermute | solution.py:44
  36.6 10.5 %collective-permute-start.10 = (bf16[192,1152]{1,0:T(8,128)(2,1)}, bf16[192,1152]{1,0:T(8,128)(2,1)}, u32[]{:S(2)}, u32[]{:S(2)}) collective-permute-start(bf16[192,1152]{1,0:T(8,128)(2,1)} %collective-permute-done.6.refs_7_), channel_id=1, source_target_pairs={{0,1},{1,0},{4,5},{5,4},{8,9},{9,8},{12,13},{13,12},{16,17},{17,16... | collective-permute-start | bytes 1327112 | tf_op jit(solution)/shard_map/ppermute | solution.py:44
  45.1 7.8 %collective-permute-start.8 = (bf16[192,1152]{1,0:T(8,128)(2,1)}, bf16[192,1152]{1,0:T(8,128)(2,1)}, u32[]{:S(2)}, u32[]{:S(2)}) collective-permute-start(bf16[192,1152]{1,0:T(8,128)(2,1)} %collective-permute-done.7.refs_8_), channel_id=1, source_target_pairs={{0,32},{1,225},{4,36},{5,229},{8,40},{9,233},{12,44},{13,237},{16,... | collective-permute-start | bytes 1327112 | tf_op jit(solution)/shard_map/ppermute | solution.py:54
  45.1 7.8 %collective-permute-start.11 = (bf16[192,1152]{1,0:T(8,128)(2,1)}, bf16[192,1152]{1,0:T(8,128)(2,1)}, u32[]{:S(2)}, u32[]{:S(2)}) collective-permute-start(bf16[192,1152]{1,0:T(8,128)(2,1)} %collective-permute-done.7.refs_8_), channel_id=1, source_target_pairs={{0,1},{1,0},{4,5},{5,4},{8,9},{9,8},{12,13},{13,12},{16,17},{17,16... | collective-permute-start | bytes 1327112 | tf_op jit(solution)/shard_map/ppermute | solution.py:44
  62.1 5.5 %collective-permute-start.12 = (bf16[2,2,256,768]{3,2,1,0:T(8,128)(2,1)}, bf16[2,2,256,768]{3,2,1,0:T(8,128)(2,1)S(1)}, u32[]{:S(2)}, u32[]{:S(2)}) collective-permute-start(bf16[2,2,256,768]{3,2,1,0:T(8,128)(2,1)} %get-tuple-element.37.own), channel_id=1, source_target_pairs={{0,1},{1,0},{4,5},{5,4},{8,9},{9,8},{12,13},{13,12},{16,17},{17,16... | collective-permute-start | bytes 4718600 | tf_op jit(solution)/shard_map/ppermute | solution.py:44
  64.3 15.3 %collective-permute-start.13 = (bf16[256,768]{1,0:T(8,128)(2,1)}, bf16[256,768]{1,0:T(8,128)(2,1)S(1)}, u32[]{:S(2)}, u32[]{:S(2)}) collective-permute-start(bf16[256,768]{1,0:T(8,128)(2,1)} %get-tuple-element.42), channel_id=1, source_target_pairs={{0,32},{1,33},{4,36},{5,37},{8,40},{9,41},{12,44},{13,45},{16,48},... | collective-permute-start | bytes 1179656 | tf_op jit(solution)/shard_map/ppermute | solution.py:40
  64.3 21.8 %collective-permute-start.23 = (bf16[2,256,768]{2,1,0:T(8,128)(2,1)}, bf16[2,256,768]{2,1,0:T(8,128)(2,1)S(1)}, u32[]{:S(2)}, u32[]{:S(2)}) collective-permute-start(bf16[2,256,768]{2,1,0:T(8,128)(2,1)} %get-tuple-element.54), channel_id=1, source_target_pairs={{0,13},{1,4},{4,1},{5,8},{8,5},{9,12},{12,9},{13,0},{16,29},{17,20... | collective-permute-start | bytes 2359304 | tf_op jit(solution)/shard_map/ppermute | solution.py:48
  64.6 18.3 %collective-permute-start.14 = (bf16[256,768]{1,0:T(8,128)(2,1)}, bf16[256,768]{1,0:T(8,128)(2,1)S(1)}, u32[]{:S(2)}, u32[]{:S(2)}) collective-permute-start(bf16[256,768]{1,0:T(8,128)(2,1)} %get-tuple-element.43), channel_id=1, source_target_pairs={{0,224},{1,225},{4,228},{5,229},{8,232},{9,233},{12,236},{13,237},... | collective-permute-start | bytes 1179656 | tf_op jit(solution)/shard_map/ppermute | solution.py:40
  67.6 17.3 %collective-permute-start.15 = (bf16[256,768]{1,0:T(8,128)(2,1)}, bf16[256,768]{1,0:T(8,128)(2,1)S(1)}, u32[]{:S(2)}, u32[]{:S(2)}) collective-permute-start(bf16[256,768]{1,0:T(8,128)(2,1)} %get-tuple-element.45), channel_id=1, source_target_pairs={{0,32},{1,33},{4,36},{5,37},{8,40},{9,41},{12,44},{13,45},{16,48},... | collective-permute-start | bytes 1179656 | tf_op jit(solution)/shard_map/ppermute | solution.py:40
  67.6 17.3 %collective-permute-start.16 = (bf16[256,768]{1,0:T(8,128)(2,1)}, bf16[256,768]{1,0:T(8,128)(2,1)S(1)}, u32[]{:S(2)}, u32[]{:S(2)}) collective-permute-start(bf16[256,768]{1,0:T(8,128)(2,1)} %get-tuple-element.47), channel_id=1, source_target_pairs={{0,224},{1,225},{4,228},{5,229},{8,232},{9,233},{12,236},{13,237},... | collective-permute-start | bytes 1179656 | tf_op jit(solution)/shard_map/ppermute | solution.py:40
  79.6 8.8 %collective-permute-start.21 = (bf16[256,768]{1,0:T(8,128)(2,1)S(1)}, bf16[256,768]{1,0:T(8,128)(2,1)S(1)}, u32[]{:S(2)}, u32[]{:S(2)}) collective-permute-start(bf16[256,768]{1,0:T(8,128)(2,1)S(1)} %collective-permute-done.13.refs_4_), channel_id=1, source_target_pairs={{0,13},{1,4},{4,1},{5,8},{8,5},{9,12},{12,9},{13,0},{16,29},{17,20... | collective-permute-start | bytes 1179656 | tf_op jit(solution)/shard_map/ppermute | solution.py:48
  83.0 9.7 %collective-permute-start.22 = (bf16[256,768]{1,0:T(8,128)(2,1)S(1)}, bf16[256,768]{1,0:T(8,128)(2,1)S(1)}, u32[]{:S(2)}, u32[]{:S(2)}) collective-permute-start(bf16[256,768]{1,0:T(8,128)(2,1)S(1)} %collective-permute-done.14.refs_5_), channel_id=1, source_target_pairs={{0,13},{1,4},{4,1},{5,8},{8,5},{9,12},{12,9},{13,0},{16,29},{17,20... | collective-permute-start | bytes 1179656 | tf_op jit(solution)/shard_map/ppermute | solution.py:48
  84.8 7.8 %collective-permute-start.17 = (bf16[256,768]{1,0:T(8,128)(2,1)S(1)}, bf16[256,768]{1,0:T(8,128)(2,1)}, u32[]{:S(2)}, u32[]{:S(2)}) collective-permute-start(bf16[256,768]{1,0:T(8,128)(2,1)S(1)} %collective-permute-done.13.refs_4_), channel_id=1, source_target_pairs={{0,1},{1,0},{4,5},{5,4},{8,9},{9,8},{12,13},{13,12},{16,17},{17,16... | collective-permute-start | bytes 1179656 | tf_op jit(solution)/shard_map/ppermute | solution.py:44
  85.8 6.8 %collective-permute-start.18 = (bf16[256,768]{1,0:T(8,128)(2,1)S(1)}, bf16[256,768]{1,0:T(8,128)(2,1)}, u32[]{:S(2)}, u32[]{:S(2)}) collective-permute-start(bf16[256,768]{1,0:T(8,128)(2,1)S(1)} %collective-permute-done.14.refs_5_), channel_id=1, source_target_pairs={{0,1},{1,0},{4,5},{5,4},{8,9},{9,8},{12,13},{13,12},{16,17},{17,16... | collective-permute-start | bytes 1179656 | tf_op jit(solution)/shard_map/ppermute | solution.py:44
  86.1 6.5 %collective-permute-start.19 = (bf16[256,768]{1,0:T(8,128)(2,1)S(1)}, bf16[256,768]{1,0:T(8,128)(2,1)}, u32[]{:S(2)}, u32[]{:S(2)}) collective-permute-start(bf16[256,768]{1,0:T(8,128)(2,1)S(1)} %collective-permute-done.15.refs_6_), channel_id=1, source_target_pairs={{0,1},{1,0},{4,5},{5,4},{8,9},{9,8},{12,13},{13,12},{16,17},{17,16... | collective-permute-start | bytes 1179656 | tf_op jit(solution)/shard_map/ppermute | solution.py:44
  88.4 4.2 %collective-permute-start.20 = (bf16[256,768]{1,0:T(8,128)(2,1)S(1)}, bf16[256,768]{1,0:T(8,128)(2,1)}, u32[]{:S(2)}, u32[]{:S(2)}) collective-permute-start(bf16[256,768]{1,0:T(8,128)(2,1)S(1)} %collective-permute-done.16.refs_7_), channel_id=1, source_target_pairs={{0,1},{1,0},{4,5},{5,4},{8,9},{9,8},{12,13},{13,12},{16,17},{17,16... | collective-permute-start | bytes 1179656 | tf_op jit(solution)/shard_map/ppermute | solution.py:44
  93.4 22.6 %copy-start.1 = (s32[3]{0:T(128)S(1)}, s32[3]{0:T(128)}, u32[]{:S(2)}) copy-start(s32[3]{0:T(128)} %pad_add_fusion.place) | copy-start | bytes 40
  101.7 11.1 %collective-permute-start.24 = (bf16[256,384]{1,0:T(8,128)(2,1)}, bf16[256,384]{1,0:T(8,128)(2,1)S(1)}, u32[]{:S(2)}, u32[]{:S(2)}) collective-permute-start(bf16[256,384]{1,0:T(8,128)(2,1)} %get-tuple-element.56), channel_id=1, source_target_pairs={{0,18},{1,19},{4,22},{5,23},{8,26},{9,27},{12,30},{13,31},{16,0},{... | collective-permute-start | bytes 589832 | tf_op jit(solution)/shard_map/ppermute | solution.py:40
  103.8 12.2 %collective-permute-start.25 = (bf16[256,384]{1,0:T(8,128)(2,1)}, bf16[256,384]{1,0:T(8,128)(2,1)S(1)}, u32[]{:S(2)}, u32[]{:S(2)}) collective-permute-start(bf16[256,384]{1,0:T(8,128)(2,1)} %get-tuple-element.57), channel_id=1, source_target_pairs={{0,16},{1,17},{4,20},{5,21},{8,24},{9,25},{12,28},{13,29},{16,2},{... | collective-permute-start | bytes 589832 | tf_op jit(solution)/shard_map/ppermute | solution.py:40
  103.8 12.2 %collective-permute-start.26 = (bf16[256,384]{1,0:T(8,128)(2,1)}, bf16[256,384]{1,0:T(8,128)(2,1)S(1)}, u32[]{:S(2)}, u32[]{:S(2)}) collective-permute-start(bf16[256,384]{1,0:T(8,128)(2,1)} %get-tuple-element.58), channel_id=1, source_target_pairs={{0,2},{1,3},{4,6},{5,7},{8,10},{9,11},{12,14},{13,15},{16,18},{17,... | collective-permute-start | bytes 589832 | tf_op jit(solution)/shard_map/ppermute | solution.py:40
  (13 other events, 73.2 us)

commit v4 on v3

--- a/solution.py
+++ b/solution.py
@@ -262,13 +262,13 @@
 
 def head_spec(array, width):
     lead = array.ndim - 1
-    return pl.BlockSpec(array.shape[:-1] + (width,), lambda h: (0,) * lead + (h,))
+    return pl.BlockSpec(array.shape[:-1] + (width,), lambda h, *_: (0,) * lead + (h,))
 
 
 PEAK, TOTAL = (
     (
         jax.ShapeDtypeStruct((GROUP_HEADS, 2, TOKENS, width), F32),
-        pl.BlockSpec((1, 2, TOKENS, width), lambda h: (h, 0, 0, 0)),
+        pl.BlockSpec((1, 2, TOKENS, width), lambda h, *_: (h, 0, 0, 0)),
     )
     for width in (HD, 2 * HD)
 )
@@ -288,35 +288,51 @@
 
 
 def attend_far(valid, q, peaks, totals, *kv):
+    part = jax.ShapeDtypeStruct((TOKENS, GROUP), BF16)
+    part_spec = pl.BlockSpec((TOKENS, HD), lambda h, info: (0, h))
     return pl.pallas_call(
         far_kernel,
         name="attend_far",
-        grid=(GROUP_HEADS,),
-        out_shape=(jax.ShapeDtypeStruct((TOKENS, GROUP), BF16),) * 4,
-        in_specs=[SMEM, head_spec(q, HD), PEAK[1], PEAK[1], TOTAL[1], TOTAL[1]]
-        + [head_spec(a, 2 * HD) for a in kv],
-        out_specs=[pl.BlockSpec((TOKENS, HD), lambda h: (0, h))] * 4,
-        scratch_shapes=[pltpu.VMEM((4, TOKENS, HD), BF16)],
+        grid_spec=pltpu.PrefetchScalarGridSpec(
+            num_scalar_prefetch=1,
+            grid=(GROUP_HEADS,),
+            in_specs=[head_spec(q, HD), PEAK[1], PEAK[1], TOTAL[1], TOTAL[1]]
+            + [head_spec(a, 2 * HD) for a in kv],
+            out_specs=[pl.BlockSpec((TOKENS, HD), lambda h, info: (0, info[4] * GROUP_HEADS + h))]
+            + [part_spec] * 3,
+            scratch_shapes=[pltpu.VMEM((4, TOKENS, HD), BF16)],
+        ),
+        out_shape=(jax.ShapeDtypeStruct((TOKENS, D), BF16), part, part, part),
         compiler_params=FAR,
         cost_estimate=LIGHT,
     )(valid, q, *peaks, *totals, *kv)
 
 
 def side_kernel(place, *refs):
-    for part, step in zip(refs[:4], STEPS, strict=True):
+    parts, out, sems = refs[:3], refs[4], refs[5]
+    copies = []
+    for n, (part, step) in enumerate(zip(parts, STEPS[1:], strict=True)):
         start = lax.rem(place[0] + step + 4, 4) * GROUP
-        refs[4][:, pl.ds(pl.multiple_of(start, HD), GROUP)] = part[...]
-
-
-def side_by_side(place, parts, shape):
+        where = out.at[:, pl.ds(pl.multiple_of(start, HD), GROUP)]
+        copies.append(pltpu.make_async_copy(part, where, sems.at[n]))
+    for copy in copies:
+        copy.start()
+    for copy in copies:
+        copy.wait()
+
+
+def side_by_side(place, whole, parts, shape):
     return pl.pallas_call(
         side_kernel,
         name="side_by_side",
         out_shape=jax.ShapeDtypeStruct((TOKENS, D), BF16),
-        in_specs=[SMEM] + [VMEM] * 4,
-        out_specs=VMEM,
+        in_specs=[SMEM] + [VMEM] * 3 + [ANY],
+        out_specs=ANY,
+        scratch_shapes=[pltpu.SemaphoreType.DMA((3,))],
+        input_output_aliases={4: 0},
         compiler_params=SIDE,
-    )(place, *parts).reshape(shape)
+        cost_estimate=LIGHT,
+    )(place, *parts, whole).reshape(shape)
 
 
 def per_device(hidden, projection, adaptive_shift, adaptive_scale, query_gain, key_gain):
@@ -373,8 +389,8 @@
         corner_above,
         edge,
     )
-    back = [attended[0]] + [shift(tile, dy=-step) for step, tile in zip(STEPS[1:], attended[1:], strict=True)]
-    return side_by_side(place, back, hidden.shape)
+    back = [shift(tile, dy=-step) for step, tile in zip(STEPS[1:], attended[1:], strict=True)]
+    return side_by_side(place, attended[0], back, hidden.shape)
 
 
 def solution(mesh):

time: 119 us -> 118 us (level)
  starting transfers between devices: 35.7 us -> 34.3 us
    ppermute x11, starting transfers between devices: 14.8 us -> 12.2 us  [shift(): lax.ppermute(array, AXES, pairs(lambda z, y, x, core: (z + dz, y + dy, x,...]
    ppermute x3, waiting for transfers between devices: 5.65 us -> 3.85 us  [outward(): lax.ppermute(array, AXES, pairs(lambda z, y, x, core: (z + dz, y, x + (1...]
    ppermute x11, waiting for transfers between devices: 30.9 us -> 32.4 us  [shift(): lax.ppermute(array, AXES, pairs(lambda z, y, x, core: (z + dz, y + dy, x,...]
    ppermute x4, starting transfers between devices: 10.2 us -> 11.7 us  [ring_step(): lax.ppermute(array, AXES, pairs(lambda z, y, x, core: (z + (-1 if core el...]
    ppermute x8, waiting for transfers between devices: 0.13 us -> 1.34 us  [swap_cores(): lax.ppermute(array, AXES, pairs(lambda z, y, x, core: (z, y, x, 1 - core)))]
  transfers between devices with their start and end apart: 27 -> 27, of which waited for: 13 -> 14; matrix products, arithmetic and copies ran while one was open for 3% -> 3% of each run, Pallas kernels for 8% -> 8%
where the time goes in v4:
time: 118 us
  waiting for transfers between devices  48.3 us (41%)
  starting transfers between devices  34.3 us (29%)
  Pallas kernels  29 us (25%)
  other arithmetic  2.93 us (2%)
  local copies, waits for them, and re-layouts  2.8 us (2%)
    ppermute x11, waiting for transfers between devices, shift(): lax.ppermute(array, AXES, pairs(lambda z, y, x, core: (z + dz, y + dy, x,...  32.4 us
    ppermute x11, starting transfers between devices, shift(): lax.ppermute(array, AXES, pairs(lambda z, y, x, core: (z + dz, y + dy, x,...  12.2 us
    ppermute x4, starting transfers between devices, ring_step(): lax.ppermute(array, AXES, pairs(lambda z, y, x, core: (z + (-1 if core el...  11.7 us
    pallas_call x1, Pallas kernels, attend_near(): pl.pallas_call(near_kernel, name='attend_near', grid=(GROUP_HEADS,), out_...  9.38 us
    pallas_call x1, Pallas kernels, project(): pl.pallas_call(project_kernel, name='project', out_shape=(jax.ShapeDtypeS...  9.2 us
    pallas_call x1, Pallas kernels, attend_far(): pl.pallas_call(far_kernel, name='attend_far', grid_spec=pltpu.PrefetchSca...  9.02 us
    ppermute x4, waiting for transfers between devices, ring_step(): lax.ppermute(array, AXES, pairs(lambda z, y, x, core: (z + (-1 if core el...  8.11 us
    ppermute x8, starting transfers between devices, swap_cores(): lax.ppermute(array, AXES, pairs(lambda z, y, x, core: (z, y, x, 1 - core)))  5.33 us
  transfers between devices with their start and end apart: 27, of which 14 were waited for; matrix products, arithmetic and copies ran while one was open for 3% of the time, Pallas kernels for 8%

profile of v4, /device:TPU:7, one launch (start us, length us, event | category | flops | bytes accessed | tf_op | source)
XLA Modules:
  0.0 117.7 jit_solution(16469421059904377874)
XLA Ops:
  0.0 1.2 %constant_dynamic-slice_fusion.2 = (bf16[96,384]{1,0:T(8,128)(2,1)S(1)}, bf16[96,384]{1,0:T(8,128)(2,1)S(1)}, bf16[96,384]{1,0:T(8,128)(2,1)S(1)}, bf16[96,384]{...) fusion(bf16[96,4608]{1,0:T(8,128)(2,1)} %param.7, s32[]{:T(128)S(6)} %select_n.26, ...), kind=kLoop, calls=%fused_computation.13 | loop fusion | bytes 884760 | tf_op jit(solution)/shard_map/dynamic_slice | solution.py:344
  1.3 1.4 %collective-permute-start = (bf16[96,1152]{1,0:T(8,128)(2,1)S(1)}, bf16[96,1152]{1,0:T(8,128)(2,1)S(1)}, u32[]{:S(2)}, u32[]{:S(2)}) collective-permute-start(bf16[96,1152]{1,0:T(8,128)(2,1)S(1)} %pad_maximum_fusion.1), channel_id=1, source_target_pairs={{0,16},{1,17},{4,20},{5,21},{8,24},{9,25},{12,28},{13,29},{16,0},{... | collective-permute-start | bytes 663560 | tf_op jit(solution)/shard_map/ppermute | solution.py:60
  2.7 1.6 %reduce_sum.18 = f32[4,4,16]{2,1,0:T(4,128)S(1)} reduce(f32[4,4,16,1536]{3,2,1,0:T(8,128)} %param.6, f32[]{:T(128)} %constant.44.clone.1), dimensions={3}, to_apply=%region_0.0 | reduce | flops 392960 | bytes 1573892 | tf_op jit(solution)/shard_map/reduce_sum | solution.py:70
  5.1 2.5 %collective-permute-done = bf16[96,1152]{1,0:T(8,128)(2,1)S(1)} collective-permute-done((bf16[96,1152]{1,0:T(8,128)(2,1)S(1)}, bf16[96,1152]{1,0:T(8,128)(2,1)S(1)}, u32[]{:S(2)}, u32[]{:S(2)}) %collective-permute-start) | collective-permute-done | bytes 221216 | tf_op jit(solution)/shard_map/ppermute | solution.py:60
  7.7 5.7 %collective-permute-start.5 = (bf16[192,1152]{1,0:T(8,128)(2,1)S(1)}, bf16[192,1152]{1,0:T(8,128)(2,1)}, u32[]{:S(2)}, u32[]{:S(2)}) collective-permute-start(bf16[192,1152]{1,0:T(8,128)(2,1)S(1)} %pad_maximum_fusion.refs_5_), channel_id=1, source_target_pairs={{0,32},{1,225},{4,36},{5,229},{8,40},{9,233},{12,44},{13,237},{16,... | collective-permute-start | bytes 1327112 | tf_op jit(solution)/shard_map/ppermute | solution.py:54
  13.4 1.3 %collective-permute-start.1 = (bf16[256,1536]{1,0:T(8,128)(2,1)S(1)}, bf16[256,1536]{1,0:T(8,128)(2,1)S(1)}, u32[]{:S(2)}, u32[]{:S(2)}) collective-permute-start(bf16[256,1536]{1,0:T(8,128)(2,1)S(1)} %fusion.3.refs_0_), channel_id=1, source_target_pairs={{0,16},{1,17},{4,20},{5,21},{8,24},{9,25},{12,28},{13,29},{16,2},{... | collective-permute-start | bytes 2359304 | tf_op jit(solution)/shard_map/ppermute | solution.py:40
  14.7 1.4 %collective-permute-start.2 = (bf16[256,1536]{1,0:T(8,128)(2,1)S(1)}, bf16[256,1536]{1,0:T(8,128)(2,1)S(1)}, u32[]{:S(2)}, u32[]{:S(2)}) collective-permute-start(bf16[256,1536]{1,0:T(8,128)(2,1)S(1)} %fusion.3.refs_0_), channel_id=1, source_target_pairs={{0,18},{1,19},{4,22},{5,23},{8,26},{9,27},{12,30},{13,31},{16,0},{... | collective-permute-start | bytes 2359304 | tf_op jit(solution)/shard_map/ppermute | solution.py:40
  16.1 2.5 %collective-permute-done.5.refs_6_ = bf16[192,1152]{1,0:T(8,128)(2,1)} collective-permute-done((bf16[192,1152]{1,0:T(8,128)(2,1)S(1)}, bf16[192,1152]{1,0:T(8,128)(2,1)}, u32[]{:S(2)}, u32[]{:S(2)}) %collective-permute-start.5) | collective-permute-done | bytes 442400 | tf_op jit(solution)/shard_map/ppermute | solution.py:54
  18.6 3.4 %collective-permute-start.6 = (bf16[192,1152]{1,0:T(8,128)(2,1)}, bf16[192,1152]{1,0:T(8,128)(2,1)}, u32[]{:S(2)}, u32[]{:S(2)}) collective-permute-start(bf16[192,1152]{1,0:T(8,128)(2,1)} %collective-permute-done.5.refs_6_), channel_id=1, source_target_pairs={{0,32},{1,225},{4,36},{5,229},{8,40},{9,233},{12,44},{13,237},{16,... | collective-permute-start | bytes 1327112 | tf_op jit(solution)/shard_map/ppermute | solution.py:54
  22.0 10.2 %collective-permute-done.1.refs_1_ = bf16[256,1536]{1,0:T(8,128)(2,1)S(1)} collective-permute-done((bf16[256,1536]{1,0:T(8,128)(2,1)S(1)}, bf16[256,1536]{1,0:T(8,128)(2,1)S(1)}, u32[]{:S(2)}, u32[]{:S(2)}) %collective-permute-start.1) | collective-permute-done | bytes 786464 | tf_op jit(solution)/shard_map/ppermute | solution.py:40
  32.6 1.1 collective-permute-start.7
  33.7 0.9 collective-permute-start.3
  34.7 1.9 %collective-permute-start.4 = (bf16[128,1536]{1,0:T(8,128)(2,1)S(1)}, bf16[128,1536]{1,0:T(8,128)(2,1)}, u32[]{:S(2)}, u32[]{:S(2)}) collective-permute-start(bf16[128,1536]{1,0:T(8,128)(2,1)S(1)} %slice.9), channel_id=1, source_target_pairs={{0,18},{1,19},{4,22},{5,23},{8,26},{9,27},{12,30},{13,31},{16,0},{... | collective-permute-start | bytes 1179656 | tf_op jit(solution)/shard_map/ppermute | solution.py:40
  37.1 7.4 %collective-permute-done.3.refs_3_ = bf16[128,1536]{1,0:T(8,128)(2,1)S(1)} collective-permute-done((bf16[128,1536]{1,0:T(8,128)(2,1)S(1)}, bf16[128,1536]{1,0:T(8,128)(2,1)S(1)}, u32[]{:S(2)}, u32[]{:S(2)}) %collective-permute-start.3) | collective-permute-done | bytes 393248 | tf_op jit(solution)/shard_map/ppermute | solution.py:40
  45.1 1.5 %collective-permute-start.8 = (bf16[192,1152]{1,0:T(8,128)(2,1)}, bf16[192,1152]{1,0:T(8,128)(2,1)}, u32[]{:S(2)}, u32[]{:S(2)}) collective-permute-start(bf16[192,1152]{1,0:T(8,128)(2,1)} %collective-permute-done.7.refs_8_), channel_id=1, source_target_pairs={{0,32},{1,225},{4,36},{5,229},{8,40},{9,233},{12,44},{13,237},{16,... | collective-permute-start | bytes 1327112 | tf_op jit(solution)/shard_map/ppermute | solution.py:54
  47.3 5.6 %collective-permute-done.8.refs_9_ = bf16[192,1152]{1,0:T(8,128)(2,1)} collective-permute-done((bf16[192,1152]{1,0:T(8,128)(2,1)}, bf16[192,1152]{1,0:T(8,128)(2,1)}, u32[]{:S(2)}, u32[]{:S(2)}) %collective-permute-start.8) | collective-permute-done | bytes 442400 | tf_op jit(solution)/shard_map/ppermute | solution.py:54
  52.9 9.2 %project.1 = (bf16[4,256,384]{2,1,0:T(8,128)(2,1)}, bf16[2,2,256,768]{3,2,1,0:T(8,128)(2,1)}, bf16[2,256,768]{2,1,0:T(8,128)(2,1)}, bf16[256,768]{1,0:T(8,128)(2...) custom-call(s32[3]{0:T(128)} %pad_add_fusion.place, ...), custom_call_target="tpu_custom_call" | custom-call | flops 10000000 | bytes 100000 | tf_op jit(solution)/shard_map/project/pallas_call | solution.py:164
  62.1 2.6 %collective-permute-start.12 = (bf16[2,2,256,768]{3,2,1,0:T(8,128)(2,1)}, bf16[2,2,256,768]{3,2,1,0:T(8,128)(2,1)S(1)}, u32[]{:S(2)}, u32[]{:S(2)}) collective-permute-start(bf16[2,2,256,768]{3,2,1,0:T(8,128)(2,1)} %get-tuple-element.37.own), channel_id=1, source_target_pairs={{0,1},{1,0},{4,5},{5,4},{8,9},{9,8},{12,13},{13,12},{16,17},{17,16... | collective-permute-start | bytes 4718600 | tf_op jit(solution)/shard_map/ppermute | solution.py:44
  65.5 1.1 collective-permute-start.13
  66.6 1.3 %collective-permute-done.12.mate = bf16[2,2,256,768]{3,2,1,0:T(8,128)(2,1)S(1)} collective-permute-done((bf16[2,2,256,768]{3,2,1,0:T(8,128)(2,1)}, bf16[2,2,256,768]{3,2,1,0:T(8,128)(2,1)S(1)}, u32[]{:S(2)}, u32[]{:S(2)}) %collective-permute-start.12) | collective-permute-done | bytes 1572896 | tf_op jit(solution)/shard_map/ppermute | solution.py:44
  68.3 1.2 collective-permute-start.15
  69.4 9.4 %attend_near.1 = (f32[3,2,256,128]{3,2,1,0:T(8,128)}, f32[3,2,256,128]{3,2,1,0:T(8,128)}, f32[3,2,256,256]{3,2,1,0:T(8,128)}, f32[3,2,256,256]{3,2,1,0:T(8,128)}) custom-call(bf16[4,256,384]{2,1,0:T(8,128)(2,1)} %get-tuple-element.36.q, bf16[2,2,256,768]{3,2,1,0:T(8,128)(2,1)} %get-tuple-element.37.own, bf16[2,2,256,768]{3,2,1,0:T(8,128)(2,1)} %copy-done.6), custom_call_target="tpu_custom_call" | custom-call | flops 10000000 | bytes 100000 | tf_op jit(solution)/shard_map/attend_near/pallas_call | solution.py:278
  78.8 2.1 %collective-permute-start.22 = (bf16[256,768]{1,0:T(8,128)(2,1)S(1)}, bf16[256,768]{1,0:T(8,128)(2,1)S(1)}, u32[]{:S(2)}, u32[]{:S(2)}) collective-permute-start(bf16[256,768]{1,0:T(8,128)(2,1)S(1)} %collective-permute-done.14.refs_5_), channel_id=1, source_target_pairs={{0,13},{1,4},{4,1},{5,8},{8,5},{9,12},{12,9},{13,0},{16,29},{17,20... | collective-permute-start | bytes 1179656 | tf_op jit(solution)/shard_map/ppermute | solution.py:48
  81.9 2.2 %collective-permute-done.16.refs_7_ = bf16[256,768]{1,0:T(8,128)(2,1)S(1)} collective-permute-done((bf16[256,768]{1,0:T(8,128)(2,1)}, bf16[256,768]{1,0:T(8,128)(2,1)S(1)}, u32[]{:S(2)}, u32[]{:S(2)}) %collective-permute-start.16) | collective-permute-done | bytes 393248 | tf_op jit(solution)/shard_map/ppermute | solution.py:40
  85.8 1.1 collective-permute-start.19
  88.0 3.5 %collective-permute-done.21.refs_12_ = bf16[256,768]{1,0:T(8,128)(2,1)S(1)} collective-permute-done((bf16[256,768]{1,0:T(8,128)(2,1)S(1)}, bf16[256,768]{1,0:T(8,128)(2,1)S(1)}, u32[]{:S(2)}, u32[]{:S(2)}) %collective-permute-start.21) | collective-permute-done | bytes 393248 | tf_op jit(solution)/shard_map/ppermute | solution.py:48
  92.3 9.0 %attend_far.1 = (bf16[256,1536]{1,0:T(8,128)(2,1)}, bf16[256,384]{1,0:T(8,128)(2,1)}, bf16[256,384]{1,0:T(8,128)(2,1)}, bf16[256,384]{1,0:T(8,128)(2,1)}) custom-call(s32[5]{0:T(128)} %stack.45.valid, bf16[4,256,384]{2,1,0:T(8,128)(2,1)} %get-tuple-element.36.q, f32[3,2,256,128]{3,2,1,0:T(8,128)} %get-tuple-element.38.refs_0_, ...), custom_call_target="tpu_custom_call" | custom-call | flops 10000000 | bytes 100000 | tf_op jit(solution)/shard_map/attend_far/pallas_call | solution.py:293
  101.3 2.7 %collective-permute-start.24 = (bf16[256,384]{1,0:T(8,128)(2,1)}, bf16[256,384]{1,0:T(8,128)(2,1)S(1)}, u32[]{:S(2)}, u32[]{:S(2)}) collective-permute-start(bf16[256,384]{1,0:T(8,128)(2,1)} %get-tuple-element.55), channel_id=1, source_target_pairs={{0,18},{1,19},{4,22},{5,23},{8,26},{9,27},{12,30},{13,31},{16,0},{... | collective-permute-start | bytes 589832 | tf_op jit(solution)/shard_map/ppermute | solution.py:40
  104.0 1.3 %collective-permute-start.26 = (bf16[256,384]{1,0:T(8,128)(2,1)}, bf16[256,384]{1,0:T(8,128)(2,1)S(1)}, u32[]{:S(2)}, u32[]{:S(2)}) collective-permute-start(bf16[256,384]{1,0:T(8,128)(2,1)} %get-tuple-element.57), channel_id=1, source_target_pairs={{0,2},{1,3},{4,6},{5,7},{8,10},{9,11},{12,14},{13,15},{16,18},{17,... | collective-permute-start | bytes 589832 | tf_op jit(solution)/shard_map/ppermute | solution.py:40
  105.3 7.6 %collective-permute-done.24.refs_0_ = bf16[256,384]{1,0:T(8,128)(2,1)S(1)} collective-permute-done((bf16[256,384]{1,0:T(8,128)(2,1)}, bf16[256,384]{1,0:T(8,128)(2,1)S(1)}, u32[]{:S(2)}, u32[]{:S(2)}) %collective-permute-start.24) | collective-permute-done | bytes 196640 | tf_op jit(solution)/shard_map/ppermute | solution.py:40
  112.9 3.2 %collective-permute-done.25.refs_1_ = bf16[256,384]{1,0:T(8,128)(2,1)S(1)} collective-permute-done((bf16[256,384]{1,0:T(8,128)(2,1)}, bf16[256,384]{1,0:T(8,128)(2,1)S(1)}, u32[]{:S(2)}, u32[]{:S(2)}) %collective-permute-start.25) | collective-permute-done | bytes 196640 | tf_op jit(solution)/shard_map/ppermute | solution.py:40
  116.2 1.4 %side_by_side.1 = bf16[256,1536]{1,0:T(8,128)(2,1)} custom-call(s32[3]{0:T(128)S(1)} %copy-done, bf16[256,384]{1,0:T(8,128)(2,1)S(1)} %collective-permute-done.24.refs_0_, bf16[256,384]{1,0:T(8,128)(2,1)S(1)} %collective-permute-done.25.refs_1_, bf16[256,384]{1,0:T(8,128)(2,1)S(1)} %collective-permute-done.26.refs_2_, ...), custom_call_target="tpu_custom_call", output_to_operand_aliasing={{}: (4, {})} | custom-call | flops 10000000 | bytes 100000 | tf_op jit(solution)/shard_map/side_by_side/pallas_call | solution.py:325
  (75 shorter events, 8.8 us)
Async XLA Ops:
  1.3 6.4 %collective-permute-start = (bf16[96,1152]{1,0:T(8,128)(2,1)S(1)}, bf16[96,1152]{1,0:T(8,128)(2,1)S(1)}, u32[]{:S(2)}, u32[]{:S(2)}) collective-permute-start(bf16[96,1152]{1,0:T(8,128)(2,1)S(1)} %pad_maximum_fusion.1), channel_id=1, source_target_pairs={{0,16},{1,17},{4,20},{5,21},{8,24},{9,25},{12,28},{13,29},{16,0},{... | collective-permute-start | bytes 663560 | tf_op jit(solution)/shard_map/ppermute | solution.py:60
  5.1 47.8 %copy-start.2 = (bf16[256,1536]{1,0:T(8,128)(2,1)}, bf16[256,1536]{1,0:T(8,128)(2,1)S(1)}, u32[]{:S(2)}) copy-start(bf16[256,1536]{1,0:T(8,128)(2,1)S(1)} %fusion.3.refs_0_) | copy-start | bytes 2359300
  7.7 45.2 %copy-start.3 = (bf16[192,1152]{1,0:T(8,128)(2,1)}, bf16[192,1152]{1,0:T(8,128)(2,1)S(1)}, u32[]{:S(2)}) copy-start(bf16[192,1152]{1,0:T(8,128)(2,1)S(1)} %pad_maximum_fusion.refs_5_) | copy-start | bytes 1327108
  7.7 10.9 %collective-permute-start.5 = (bf16[192,1152]{1,0:T(8,128)(2,1)S(1)}, bf16[192,1152]{1,0:T(8,128)(2,1)}, u32[]{:S(2)}, u32[]{:S(2)}) collective-permute-start(bf16[192,1152]{1,0:T(8,128)(2,1)S(1)} %pad_maximum_fusion.refs_5_), channel_id=1, source_target_pairs={{0,32},{1,225},{4,36},{5,229},{8,40},{9,233},{12,44},{13,237},{16,... | collective-permute-start | bytes 1327112 | tf_op jit(solution)/shard_map/ppermute | solution.py:54
  13.4 18.8 %collective-permute-start.1 = (bf16[256,1536]{1,0:T(8,128)(2,1)S(1)}, bf16[256,1536]{1,0:T(8,128)(2,1)S(1)}, u32[]{:S(2)}, u32[]{:S(2)}) collective-permute-start(bf16[256,1536]{1,0:T(8,128)(2,1)S(1)} %fusion.3.refs_0_), channel_id=1, source_target_pairs={{0,16},{1,17},{4,20},{5,21},{8,24},{9,25},{12,28},{13,29},{16,2},{... | collective-permute-start | bytes 2359304 | tf_op jit(solution)/shard_map/ppermute | solution.py:40
  14.7 17.9 %collective-permute-start.2 = (bf16[256,1536]{1,0:T(8,128)(2,1)S(1)}, bf16[256,1536]{1,0:T(8,128)(2,1)S(1)}, u32[]{:S(2)}, u32[]{:S(2)}) collective-permute-start(bf16[256,1536]{1,0:T(8,128)(2,1)S(1)} %fusion.3.refs_0_), channel_id=1, source_target_pairs={{0,18},{1,19},{4,22},{5,23},{8,26},{9,27},{12,30},{13,31},{16,0},{... | collective-permute-start | bytes 2359304 | tf_op jit(solution)/shard_map/ppermute | solution.py:40
  18.6 13.9 %collective-permute-start.6 = (bf16[192,1152]{1,0:T(8,128)(2,1)}, bf16[192,1152]{1,0:T(8,128)(2,1)}, u32[]{:S(2)}, u32[]{:S(2)}) collective-permute-start(bf16[192,1152]{1,0:T(8,128)(2,1)} %collective-permute-done.5.refs_6_), channel_id=1, source_target_pairs={{0,32},{1,225},{4,36},{5,229},{8,40},{9,233},{12,44},{13,237},{16,... | collective-permute-start | bytes 1327112 | tf_op jit(solution)/shard_map/ppermute | solution.py:54
  32.2 20.7 %copy-start.4 = (bf16[256,1536]{1,0:T(8,128)(2,1)}, bf16[256,1536]{1,0:T(8,128)(2,1)S(1)}, u32[]{:S(2)}) copy-start(bf16[256,1536]{1,0:T(8,128)(2,1)S(1)} %collective-permute-done.1.refs_1_) | copy-start | bytes 2359300
  32.6 20.3 %copy-start.5 = (bf16[256,1536]{1,0:T(8,128)(2,1)}, bf16[256,1536]{1,0:T(8,128)(2,1)S(1)}, u32[]{:S(2)}) copy-start(bf16[256,1536]{1,0:T(8,128)(2,1)S(1)} %collective-permute-done.2.refs_2_) | copy-start | bytes 2359300
  32.6 12.5 %collective-permute-start.7 = (bf16[192,1152]{1,0:T(8,128)(2,1)}, bf16[192,1152]{1,0:T(8,128)(2,1)}, u32[]{:S(2)}, u32[]{:S(2)}) collective-permute-start(bf16[192,1152]{1,0:T(8,128)(2,1)} %collective-permute-done.6.refs_7_), channel_id=1, source_target_pairs={{0,32},{1,225},{4,36},{5,229},{8,40},{9,233},{12,44},{13,237},{16,... | collective-permute-start | bytes 1327112 | tf_op jit(solution)/shard_map/ppermute | solution.py:54
  33.7 10.8 %collective-permute-start.3 = (bf16[128,1536]{1,0:T(8,128)(2,1)S(1)}, bf16[128,1536]{1,0:T(8,128)(2,1)S(1)}, u32[]{:S(2)}, u32[]{:S(2)}) collective-permute-start(bf16[128,1536]{1,0:T(8,128)(2,1)S(1)} %slice.8), channel_id=1, source_target_pairs={{0,16},{1,17},{4,20},{5,21},{8,24},{9,25},{12,28},{13,29},{16,2},{... | collective-permute-start | bytes 1179656 | tf_op jit(solution)/shard_map/ppermute | solution.py:40
  34.7 10.4 %collective-permute-start.4 = (bf16[128,1536]{1,0:T(8,128)(2,1)S(1)}, bf16[128,1536]{1,0:T(8,128)(2,1)}, u32[]{:S(2)}, u32[]{:S(2)}) collective-permute-start(bf16[128,1536]{1,0:T(8,128)(2,1)S(1)} %slice.9), channel_id=1, source_target_pairs={{0,18},{1,19},{4,22},{5,23},{8,26},{9,27},{12,30},{13,31},{16,0},{... | collective-permute-start | bytes 1179656 | tf_op jit(solution)/shard_map/ppermute | solution.py:40
  36.6 10.7 %collective-permute-start.9 = (bf16[192,1152]{1,0:T(8,128)(2,1)}, bf16[192,1152]{1,0:T(8,128)(2,1)}, u32[]{:S(2)}, u32[]{:S(2)}) collective-permute-start(bf16[192,1152]{1,0:T(8,128)(2,1)} %collective-permute-done.5.refs_6_), channel_id=1, source_target_pairs={{0,1},{1,0},{4,5},{5,4},{8,9},{9,8},{12,13},{13,12},{16,17},{17,16... | collective-permute-start | bytes 1327112 | tf_op jit(solution)/shard_map/ppermute | solution.py:44
  36.6 10.7 %collective-permute-start.10 = (bf16[192,1152]{1,0:T(8,128)(2,1)}, bf16[192,1152]{1,0:T(8,128)(2,1)}, u32[]{:S(2)}, u32[]{:S(2)}) collective-permute-start(bf16[192,1152]{1,0:T(8,128)(2,1)} %collective-permute-done.6.refs_7_), channel_id=1, source_target_pairs={{0,1},{1,0},{4,5},{5,4},{8,9},{9,8},{12,13},{13,12},{16,17},{17,16... | collective-permute-start | bytes 1327112 | tf_op jit(solution)/shard_map/ppermute | solution.py:44
  45.1 2.2 %collective-permute-start.11 = (bf16[192,1152]{1,0:T(8,128)(2,1)}, bf16[192,1152]{1,0:T(8,128)(2,1)}, u32[]{:S(2)}, u32[]{:S(2)}) collective-permute-start(bf16[192,1152]{1,0:T(8,128)(2,1)} %collective-permute-done.7.refs_8_), channel_id=1, source_target_pairs={{0,1},{1,0},{4,5},{5,4},{8,9},{9,8},{12,13},{13,12},{16,17},{17,16... | collective-permute-start | bytes 1327112 | tf_op jit(solution)/shard_map/ppermute | solution.py:44
  45.1 7.8 %collective-permute-start.8 = (bf16[192,1152]{1,0:T(8,128)(2,1)}, bf16[192,1152]{1,0:T(8,128)(2,1)}, u32[]{:S(2)}, u32[]{:S(2)}) collective-permute-start(bf16[192,1152]{1,0:T(8,128)(2,1)} %collective-permute-done.7.refs_8_), channel_id=1, source_target_pairs={{0,32},{1,225},{4,36},{5,229},{8,40},{9,233},{12,44},{13,237},{16,... | collective-permute-start | bytes 1327112 | tf_op jit(solution)/shard_map/ppermute | solution.py:54
  62.1 5.8 %collective-permute-start.12 = (bf16[2,2,256,768]{3,2,1,0:T(8,128)(2,1)}, bf16[2,2,256,768]{3,2,1,0:T(8,128)(2,1)S(1)}, u32[]{:S(2)}, u32[]{:S(2)}) collective-permute-start(bf16[2,2,256,768]{3,2,1,0:T(8,128)(2,1)} %get-tuple-element.37.own), channel_id=1, source_target_pairs={{0,1},{1,0},{4,5},{5,4},{8,9},{9,8},{12,13},{13,12},{16,17},{17,16... | collective-permute-start | bytes 4718600 | tf_op jit(solution)/shard_map/ppermute | solution.py:44
  64.7 14.1 %collective-permute-start.14 = (bf16[256,768]{1,0:T(8,128)(2,1)}, bf16[256,768]{1,0:T(8,128)(2,1)S(1)}, u32[]{:S(2)}, u32[]{:S(2)}) collective-permute-start(bf16[256,768]{1,0:T(8,128)(2,1)} %get-tuple-element.43), channel_id=1, source_target_pairs={{0,224},{1,225},{4,228},{5,229},{8,232},{9,233},{12,236},{13,237},... | collective-permute-start | bytes 1179656 | tf_op jit(solution)/shard_map/ppermute | solution.py:40
  64.9 22.0 %collective-permute-start.23 = (bf16[2,256,768]{2,1,0:T(8,128)(2,1)}, bf16[2,256,768]{2,1,0:T(8,128)(2,1)S(1)}, u32[]{:S(2)}, u32[]{:S(2)}) collective-permute-start(bf16[2,256,768]{2,1,0:T(8,128)(2,1)} %get-tuple-element.54), channel_id=1, source_target_pairs={{0,13},{1,4},{4,1},{5,8},{8,5},{9,12},{12,9},{13,0},{16,29},{17,20... | collective-permute-start | bytes 2359304 | tf_op jit(solution)/shard_map/ppermute | solution.py:48
  65.5 15.4 %collective-permute-start.13 = (bf16[256,768]{1,0:T(8,128)(2,1)}, bf16[256,768]{1,0:T(8,128)(2,1)S(1)}, u32[]{:S(2)}, u32[]{:S(2)}) collective-permute-start(bf16[256,768]{1,0:T(8,128)(2,1)} %get-tuple-element.42), channel_id=1, source_target_pairs={{0,32},{1,33},{4,36},{5,37},{8,40},{9,41},{12,44},{13,45},{16,48},... | collective-permute-start | bytes 1179656 | tf_op jit(solution)/shard_map/ppermute | solution.py:40
  68.0 16.1 %collective-permute-start.16 = (bf16[256,768]{1,0:T(8,128)(2,1)}, bf16[256,768]{1,0:T(8,128)(2,1)S(1)}, u32[]{:S(2)}, u32[]{:S(2)}) collective-permute-start(bf16[256,768]{1,0:T(8,128)(2,1)} %get-tuple-element.47), channel_id=1, source_target_pairs={{0,224},{1,225},{4,228},{5,229},{8,232},{9,233},{12,236},{13,237},... | collective-permute-start | bytes 1179656 | tf_op jit(solution)/shard_map/ppermute | solution.py:40
  68.3 17.5 %collective-permute-start.15 = (bf16[256,768]{1,0:T(8,128)(2,1)}, bf16[256,768]{1,0:T(8,128)(2,1)S(1)}, u32[]{:S(2)}, u32[]{:S(2)}) collective-permute-start(bf16[256,768]{1,0:T(8,128)(2,1)} %get-tuple-element.45), channel_id=1, source_target_pairs={{0,32},{1,33},{4,36},{5,37},{8,40},{9,41},{12,44},{13,45},{16,48},... | collective-permute-start | bytes 1179656 | tf_op jit(solution)/shard_map/ppermute | solution.py:40
  78.8 8.5 %collective-permute-start.22 = (bf16[256,768]{1,0:T(8,128)(2,1)S(1)}, bf16[256,768]{1,0:T(8,128)(2,1)S(1)}, u32[]{:S(2)}, u32[]{:S(2)}) collective-permute-start(bf16[256,768]{1,0:T(8,128)(2,1)S(1)} %collective-permute-done.14.refs_5_), channel_id=1, source_target_pairs={{0,13},{1,4},{4,1},{5,8},{8,5},{9,12},{12,9},{13,0},{16,29},{17,20... | collective-permute-start | bytes 1179656 | tf_op jit(solution)/shard_map/ppermute | solution.py:48
  81.0 10.6 %collective-permute-start.21 = (bf16[256,768]{1,0:T(8,128)(2,1)S(1)}, bf16[256,768]{1,0:T(8,128)(2,1)S(1)}, u32[]{:S(2)}, u32[]{:S(2)}) collective-permute-start(bf16[256,768]{1,0:T(8,128)(2,1)S(1)} %collective-permute-done.13.refs_4_), channel_id=1, source_target_pairs={{0,13},{1,4},{4,1},{5,8},{8,5},{9,12},{12,9},{13,0},{16,29},{17,20... | collective-permute-start | bytes 1179656 | tf_op jit(solution)/shard_map/ppermute | solution.py:48
  84.0 7.5 %collective-permute-start.20 = (bf16[256,768]{1,0:T(8,128)(2,1)S(1)}, bf16[256,768]{1,0:T(8,128)(2,1)}, u32[]{:S(2)}, u32[]{:S(2)}) collective-permute-start(bf16[256,768]{1,0:T(8,128)(2,1)S(1)} %collective-permute-done.16.refs_7_), channel_id=1, source_target_pairs={{0,1},{1,0},{4,5},{5,4},{8,9},{9,8},{12,13},{13,12},{16,17},{17,16... | collective-permute-start | bytes 1179656 | tf_op jit(solution)/shard_map/ppermute | solution.py:44
  85.8 5.7 %collective-permute-start.19 = (bf16[256,768]{1,0:T(8,128)(2,1)S(1)}, bf16[256,768]{1,0:T(8,128)(2,1)}, u32[]{:S(2)}, u32[]{:S(2)}) collective-permute-start(bf16[256,768]{1,0:T(8,128)(2,1)S(1)} %collective-permute-done.15.refs_6_), channel_id=1, source_target_pairs={{0,1},{1,0},{4,5},{5,4},{8,9},{9,8},{12,13},{13,12},{16,17},{17,16... | collective-permute-start | bytes 1179656 | tf_op jit(solution)/shard_map/ppermute | solution.py:44
  86.9 4.6 %collective-permute-start.18 = (bf16[256,768]{1,0:T(8,128)(2,1)S(1)}, bf16[256,768]{1,0:T(8,128)(2,1)}, u32[]{:S(2)}, u32[]{:S(2)}) collective-permute-start(bf16[256,768]{1,0:T(8,128)(2,1)S(1)} %collective-permute-done.14.refs_5_), channel_id=1, source_target_pairs={{0,1},{1,0},{4,5},{5,4},{8,9},{9,8},{12,13},{13,12},{16,17},{17,16... | collective-permute-start | bytes 1179656 | tf_op jit(solution)/shard_map/ppermute | solution.py:44
  87.3 4.2 %collective-permute-start.17 = (bf16[256,768]{1,0:T(8,128)(2,1)S(1)}, bf16[256,768]{1,0:T(8,128)(2,1)}, u32[]{:S(2)}, u32[]{:S(2)}) collective-permute-start(bf16[256,768]{1,0:T(8,128)(2,1)S(1)} %collective-permute-done.13.refs_4_), channel_id=1, source_target_pairs={{0,1},{1,0},{4,5},{5,4},{8,9},{9,8},{12,13},{13,12},{16,17},{17,16... | collective-permute-start | bytes 1179656 | tf_op jit(solution)/shard_map/ppermute | solution.py:44
  92.3 23.9 %copy-start = (s32[3]{0:T(128)S(1)}, s32[3]{0:T(128)}, u32[]{:S(2)}) copy-start(s32[3]{0:T(128)} %pad_add_fusion.place) | copy-start | bytes 40
  101.3 11.6 %collective-permute-start.24 = (bf16[256,384]{1,0:T(8,128)(2,1)}, bf16[256,384]{1,0:T(8,128)(2,1)S(1)}, u32[]{:S(2)}, u32[]{:S(2)}) collective-permute-start(bf16[256,384]{1,0:T(8,128)(2,1)} %get-tuple-element.55), channel_id=1, source_target_pairs={{0,18},{1,19},{4,22},{5,23},{8,26},{9,27},{12,30},{13,31},{16,0},{... | collective-permute-start | bytes 589832 | tf_op jit(solution)/shard_map/ppermute | solution.py:40
  104.0 12.2 %collective-permute-start.25 = (bf16[256,384]{1,0:T(8,128)(2,1)}, bf16[256,384]{1,0:T(8,128)(2,1)S(1)}, u32[]{:S(2)}, u32[]{:S(2)}) collective-permute-start(bf16[256,384]{1,0:T(8,128)(2,1)} %get-tuple-element.56), channel_id=1, source_target_pairs={{0,16},{1,17},{4,20},{5,21},{8,24},{9,25},{12,28},{13,29},{16,2},{... | collective-permute-start | bytes 589832 | tf_op jit(solution)/shard_map/ppermute | solution.py:40
  104.0 12.2 %collective-permute-start.26 = (bf16[256,384]{1,0:T(8,128)(2,1)}, bf16[256,384]{1,0:T(8,128)(2,1)S(1)}, u32[]{:S(2)}, u32[]{:S(2)}) collective-permute-start(bf16[256,384]{1,0:T(8,128)(2,1)} %get-tuple-element.57), channel_id=1, source_target_pairs={{0,2},{1,3},{4,6},{5,7},{8,10},{9,11},{12,14},{13,15},{16,18},{17,... | collective-permute-start | bytes 589832 | tf_op jit(solution)/shard_map/ppermute | solution.py:40
  (12 other events, 67.7 us)

commit v5 on v4

--- a/solution.py
+++ b/solution.py
@@ -274,17 +274,31 @@
 )
 
 
-def attend_near(q, own, mate):
+def attend_near(q, own, mate, states=None):
+    first = GROUP_HEADS - 1 if states else 0
+
+    def block(array, width):
+        lead = array.ndim - 1
+        return pl.BlockSpec(array.shape[:-1] + (width,), lambda h: (0,) * lead + (h + first,))
+
+    def state(pair):
+        return pl.BlockSpec(pair[1].block_shape, lambda h: (h + first, 0, 0, 0))
+
+    def kernel(*refs):
+        near_kernel(*refs[:3], *refs[-4:])
+
+    shapes = (PEAK[0], PEAK[0], TOTAL[0], TOTAL[0])
     return pl.pallas_call(
-        near_kernel,
-        name="attend_near",
-        grid=(GROUP_HEADS,),
-        out_shape=(PEAK[0], PEAK[0], TOTAL[0], TOTAL[0]),
-        in_specs=[head_spec(q, HD), head_spec(own, 2 * HD), head_spec(mate, 2 * HD)],
-        out_specs=[PEAK[1], PEAK[1], TOTAL[1], TOTAL[1]],
+        kernel,
+        name="attend_near_last" if states else "attend_near",
+        grid=(1 if states else GROUP_HEADS - 1,),
+        out_shape=shapes,
+        in_specs=[block(q, HD), block(own, 2 * HD), block(mate, 2 * HD)] + [ANY] * (4 if states else 0),
+        out_specs=[state(PEAK), state(PEAK), state(TOTAL), state(TOTAL)],
+        input_output_aliases={3 + n: n for n in range(4)} if states else {},
         compiler_params=NEAR,
         cost_estimate=LIGHT,
-    )(q, own, mate)
+    )(q, own, mate, *(states or ()))
 
 
 def attend_far(valid, q, peaks, totals, *kv):
@@ -368,9 +382,12 @@
     mate = swap_cores(own)
     inner_below = shift(after(inner_high, mate), dz=1)
     inner_above = shift(after(inner_low, mate), dz=-1)
-    outer_peak, inner_peak, outer_total, inner_total = attend_near(q, own, mate)
-    corner_below = outward(after(outer_below, inner_peak))
-    corner_above = outward(after(outer_above, inner_peak))
+    states = attend_near(q, own, mate)
+    (outer_below, outer_above), states = lax.optimization_barrier(((outer_below, outer_above), states))
+    states = attend_near(q, own, mate, states)
+    outer_peak, inner_peak, outer_total, inner_total = states
+    corner_below = outward(outer_below)
+    corner_above = outward(outer_above)
     last_x = jnp.where(core == 0, 0, 3)
     valid = jnp.stack([z > 0, z < 7, x != last_x, core, y]).astype(jnp.int32)
     outer_rows, inner_rows = (outer_below, outer_above), (inner_below, inner_above)

time: 118 us -> 117 us (level)
  Pallas kernels: 29 us -> 31.1 us
  waiting for transfers between devices: 48.3 us -> 46.2 us
    pallas_call x1 -> x2, Pallas kernels: 9.38 us -> 11.4 us  [attend_near(): pl.pallas_call(kernel, name='attend_near_last' if states else 'attend_nea...]
    ppermute x8, waiting for transfers between devices: 1.34 us -> 0.02 us  [swap_cores(): lax.ppermute(array, AXES, pairs(lambda z, y, x, core: (z, y, x, 1 - core)))]
  transfers between devices with their start and end apart: 27 -> 27, of which waited for: 14 -> 10; matrix products, arithmetic and copies ran while one was open for 3% -> 3% of each run, Pallas kernels for 8% -> 10%
where the time goes in v5:
time: 117 us
  waiting for transfers between devices  46.2 us (39%)
  starting transfers between devices  33.3 us (28%)
  Pallas kernels  31.1 us (27%)
  other arithmetic  2.95 us (3%)
  local copies, waits for them, and re-layouts  2.84 us (2%)
    ppermute x11, waiting for transfers between devices, shift(): lax.ppermute(array, AXES, pairs(lambda z, y, x, core: (z + dz, y + dy, x,...  32.9 us
    ppermute x11, starting transfers between devices, shift(): lax.ppermute(array, AXES, pairs(lambda z, y, x, core: (z + dz, y + dy, x,...  12.1 us
    ppermute x4, starting transfers between devices, ring_step(): lax.ppermute(array, AXES, pairs(lambda z, y, x, core: (z + (-1 if core el...  11.6 us
    pallas_call x2, Pallas kernels, attend_near(): pl.pallas_call(kernel, name='attend_near_last' if states else 'attend_nea...  11.4 us
    pallas_call x1, Pallas kernels, project(): pl.pallas_call(project_kernel, name='project', out_shape=(jax.ShapeDtypeS...  9.19 us
    pallas_call x1, Pallas kernels, attend_far(): pl.pallas_call(far_kernel, name='attend_far', grid_spec=pltpu.PrefetchSca...  9.09 us
    ppermute x4, waiting for transfers between devices, ring_step(): lax.ppermute(array, AXES, pairs(lambda z, y, x, core: (z + (-1 if core el...  7.59 us
    ppermute x8, starting transfers between devices, swap_cores(): lax.ppermute(array, AXES, pairs(lambda z, y, x, core: (z, y, x, 1 - core)))  4.39 us
  transfers between devices with their start and end apart: 27, of which 10 were waited for; matrix products, arithmetic and copies ran while one was open for 3% of the time, Pallas kernels for 10%

profile of v5, /device:TPU:7, one launch (start us, length us, event | category | flops | bytes accessed | tf_op | source)
XLA Modules:
  0.0 116.9 jit_solution(15716415715235224443)
XLA Ops:
  0.0 1.2 %constant_dynamic-slice_fusion.2 = (bf16[96,384]{1,0:T(8,128)(2,1)S(1)}, bf16[96,384]{1,0:T(8,128)(2,1)S(1)}, bf16[96,384]{1,0:T(8,128)(2,1)S(1)}, bf16[96,384]{...) fusion(bf16[96,4608]{1,0:T(8,128)(2,1)} %param.7, s32[]{:T(128)S(6)} %select_n.26, ...), kind=kLoop, calls=%fused_computation.13 | loop fusion | bytes 884760 | tf_op jit(solution)/shard_map/dynamic_slice | solution.py:358
  1.3 1.4 %collective-permute-start = (bf16[96,1152]{1,0:T(8,128)(2,1)S(1)}, bf16[96,1152]{1,0:T(8,128)(2,1)S(1)}, u32[]{:S(2)}, u32[]{:S(2)}) collective-permute-start(bf16[96,1152]{1,0:T(8,128)(2,1)S(1)} %pad_maximum_fusion.1), channel_id=1, source_target_pairs={{0,16},{1,17},{4,20},{5,21},{8,24},{9,25},{12,28},{13,29},{16,0},{... | collective-permute-start | bytes 663560 | tf_op jit(solution)/shard_map/ppermute | solution.py:60
  2.7 1.6 %reduce_sum.18 = f32[4,4,16]{2,1,0:T(4,128)S(1)} reduce(f32[4,4,16,1536]{3,2,1,0:T(8,128)} %param.6, f32[]{:T(128)} %constant.44.clone.1), dimensions={3}, to_apply=%region_0.0 | reduce | flops 392960 | bytes 1573892 | tf_op jit(solution)/shard_map/reduce_sum | solution.py:70
  5.1 2.5 %collective-permute-done = bf16[96,1152]{1,0:T(8,128)(2,1)S(1)} collective-permute-done((bf16[96,1152]{1,0:T(8,128)(2,1)S(1)}, bf16[96,1152]{1,0:T(8,128)(2,1)S(1)}, u32[]{:S(2)}, u32[]{:S(2)}) %collective-permute-start) | collective-permute-done | bytes 221216 | tf_op jit(solution)/shard_map/ppermute | solution.py:60
  7.7 5.7 %collective-permute-start.5 = (bf16[192,1152]{1,0:T(8,128)(2,1)S(1)}, bf16[192,1152]{1,0:T(8,128)(2,1)}, u32[]{:S(2)}, u32[]{:S(2)}) collective-permute-start(bf16[192,1152]{1,0:T(8,128)(2,1)S(1)} %pad_maximum_fusion.refs_5_), channel_id=1, source_target_pairs={{0,32},{1,225},{4,36},{5,229},{8,40},{9,233},{12,44},{13,237},{16,... | collective-permute-start | bytes 1327112 | tf_op jit(solution)/shard_map/ppermute | solution.py:54
  13.4 2.7 %collective-permute-start.2 = (bf16[256,1536]{1,0:T(8,128)(2,1)S(1)}, bf16[256,1536]{1,0:T(8,128)(2,1)S(1)}, u32[]{:S(2)}, u32[]{:S(2)}) collective-permute-start(bf16[256,1536]{1,0:T(8,128)(2,1)S(1)} %fusion.3.refs_0_), channel_id=1, source_target_pairs={{0,18},{1,19},{4,22},{5,23},{8,26},{9,27},{12,30},{13,31},{16,0},{... | collective-permute-start | bytes 2359304 | tf_op jit(solution)/shard_map/ppermute | solution.py:40
  16.1 2.5 %collective-permute-done.5.refs_6_ = bf16[192,1152]{1,0:T(8,128)(2,1)} collective-permute-done((bf16[192,1152]{1,0:T(8,128)(2,1)S(1)}, bf16[192,1152]{1,0:T(8,128)(2,1)}, u32[]{:S(2)}, u32[]{:S(2)}) %collective-permute-start.5) | collective-permute-done | bytes 442400 | tf_op jit(solution)/shard_map/ppermute | solution.py:54
  18.6 3.2 %collective-permute-start.6 = (bf16[192,1152]{1,0:T(8,128)(2,1)}, bf16[192,1152]{1,0:T(8,128)(2,1)}, u32[]{:S(2)}, u32[]{:S(2)}) collective-permute-start(bf16[192,1152]{1,0:T(8,128)(2,1)} %collective-permute-done.5.refs_6_), channel_id=1, source_target_pairs={{0,32},{1,225},{4,36},{5,229},{8,40},{9,233},{12,44},{13,237},{16,... | collective-permute-start | bytes 1327112 | tf_op jit(solution)/shard_map/ppermute | solution.py:54
  21.8 10.0 %collective-permute-done.2.refs_2_ = bf16[256,1536]{1,0:T(8,128)(2,1)S(1)} collective-permute-done((bf16[256,1536]{1,0:T(8,128)(2,1)S(1)}, bf16[256,1536]{1,0:T(8,128)(2,1)S(1)}, u32[]{:S(2)}, u32[]{:S(2)}) %collective-permute-start.2) | collective-permute-done | bytes 786464 | tf_op jit(solution)/shard_map/ppermute | solution.py:40
  31.8 3.4 %collective-permute-done.1.refs_1_ = bf16[256,1536]{1,0:T(8,128)(2,1)S(1)} collective-permute-done((bf16[256,1536]{1,0:T(8,128)(2,1)S(1)}, bf16[256,1536]{1,0:T(8,128)(2,1)S(1)}, u32[]{:S(2)}, u32[]{:S(2)}) %collective-permute-start.1) | collective-permute-done | bytes 786464 | tf_op jit(solution)/shard_map/ppermute | solution.py:40
  35.2 0.7 collective-permute-start.7
  36.4 1.2 collective-permute-start.3
  38.1 8.2 %collective-permute-done.4.refs_4_ = bf16[128,1536]{1,0:T(8,128)(2,1)S(1)} collective-permute-done((bf16[128,1536]{1,0:T(8,128)(2,1)S(1)}, bf16[128,1536]{1,0:T(8,128)(2,1)S(1)}, u32[]{:S(2)}, u32[]{:S(2)}) %collective-permute-start.4) | collective-permute-done | bytes 393248 | tf_op jit(solution)/shard_map/ppermute | solution.py:40
  46.3 1.0 collective-permute-done.3.refs_3_
  47.4 2.0 %collective-permute-start.8 = (bf16[192,1152]{1,0:T(8,128)(2,1)}, bf16[192,1152]{1,0:T(8,128)(2,1)}, u32[]{:S(2)}, u32[]{:S(2)}) collective-permute-start(bf16[192,1152]{1,0:T(8,128)(2,1)} %collective-permute-done.7.refs_8_), channel_id=1, source_target_pairs={{0,32},{1,225},{4,36},{5,229},{8,40},{9,233},{12,44},{13,237},{16,... | collective-permute-start | bytes 1327112 | tf_op jit(solution)/shard_map/ppermute | solution.py:54
  50.1 5.1 %collective-permute-done.8.refs_9_ = bf16[192,1152]{1,0:T(8,128)(2,1)} collective-permute-done((bf16[192,1152]{1,0:T(8,128)(2,1)}, bf16[192,1152]{1,0:T(8,128)(2,1)}, u32[]{:S(2)}, u32[]{:S(2)}) %collective-permute-start.8) | collective-permute-done | bytes 442400 | tf_op jit(solution)/shard_map/ppermute | solution.py:54
  55.2 9.2 %project.1 = (bf16[4,256,384]{2,1,0:T(8,128)(2,1)}, bf16[2,2,256,768]{3,2,1,0:T(8,128)(2,1)}, bf16[2,256,768]{2,1,0:T(8,128)(2,1)}, bf16[256,768]{1,0:T(8,128)(2...) custom-call(s32[3]{0:T(128)} %pad_add_fusion.place, ...), custom_call_target="tpu_custom_call" | custom-call | flops 10000000 | bytes 100000 | tf_op jit(solution)/shard_map/project/pallas_call | solution.py:164
  64.4 2.7 %collective-permute-start.12 = (bf16[2,2,256,768]{3,2,1,0:T(8,128)(2,1)}, bf16[2,2,256,768]{3,2,1,0:T(8,128)(2,1)S(1)}, u32[]{:S(2)}, u32[]{:S(2)}) collective-permute-start(bf16[2,2,256,768]{3,2,1,0:T(8,128)(2,1)} %get-tuple-element.45.refs_1_), channel_id=1, source_target_pairs={{0,1},{1,0},{4,5},{5,4},{8,9},{9,8},{12,13},{13,12},{16,17},{17,16... | collective-permute-start | bytes 4718600 | tf_op jit(solution)/shard_map/ppermute | solution.py:44
  67.0 2.7 %collective-permute-start.14 = (bf16[256,768]{1,0:T(8,128)(2,1)}, bf16[256,768]{1,0:T(8,128)(2,1)S(1)}, u32[]{:S(2)}, u32[]{:S(2)}) collective-permute-start(bf16[256,768]{1,0:T(8,128)(2,1)} %get-tuple-element.47), channel_id=1, source_target_pairs={{0,224},{1,225},{4,228},{5,229},{8,232},{9,233},{12,236},{13,237},... | collective-permute-start | bytes 1179656 | tf_op jit(solution)/shard_map/ppermute | solution.py:40
  69.7 0.7 collective-permute-start.23
  70.4 2.7 %collective-permute-start.16 = (bf16[256,768]{1,0:T(8,128)(2,1)}, bf16[256,768]{1,0:T(8,128)(2,1)S(1)}, u32[]{:S(2)}, u32[]{:S(2)}) collective-permute-start(bf16[256,768]{1,0:T(8,128)(2,1)} %get-tuple-element.65), channel_id=1, source_target_pairs={{0,224},{1,225},{4,228},{5,229},{8,232},{9,233},{12,236},{13,237},... | collective-permute-start | bytes 1179656 | tf_op jit(solution)/shard_map/ppermute | solution.py:40
  73.1 6.9 %attend_near.1 = (f32[3,2,256,128]{3,2,1,0:T(8,128)}, f32[3,2,256,128]{3,2,1,0:T(8,128)}, f32[3,2,256,256]{3,2,1,0:T(8,128)}, f32[3,2,256,256]{3,2,1,0:T(8,128)}) custom-call(bf16[4,256,384]{2,1,0:T(8,128)(2,1)} %get-tuple-element.44.refs_0_.q, bf16[2,2,256,768]{3,2,1,0:T(8,128)(2,1)} %get-tuple-element.45.refs_1_, bf16[2,2,256,768]{3,2,1,0:T(8,128)(2,1)} %copy-done.2), custom_call_target="tpu_custom_call" | custom-call | flops 10000000 | bytes 100000 | tf_op jit(solution)/shard_map/attend_near/pallas_call | solution.py:291
  80.1 2.9 %collective-permute-start.21 = (bf16[256,768]{1,0:T(8,128)(2,1)S(1)}, bf16[256,768]{1,0:T(8,128)(2,1)S(1)}, u32[]{:S(2)}, u32[]{:S(2)}) collective-permute-start(bf16[256,768]{1,0:T(8,128)(2,1)S(1)} %collective-permute-done.13.refs_4_), channel_id=1, source_target_pairs={{0,13},{1,4},{4,1},{5,8},{8,5},{9,12},{12,9},{13,0},{16,29},{17,20... | collective-permute-start | bytes 1179656 | tf_op jit(solution)/shard_map/ppermute | solution.py:48
  83.3 4.5 %attend_near_last.1 = (f32[3,2,256,128]{3,2,1,0:T(8,128)}, f32[3,2,256,128]{3,2,1,0:T(8,128)}, f32[3,2,256,256]{3,2,1,0:T(8,128)}, f32[3,2,256,256]{3,2,1,0:T(8,128)}) custom-call(bf16[4,256,384]{2,1,0:T(8,128)(2,1)} %get-tuple-element.44.refs_0_.q, ...), custom_call_target="tpu_custom_call", output_to_operand_aliasing={{0}: (3, {}), {1}: (4, {}), {2}: (5, {}), {3}: (6, {})} | custom-call | flops 10000000 | bytes 100000 | tf_op jit(solution)/shard_map/attend_near_last/pallas_call | solution.py:291
  89.7 3.1 %collective-permute-done.22.refs_13_ = bf16[256,768]{1,0:T(8,128)(2,1)S(1)} collective-permute-done((bf16[256,768]{1,0:T(8,128)(2,1)S(1)}, bf16[256,768]{1,0:T(8,128)(2,1)S(1)}, u32[]{:S(2)}, u32[]{:S(2)}) %collective-permute-start.22) | collective-permute-done | bytes 393248 | tf_op jit(solution)/shard_map/ppermute | solution.py:48
  92.9 0.7 copy-done.13
  93.5 9.1 %attend_far.1 = (bf16[256,1536]{1,0:T(8,128)(2,1)}, bf16[256,384]{1,0:T(8,128)(2,1)}, bf16[256,384]{1,0:T(8,128)(2,1)}, bf16[256,384]{1,0:T(8,128)(2,1)}) custom-call(s32[5]{0:T(128)} %stack.45.valid, bf16[4,256,384]{2,1,0:T(8,128)(2,1)} %get-tuple-element.44.refs_0_.q, f32[3,2,256,128]{3,2,1,0:T(8,128)} %get-tuple-element.56.refs_0_, ...), custom_call_target="tpu_custom_call" | custom-call | flops 10000000 | bytes 100000 | tf_op jit(solution)/shard_map/attend_far/pallas_call | solution.py:307
  102.7 1.5 %collective-permute-start.25 = (bf16[256,384]{1,0:T(8,128)(2,1)}, bf16[256,384]{1,0:T(8,128)(2,1)S(1)}, u32[]{:S(2)}, u32[]{:S(2)}) collective-permute-start(bf16[256,384]{1,0:T(8,128)(2,1)} %get-tuple-element.72), channel_id=1, source_target_pairs={{0,16},{1,17},{4,20},{5,21},{8,24},{9,25},{12,28},{13,29},{16,2},{... | collective-permute-start | bytes 589832 | tf_op jit(solution)/shard_map/ppermute | solution.py:40
  104.2 0.8 collective-permute-start.26
  105.0 4.8 %collective-permute-done.24.refs_0_ = bf16[256,384]{1,0:T(8,128)(2,1)S(1)} collective-permute-done((bf16[256,384]{1,0:T(8,128)(2,1)}, bf16[256,384]{1,0:T(8,128)(2,1)S(1)}, u32[]{:S(2)}, u32[]{:S(2)}) %collective-permute-start.24) | collective-permute-done | bytes 196640 | tf_op jit(solution)/shard_map/ppermute | solution.py:40
  109.8 5.5 %collective-permute-done.25.refs_1_ = bf16[256,384]{1,0:T(8,128)(2,1)S(1)} collective-permute-done((bf16[256,384]{1,0:T(8,128)(2,1)}, bf16[256,384]{1,0:T(8,128)(2,1)S(1)}, u32[]{:S(2)}, u32[]{:S(2)}) %collective-permute-start.25) | collective-permute-done | bytes 196640 | tf_op jit(solution)/shard_map/ppermute | solution.py:40
  115.3 1.4 %side_by_side.1 = bf16[256,1536]{1,0:T(8,128)(2,1)} custom-call(s32[3]{0:T(128)S(1)} %copy-done, bf16[256,384]{1,0:T(8,128)(2,1)S(1)} %collective-permute-done.24.refs_0_, bf16[256,384]{1,0:T(8,128)(2,1)S(1)} %collective-permute-done.25.refs_1_, bf16[256,384]{1,0:T(8,128)(2,1)S(1)} %collective-permute-done.26.refs_2_, ...), custom_call_target="tpu_custom_call", output_to_operand_aliasing={{}: (4, {})} | custom-call | flops 10000000 | bytes 100000 | tf_op jit(solution)/shard_map/side_by_side/pallas_call | solution.py:339
  (76 shorter events, 5.0 us)
Async XLA Ops:
  1.3 6.4 %collective-permute-start = (bf16[96,1152]{1,0:T(8,128)(2,1)S(1)}, bf16[96,1152]{1,0:T(8,128)(2,1)S(1)}, u32[]{:S(2)}, u32[]{:S(2)}) collective-permute-start(bf16[96,1152]{1,0:T(8,128)(2,1)S(1)} %pad_maximum_fusion.1), channel_id=1, source_target_pairs={{0,16},{1,17},{4,20},{5,21},{8,24},{9,25},{12,28},{13,29},{16,0},{... | collective-permute-start | bytes 663560 | tf_op jit(solution)/shard_map/ppermute | solution.py:60
  5.1 50.0 %copy-start.3 = (bf16[256,1536]{1,0:T(8,128)(2,1)}, bf16[256,1536]{1,0:T(8,128)(2,1)S(1)}, u32[]{:S(2)}) copy-start(bf16[256,1536]{1,0:T(8,128)(2,1)S(1)} %fusion.3.refs_0_) | copy-start | bytes 2359300
  7.7 47.4 %copy-start.4 = (bf16[192,1152]{1,0:T(8,128)(2,1)}, bf16[192,1152]{1,0:T(8,128)(2,1)S(1)}, u32[]{:S(2)}) copy-start(bf16[192,1152]{1,0:T(8,128)(2,1)S(1)} %pad_maximum_fusion.refs_5_) | copy-start | bytes 1327108
  7.7 10.9 %collective-permute-start.5 = (bf16[192,1152]{1,0:T(8,128)(2,1)S(1)}, bf16[192,1152]{1,0:T(8,128)(2,1)}, u32[]{:S(2)}, u32[]{:S(2)}) collective-permute-start(bf16[192,1152]{1,0:T(8,128)(2,1)S(1)} %pad_maximum_fusion.refs_5_), channel_id=1, source_target_pairs={{0,32},{1,225},{4,36},{5,229},{8,40},{9,233},{12,44},{13,237},{16,... | collective-permute-start | bytes 1327112 | tf_op jit(solution)/shard_map/ppermute | solution.py:54
  13.4 18.4 %collective-permute-start.2 = (bf16[256,1536]{1,0:T(8,128)(2,1)S(1)}, bf16[256,1536]{1,0:T(8,128)(2,1)S(1)}, u32[]{:S(2)}, u32[]{:S(2)}) collective-permute-start(bf16[256,1536]{1,0:T(8,128)(2,1)S(1)} %fusion.3.refs_0_), channel_id=1, source_target_pairs={{0,18},{1,19},{4,22},{5,23},{8,26},{9,27},{12,30},{13,31},{16,0},{... | collective-permute-start | bytes 2359304 | tf_op jit(solution)/shard_map/ppermute | solution.py:40
  16.1 19.1 %collective-permute-start.1 = (bf16[256,1536]{1,0:T(8,128)(2,1)S(1)}, bf16[256,1536]{1,0:T(8,128)(2,1)S(1)}, u32[]{:S(2)}, u32[]{:S(2)}) collective-permute-start(bf16[256,1536]{1,0:T(8,128)(2,1)S(1)} %fusion.3.refs_0_), channel_id=1, source_target_pairs={{0,16},{1,17},{4,20},{5,21},{8,24},{9,25},{12,28},{13,29},{16,2},{... | collective-permute-start | bytes 2359304 | tf_op jit(solution)/shard_map/ppermute | solution.py:40
  18.6 16.6 %collective-permute-start.6 = (bf16[192,1152]{1,0:T(8,128)(2,1)}, bf16[192,1152]{1,0:T(8,128)(2,1)}, u32[]{:S(2)}, u32[]{:S(2)}) collective-permute-start(bf16[192,1152]{1,0:T(8,128)(2,1)} %collective-permute-done.5.refs_6_), channel_id=1, source_target_pairs={{0,32},{1,225},{4,36},{5,229},{8,40},{9,233},{12,44},{13,237},{16,... | collective-permute-start | bytes 1327112 | tf_op jit(solution)/shard_map/ppermute | solution.py:54
  31.8 23.3 %copy-start.5 = (bf16[256,1536]{1,0:T(8,128)(2,1)}, bf16[256,1536]{1,0:T(8,128)(2,1)S(1)}, u32[]{:S(2)}) copy-start(bf16[256,1536]{1,0:T(8,128)(2,1)S(1)} %collective-permute-done.2.refs_2_) | copy-start | bytes 2359300
  35.2 19.9 %copy-start.6 = (bf16[256,1536]{1,0:T(8,128)(2,1)}, bf16[256,1536]{1,0:T(8,128)(2,1)S(1)}, u32[]{:S(2)}) copy-start(bf16[256,1536]{1,0:T(8,128)(2,1)S(1)} %collective-permute-done.1.refs_1_) | copy-start | bytes 2359300
  35.2 12.1 %collective-permute-start.7 = (bf16[192,1152]{1,0:T(8,128)(2,1)}, bf16[192,1152]{1,0:T(8,128)(2,1)}, u32[]{:S(2)}, u32[]{:S(2)}) collective-permute-start(bf16[192,1152]{1,0:T(8,128)(2,1)} %collective-permute-done.6.refs_7_), channel_id=1, source_target_pairs={{0,32},{1,225},{4,36},{5,229},{8,40},{9,233},{12,44},{13,237},{16,... | collective-permute-start | bytes 1327112 | tf_op jit(solution)/shard_map/ppermute | solution.py:54
  35.9 10.4 %collective-permute-start.4 = (bf16[128,1536]{1,0:T(8,128)(2,1)S(1)}, bf16[128,1536]{1,0:T(8,128)(2,1)S(1)}, u32[]{:S(2)}, u32[]{:S(2)}) collective-permute-start(bf16[128,1536]{1,0:T(8,128)(2,1)S(1)} %slice.9), channel_id=1, source_target_pairs={{0,18},{1,19},{4,22},{5,23},{8,26},{9,27},{12,30},{13,31},{16,0},{... | collective-permute-start | bytes 1179656 | tf_op jit(solution)/shard_map/ppermute | solution.py:40
  36.4 10.9 %collective-permute-start.3 = (bf16[128,1536]{1,0:T(8,128)(2,1)S(1)}, bf16[128,1536]{1,0:T(8,128)(2,1)}, u32[]{:S(2)}, u32[]{:S(2)}) collective-permute-start(bf16[128,1536]{1,0:T(8,128)(2,1)S(1)} %slice.8), channel_id=1, source_target_pairs={{0,16},{1,17},{4,20},{5,21},{8,24},{9,25},{12,28},{13,29},{16,2},{... | collective-permute-start | bytes 1179656 | tf_op jit(solution)/shard_map/ppermute | solution.py:40
  37.6 12.5 %collective-permute-start.9 = (bf16[192,1152]{1,0:T(8,128)(2,1)}, bf16[192,1152]{1,0:T(8,128)(2,1)}, u32[]{:S(2)}, u32[]{:S(2)}) collective-permute-start(bf16[192,1152]{1,0:T(8,128)(2,1)} %collective-permute-done.5.refs_6_), channel_id=1, source_target_pairs={{0,1},{1,0},{4,5},{5,4},{8,9},{9,8},{12,13},{13,12},{16,17},{17,16... | collective-permute-start | bytes 1327112 | tf_op jit(solution)/shard_map/ppermute | solution.py:44
  37.6 12.5 %collective-permute-start.10 = (bf16[192,1152]{1,0:T(8,128)(2,1)}, bf16[192,1152]{1,0:T(8,128)(2,1)}, u32[]{:S(2)}, u32[]{:S(2)}) collective-permute-start(bf16[192,1152]{1,0:T(8,128)(2,1)} %collective-permute-done.6.refs_7_), channel_id=1, source_target_pairs={{0,1},{1,0},{4,5},{5,4},{8,9},{9,8},{12,13},{13,12},{16,17},{17,16... | collective-permute-start | bytes 1327112 | tf_op jit(solution)/shard_map/ppermute | solution.py:44
  47.4 2.7 %collective-permute-start.11 = (bf16[192,1152]{1,0:T(8,128)(2,1)}, bf16[192,1152]{1,0:T(8,128)(2,1)}, u32[]{:S(2)}, u32[]{:S(2)}) collective-permute-start(bf16[192,1152]{1,0:T(8,128)(2,1)} %collective-permute-done.7.refs_8_), channel_id=1, source_target_pairs={{0,1},{1,0},{4,5},{5,4},{8,9},{9,8},{12,13},{13,12},{16,17},{17,16... | collective-permute-start | bytes 1327112 | tf_op jit(solution)/shard_map/ppermute | solution.py:44
  47.4 7.8 %collective-permute-start.8 = (bf16[192,1152]{1,0:T(8,128)(2,1)}, bf16[192,1152]{1,0:T(8,128)(2,1)}, u32[]{:S(2)}, u32[]{:S(2)}) collective-permute-start(bf16[192,1152]{1,0:T(8,128)(2,1)} %collective-permute-done.7.refs_8_), channel_id=1, source_target_pairs={{0,32},{1,225},{4,36},{5,229},{8,40},{9,233},{12,44},{13,237},{16,... | collective-permute-start | bytes 1327112 | tf_op jit(solution)/shard_map/ppermute | solution.py:54
  64.4 6.1 %collective-permute-start.12 = (bf16[2,2,256,768]{3,2,1,0:T(8,128)(2,1)}, bf16[2,2,256,768]{3,2,1,0:T(8,128)(2,1)S(1)}, u32[]{:S(2)}, u32[]{:S(2)}) collective-permute-start(bf16[2,2,256,768]{3,2,1,0:T(8,128)(2,1)} %get-tuple-element.45.refs_1_), channel_id=1, source_target_pairs={{0,1},{1,0},{4,5},{5,4},{8,9},{9,8},{12,13},{13,12},{16,17},{17,16... | collective-permute-start | bytes 4718600 | tf_op jit(solution)/shard_map/ppermute | solution.py:44
  67.0 13.0 %collective-permute-start.13 = (bf16[256,768]{1,0:T(8,128)(2,1)}, bf16[256,768]{1,0:T(8,128)(2,1)S(1)}, u32[]{:S(2)}, u32[]{:S(2)}) collective-permute-start(bf16[256,768]{1,0:T(8,128)(2,1)} %get-tuple-element.46), channel_id=1, source_target_pairs={{0,32},{1,33},{4,36},{5,37},{8,40},{9,41},{12,44},{13,45},{16,48},... | collective-permute-start | bytes 1179656 | tf_op jit(solution)/shard_map/ppermute | solution.py:40
  67.0 13.0 %collective-permute-start.14 = (bf16[256,768]{1,0:T(8,128)(2,1)}, bf16[256,768]{1,0:T(8,128)(2,1)S(1)}, u32[]{:S(2)}, u32[]{:S(2)}) collective-permute-start(bf16[256,768]{1,0:T(8,128)(2,1)} %get-tuple-element.47), channel_id=1, source_target_pairs={{0,224},{1,225},{4,228},{5,229},{8,232},{9,233},{12,236},{13,237},... | collective-permute-start | bytes 1179656 | tf_op jit(solution)/shard_map/ppermute | solution.py:40
  69.7 18.8 %collective-permute-start.23 = (bf16[2,256,768]{2,1,0:T(8,128)(2,1)}, bf16[2,256,768]{2,1,0:T(8,128)(2,1)S(1)}, u32[]{:S(2)}, u32[]{:S(2)}) collective-permute-start(bf16[2,256,768]{2,1,0:T(8,128)(2,1)} %get-tuple-element.70), channel_id=1, source_target_pairs={{0,13},{1,4},{4,1},{5,8},{8,5},{9,12},{12,9},{13,0},{16,29},{17,20... | collective-permute-start | bytes 2359304 | tf_op jit(solution)/shard_map/ppermute | solution.py:48
  70.4 17.4 %collective-permute-start.15 = (bf16[256,768]{1,0:T(8,128)(2,1)}, bf16[256,768]{1,0:T(8,128)(2,1)S(1)}, u32[]{:S(2)}, u32[]{:S(2)}) collective-permute-start(bf16[256,768]{1,0:T(8,128)(2,1)} %get-tuple-element.63), channel_id=1, source_target_pairs={{0,32},{1,33},{4,36},{5,37},{8,40},{9,41},{12,44},{13,45},{16,48},... | collective-permute-start | bytes 1179656 | tf_op jit(solution)/shard_map/ppermute | solution.py:40
  70.4 17.3 %collective-permute-start.16 = (bf16[256,768]{1,0:T(8,128)(2,1)}, bf16[256,768]{1,0:T(8,128)(2,1)S(1)}, u32[]{:S(2)}, u32[]{:S(2)}) collective-permute-start(bf16[256,768]{1,0:T(8,128)(2,1)} %get-tuple-element.65), channel_id=1, source_target_pairs={{0,224},{1,225},{4,228},{5,229},{8,232},{9,233},{12,236},{13,237},... | collective-permute-start | bytes 1179656 | tf_op jit(solution)/shard_map/ppermute | solution.py:40
  80.1 8.9 %collective-permute-start.21 = (bf16[256,768]{1,0:T(8,128)(2,1)S(1)}, bf16[256,768]{1,0:T(8,128)(2,1)S(1)}, u32[]{:S(2)}, u32[]{:S(2)}) collective-permute-start(bf16[256,768]{1,0:T(8,128)(2,1)S(1)} %collective-permute-done.13.refs_4_), channel_id=1, source_target_pairs={{0,13},{1,4},{4,1},{5,8},{8,5},{9,12},{12,9},{13,0},{16,29},{17,20... | collective-permute-start | bytes 1179656 | tf_op jit(solution)/shard_map/ppermute | solution.py:48
  83.0 9.8 %collective-permute-start.22 = (bf16[256,768]{1,0:T(8,128)(2,1)S(1)}, bf16[256,768]{1,0:T(8,128)(2,1)S(1)}, u32[]{:S(2)}, u32[]{:S(2)}) collective-permute-start(bf16[256,768]{1,0:T(8,128)(2,1)S(1)} %collective-permute-done.14.refs_5_), channel_id=1, source_target_pairs={{0,13},{1,4},{4,1},{5,8},{8,5},{9,12},{12,9},{13,0},{16,29},{17,20... | collective-permute-start | bytes 1179656 | tf_op jit(solution)/shard_map/ppermute | solution.py:48
  87.8 5.0 %collective-permute-start.18 = (bf16[256,768]{1,0:T(8,128)(2,1)S(1)}, bf16[256,768]{1,0:T(8,128)(2,1)}, u32[]{:S(2)}, u32[]{:S(2)}) collective-permute-start(bf16[256,768]{1,0:T(8,128)(2,1)S(1)} %collective-permute-done.14.refs_5_), channel_id=1, source_target_pairs={{0,1},{1,0},{4,5},{5,4},{8,9},{9,8},{12,13},{13,12},{16,17},{17,16... | collective-permute-start | bytes 1179656 | tf_op jit(solution)/shard_map/ppermute | solution.py:44
  88.4 4.4 %collective-permute-start.17 = (bf16[256,768]{1,0:T(8,128)(2,1)S(1)}, bf16[256,768]{1,0:T(8,128)(2,1)}, u32[]{:S(2)}, u32[]{:S(2)}) collective-permute-start(bf16[256,768]{1,0:T(8,128)(2,1)S(1)} %collective-permute-done.13.refs_4_), channel_id=1, source_target_pairs={{0,1},{1,0},{4,5},{5,4},{8,9},{9,8},{12,13},{13,12},{16,17},{17,16... | collective-permute-start | bytes 1179656 | tf_op jit(solution)/shard_map/ppermute | solution.py:44
  88.5 4.3 %collective-permute-start.19 = (bf16[256,768]{1,0:T(8,128)(2,1)S(1)}, bf16[256,768]{1,0:T(8,128)(2,1)}, u32[]{:S(2)}, u32[]{:S(2)}) collective-permute-start(bf16[256,768]{1,0:T(8,128)(2,1)S(1)} %collective-permute-done.15.refs_6_), channel_id=1, source_target_pairs={{0,1},{1,0},{4,5},{5,4},{8,9},{9,8},{12,13},{13,12},{16,17},{17,16... | collective-permute-start | bytes 1179656 | tf_op jit(solution)/shard_map/ppermute | solution.py:44
  88.9 3.9 %collective-permute-start.20 = (bf16[256,768]{1,0:T(8,128)(2,1)S(1)}, bf16[256,768]{1,0:T(8,128)(2,1)}, u32[]{:S(2)}, u32[]{:S(2)}) collective-permute-start(bf16[256,768]{1,0:T(8,128)(2,1)S(1)} %collective-permute-done.16.refs_7_), channel_id=1, source_target_pairs={{0,1},{1,0},{4,5},{5,4},{8,9},{9,8},{12,13},{13,12},{16,17},{17,16... | collective-permute-start | bytes 1179656 | tf_op jit(solution)/shard_map/ppermute | solution.py:44
  93.5 21.8 %copy-start = (s32[3]{0:T(128)S(1)}, s32[3]{0:T(128)}, u32[]{:S(2)}) copy-start(s32[3]{0:T(128)} %pad_add_fusion.place) | copy-start | bytes 40
  102.6 7.2 %collective-permute-start.24 = (bf16[256,384]{1,0:T(8,128)(2,1)}, bf16[256,384]{1,0:T(8,128)(2,1)S(1)}, u32[]{:S(2)}, u32[]{:S(2)}) collective-permute-start(bf16[256,384]{1,0:T(8,128)(2,1)} %get-tuple-element.71), channel_id=1, source_target_pairs={{0,18},{1,19},{4,22},{5,23},{8,26},{9,27},{12,30},{13,31},{16,0},{... | collective-permute-start | bytes 589832 | tf_op jit(solution)/shard_map/ppermute | solution.py:40
  102.7 12.6 %collective-permute-start.25 = (bf16[256,384]{1,0:T(8,128)(2,1)}, bf16[256,384]{1,0:T(8,128)(2,1)S(1)}, u32[]{:S(2)}, u32[]{:S(2)}) collective-permute-start(bf16[256,384]{1,0:T(8,128)(2,1)} %get-tuple-element.72), channel_id=1, source_target_pairs={{0,16},{1,17},{4,20},{5,21},{8,24},{9,25},{12,28},{13,29},{16,2},{... | collective-permute-start | bytes 589832 | tf_op jit(solution)/shard_map/ppermute | solution.py:40
  104.2 11.2 %collective-permute-start.26 = (bf16[256,384]{1,0:T(8,128)(2,1)}, bf16[256,384]{1,0:T(8,128)(2,1)S(1)}, u32[]{:S(2)}, u32[]{:S(2)}) collective-permute-start(bf16[256,384]{1,0:T(8,128)(2,1)} %get-tuple-element.73), channel_id=1, source_target_pairs={{0,2},{1,3},{4,6},{5,7},{8,10},{9,11},{12,14},{13,15},{16,18},{17,... | collective-permute-start | bytes 589832 | tf_op jit(solution)/shard_map/ppermute | solution.py:40
  (12 other events, 57.9 us)
